TPU v7x, 32 devices: a whole 2x2x4 slice. The times are simulated.
32 devices in a mesh: clip: 8 (over z, y), ha: 2 (over core), wa: 2 (over x).
Axes of the slice: x: 2, y: 2, z: 4, core: 2. Of those that a mesh axis runs over, the one named last changes fastest.
Arguments:
- slow_input: bfloat16 [32, 12, 14, 14, 1024], P('clip', None, 'ha', 'wa'), may hold values from -6 to 6
- fast_input: bfloat16 [32, 48, 14, 14, 128], P('clip', None, 'ha', 'wa'), may hold values from -6 to 6
- frame_counts: int32 [32], replicated, may hold values from 4 to 12, as said below
- lateral_weight: bfloat16 [5, 128, 256], replicated, may hold values from -0.25 to 0.25
- slow_a_weight: bfloat16 [3, 1280, 256], replicated, may hold values from -0.09375 to 0.09375
- slow_b_weight: bfloat16 [3, 3, 256, 256], replicated, may hold values from -0.125 to 0.125
- slow_c_weight: bfloat16 [256, 1024], replicated, may hold values from -0.375 to 0.375
- slow_proj_weight: bfloat16 [1280, 1024], replicated, may hold values from -0.15625 to 0.15625
- fast_a_weight: bfloat16 [3, 128, 32], replicated, may hold values from -0.3125 to 0.3125
- fast_b_weight: bfloat16 [3, 3, 32, 32], replicated, may hold values from -0.375 to 0.375
- fast_c_weight: bfloat16 [32, 128], replicated, may hold values from -1 to 1
- slow_gain: float32 [2560], replicated, may hold values from 0.1 to 1.9
- slow_shift: float32 [2560], replicated, may hold values from -3 to 3
- fast_gain: float32 [192], replicated, may hold values from 0.1 to 1.9
- fast_shift: float32 [192], replicated, may hold values from -3 to 3
- slow_cotangent: bfloat16 [32, 12, 14, 14, 1024], P('clip', None, 'ha', 'wa'), may hold values from -6 to 6
- fast_cotangent: bfloat16 [32, 48, 14, 14, 128], P('clip', None, 'ha', 'wa'), may hold values from -6 to 6
Outputs:
- slow_output: bfloat16 [32, 12, 14, 14, 1024], P('clip', None, 'ha', 'wa')
- fast_output: bfloat16 [32, 48, 14, 14, 128], P('clip', None, 'ha', 'wa')
- slow_input_grad: bfloat16 [32, 12, 14, 14, 1024], P('clip', None, 'ha', 'wa')
- fast_input_grad: bfloat16 [32, 48, 14, 14, 128], P('clip', None, 'ha', 'wa')
- lateral_weight_grad: float32 [5, 128, 256], replicated
- slow_a_weight_grad: float32 [3, 1280, 256], replicated
- slow_b_weight_grad: float32 [3, 3, 256, 256], replicated
- slow_c_weight_grad: float32 [256, 1024], replicated
- slow_proj_weight_grad: float32 [1280, 1024], replicated
- fast_a_weight_grad: float32 [3, 128, 32], replicated
- fast_b_weight_grad: float32 [3, 3, 32, 32], replicated
- fast_c_weight_grad: float32 [32, 128], replicated
- slow_gain_grad: float32 [2560], replicated
- slow_shift_grad: float32 [2560], replicated
- fast_gain_grad: float32 [192], replicated
- fast_shift_grad: float32 [192], replicated
Inputs may be any that keep to these rules, and one draw needn't show every extreme that they name: `frame_counts`: some clip has exactly 12 real frames and some exactly 4.
All inputs are finite; a program needn't handle non-finite values.
Results may differ from a plain program's by a relative error of at most 0.0088.
Values may be sent and summed in bfloat16 or wider, within the bound.
A program may use at most 256 MiB of HBM per device.

v0:
```python
import jax
import jax.numpy as jnp
from jax import lax
from jax.sharding import PartitionSpec as P

ALPHA = 4
H = 14
W = 14
C_IN = 1024
C_MID = 256
C_FAST = 128
C_FMID = 32


eps_norm = 1e-05


def padded_2(cells, sides, width):
    for axis, dim in sides:
        count = lax.axis_size(axis)
        ends = count - 1
        head = lax.slice_in_dim(cells, 0, width, axis=dim)
        tail = lax.slice_in_dim(cells, cells.shape[dim] - width, cells.shape[dim], axis=dim)
        cells = jnp.concatenate(
            [
                lax.ppermute(tail, axis, [(i, (i + 1) % count) for i in range(ends)]),
                cells,
                lax.ppermute(head, axis, [((i + 1) % count, i) for i in range(ends)]),
            ],
            axis=dim,
        )
    return cells


def smooth(values):
    return values * jax.nn.sigmoid(values)


def smooth_slope(values):
    sigma = jax.nn.sigmoid(values)
    return sigma * (1.0 + values * (1.0 - sigma))


def product(values, weight):
    return lax.dot_general(
        values, weight, (((values.ndim - 1,), (0,)), ((), ())), preferred_element_type=jnp.float32
    )


def product_back(grads, weight):
    return lax.dot_general(
        grads, weight, (((grads.ndim - 1,), (1,)), ((), ())), preferred_element_type=jnp.float32
    )


def weight_sum(values, grads):
    flat_values = values.reshape(-1, values.shape[-1])
    flat_grads = grads.reshape(-1, grads.shape[-1])
    return lax.dot_general(
        flat_values, flat_grads, (((0,), (0,)), ((), ())), preferred_element_type=jnp.float32
    )


def pad_frames(values, margin):
    return jnp.pad(values, ((0, 0), (margin, margin), (0, 0), (0, 0), (0, 0)))


def conv_time(values, weight):
    frames = values.shape[1]
    padded = pad_frames(values, 1)
    return sum((product(padded[:, k : k + frames], weight[k]) for k in range(3)))


def conv_time_back(grads, weight):
    frames = grads.shape[1]
    padded = pad_frames(grads, 1)
    return sum((product_back(padded[:, 2 - k : 2 - k + frames], weight[k]) for k in range(3)))


def conv_time_weights(values, grads):
    frames = values.shape[1]
    padded = pad_frames(values, 1)
    return jnp.stack([weight_sum(padded[:, k : k + frames], grads) for k in range(3)])


def conv_space(wide, weight):
    height = wide.shape[2] - 2
    width = wide.shape[3] - 2
    return sum(
        (
            product(wide[:, :, i : i + height, j : j + width], weight[i, j])
            for i in range(3)
            for j in range(3)
        )
    )


def conv_space_back(wide_grads, weight):
    height = wide_grads.shape[2] - 2
    width = wide_grads.shape[3] - 2
    return sum(
        (
            product_back(
                wide_grads[:, :, 2 - i : 2 - i + height, 2 - j : 2 - j + width], weight[i, j]
            )
            for i in range(3)
            for j in range(3)
        )
    )


def conv_space_weights(wide, grads):
    height = grads.shape[2]
    width = grads.shape[3]
    return jnp.stack(
        [
            jnp.stack(
                [weight_sum(wide[:, :, i : i + height, j : j + width], grads) for j in range(3)]
            )
            for i in range(3)
        ]
    )


def lateral_taps(fast_in, slow_frames):
    padded = pad_frames(fast_in, 2)
    blocks = padded.reshape((padded.shape[0], slow_frames + 1, ALPHA) + padded.shape[2:])
    return [blocks[:, :slow_frames, k] for k in range(ALPHA)] + [blocks[:, 1:, 0]]


def lateral_back(lat_grads, weight):
    taps = [product_back(lat_grads, weight[k]) for k in range(5)]
    leading = jnp.stack(taps[:4], axis=2)
    blocks = jnp.pad(leading, ((0, 0), (0, 1), (0, 0), (0, 0), (0, 0), (0, 0)))
    blocks = blocks + jnp.pad(taps[4][:, :, None], ((0, 0), (1, 0), (0, 3), (0, 0), (0, 0), (0, 0)))
    shaped = blocks.reshape((blocks.shape[0], -1) + blocks.shape[3:])
    return shaped[:, 2 : shaped.shape[1] - 2]


def split_widths(vector, widths):
    borders = [sum(widths[:k]) for k in range(1, len(widths))]
    return jnp.split(vector, borders)


def moments(items):
    widths = [values.shape[-1] for values, frame_mask, counted in items]
    totals = jnp.concatenate(
        [
            jnp.full((values.shape[-1],), counted, jnp.float32)
            for values, frame_mask, counted in items
        ]
    )
    firsts = jnp.concatenate(
        [jnp.sum(frame_mask * values, axis=(0, 1, 2, 3)) for values, frame_mask, counted in items]
    )
    firsts = lax.psum(firsts, ("clip", "ha", "wa"))
    means = firsts / totals
    pieces = split_widths(means, widths)
    centred = jnp.concatenate(
        [
            jnp.sum(item[1] * (item[0] - piece) ** 2, axis=(0, 1, 2, 3))
            for item, piece in zip(items, pieces)
        ]
    )
    spread = lax.psum(centred, ("clip", "ha", "wa")) / totals
    scales = lax.rsqrt(spread + eps_norm)
    return list(zip(split_widths(means, widths), split_widths(scales, widths)))


def back_sums(items):
    widths = [grads.shape[-1] for grads, normed in items]
    firsts = jnp.concatenate([jnp.sum(grads, axis=(0, 1, 2, 3)) for grads, normed in items])
    seconds = jnp.concatenate(
        [jnp.sum(grads * normed, axis=(0, 1, 2, 3)) for grads, normed in items]
    )
    firsts, seconds = lax.psum((firsts, seconds), ("clip", "ha", "wa"))
    return list(zip(split_widths(firsts, widths), split_widths(seconds, widths)))


def norm_back(grads, normed, gains, scales, frame_mask, counted, shift_sum, gain_sum):
    return (
        gains * scales * (grads - frame_mask * (shift_sum + normed * gain_sum) / counted)
    ).astype(jnp.bfloat16)


def on_device(
    slow_input,
    fast_input,
    frame_counts,
    lateral_weight,
    slow_a_weight,
    slow_b_weight,
    slow_c_weight,
    slow_proj_weight,
    fast_a_weight,
    fast_b_weight,
    fast_c_weight,
    slow_gain,
    slow_shift,
    fast_gain,
    fast_shift,
    slow_cotangent,
    fast_cotangent,
):
    clips_here = slow_input.shape[0]
    slow_frames = slow_input.shape[1]
    fast_frames = fast_input.shape[1]
    own_counts = lax.dynamic_slice_in_dim(
        frame_counts, lax.axis_index("clip") * clips_here, clips_here
    )
    slow_mask = (jnp.arange(slow_frames)[None, :] < own_counts[:, None]).astype(jnp.float32)[
        :, :, None, None, None
    ]
    fast_mask = (jnp.arange(fast_frames)[None, :] < ALPHA * own_counts[:, None]).astype(
        jnp.float32
    )[:, :, None, None, None]
    slow_total = jnp.sum(frame_counts).astype(jnp.float32) * (H * W)
    fast_total = slow_total * ALPHA
    slow_bounds = [0, C_MID, 2 * C_MID, 2 * C_MID + C_IN, 2 * C_MID + 2 * C_IN]
    fast_bounds = [0, C_FMID, 2 * C_FMID, 2 * C_FMID + C_FAST]
    slow_gains = [slow_gain[slow_bounds[k] : slow_bounds[k + 1]] for k in range(4)]
    slow_shifts = [slow_shift[slow_bounds[k] : slow_bounds[k + 1]] for k in range(4)]
    fast_gains = [fast_gain[fast_bounds[k] : fast_bounds[k + 1]] for k in range(3)]
    fast_shifts = [fast_shift[fast_bounds[k] : fast_bounds[k + 1]] for k in range(3)]
    slow_zero = slow_input * slow_mask.astype(jnp.bfloat16)
    fast_zero = fast_input * fast_mask.astype(jnp.bfloat16)
    taps = lateral_taps(fast_zero, slow_frames)
    lateral = sum((product(taps[k], lateral_weight[k]) for k in range(5))).astype(jnp.bfloat16)
    joined = jnp.concatenate([slow_zero, lateral], axis=-1)
    slow_za = conv_time(joined, slow_a_weight)
    fast_za = conv_time(fast_zero, fast_a_weight)
    (centre_sa, scale_sa), (centre_fa, scale_fa) = moments(
        [(slow_za, slow_mask, slow_total), (fast_za, fast_mask, fast_total)]
    )
    normed_sa = (slow_za - centre_sa) * scale_sa
    normed_fa = (fast_za - centre_fa) * scale_fa
    pre_sa = slow_gains[0] * normed_sa + slow_shifts[0]
    pre_fa = fast_gains[0] * normed_fa + fast_shifts[0]
    slow_first = (smooth(pre_sa) * slow_mask).astype(jnp.bfloat16)
    fast_first = (smooth(pre_fa) * fast_mask).astype(jnp.bfloat16)
    slow_wide = padded_2(slow_first, (("ha", 2), ("wa", 3)), 1)
    fast_wide = padded_2(fast_first, (("ha", 2), ("wa", 3)), 1)
    slow_zb = conv_space(slow_wide, slow_b_weight)
    fast_zb = conv_space(fast_wide, fast_b_weight)
    (centre_sb, scale_sb), (centre_fb, scale_fb) = moments(
        [(slow_zb, slow_mask, slow_total), (fast_zb, fast_mask, fast_total)]
    )
    normed_sb = (slow_zb - centre_sb) * scale_sb
    normed_fb = (fast_zb - centre_fb) * scale_fb
    pre_sb = slow_gains[1] * normed_sb + slow_shifts[1]
    pre_fb = fast_gains[1] * normed_fb + fast_shifts[1]
    slow_second = (smooth(pre_sb) * slow_mask).astype(jnp.bfloat16)
    fast_second = (smooth(pre_fb) * fast_mask).astype(jnp.bfloat16)
    slow_zc = product(slow_second, slow_c_weight)
    slow_zp = product(joined, slow_proj_weight)
    fast_zc = product(fast_second, fast_c_weight)
    (centre_sc, scale_sc), (centre_sp, scale_sp), (centre_fc, scale_fc) = moments(
        [
            (slow_zc, slow_mask, slow_total),
            (slow_zp, slow_mask, slow_total),
            (fast_zc, fast_mask, fast_total),
        ]
    )
    normed_sc = (slow_zc - centre_sc) * scale_sc
    normed_sp = (slow_zp - centre_sp) * scale_sp
    normed_fc = (fast_zc - centre_fc) * scale_fc
    slow_pre = (
        slow_gains[2] * normed_sc + slow_shifts[2] + slow_gains[3] * normed_sp + slow_shifts[3]
    )
    fast_pre = fast_gains[2] * normed_fc + fast_shifts[2] + fast_zero.astype(jnp.float32)
    slow_output = (smooth(slow_pre) * slow_mask).astype(jnp.bfloat16)
    fast_output = (smooth(fast_pre) * fast_mask).astype(jnp.bfloat16)
    slow_back = slow_cotangent.astype(jnp.float32) * slow_mask * smooth_slope(slow_pre)
    fast_back = fast_cotangent.astype(jnp.float32) * fast_mask * smooth_slope(fast_pre)
    (shift_sc, gain_sc), (shift_sp, gain_sp), (shift_fc, gain_fc) = back_sums(
        [(slow_back, normed_sc), (slow_back, normed_sp), (fast_back, normed_fc)]
    )
    grad_zc = norm_back(
        slow_back, normed_sc, slow_gains[2], scale_sc, slow_mask, slow_total, shift_sc, gain_sc
    )
    grad_zp = norm_back(
        slow_back, normed_sp, slow_gains[3], scale_sp, slow_mask, slow_total, shift_sp, gain_sp
    )
    grad_fzc = norm_back(
        fast_back, normed_fc, fast_gains[2], scale_fc, fast_mask, fast_total, shift_fc, gain_fc
    )
    slow_c_grad = weight_sum(slow_second, grad_zc)
    slow_proj_grad = weight_sum(joined, grad_zp)
    fast_c_grad = weight_sum(fast_second, grad_fzc)
    joined_grad = product_back(grad_zp, slow_proj_weight)
    slow_second_grad = product_back(grad_zc, slow_c_weight)
    fast_second_grad = product_back(grad_fzc, fast_c_weight)
    back_sb = slow_second_grad * slow_mask * smooth_slope(pre_sb)
    back_fb = fast_second_grad * fast_mask * smooth_slope(pre_fb)
    (shift_sb, gain_sb), (shift_fb, gain_fb) = back_sums(
        [(back_sb, normed_sb), (back_fb, normed_fb)]
    )
    grad_zb = norm_back(
        back_sb, normed_sb, slow_gains[1], scale_sb, slow_mask, slow_total, shift_sb, gain_sb
    )
    grad_fzb = norm_back(
        back_fb, normed_fb, fast_gains[1], scale_fb, fast_mask, fast_total, shift_fb, gain_fb
    )
    slow_b_grad = conv_space_weights(slow_wide, grad_zb)
    fast_b_grad = conv_space_weights(fast_wide, grad_fzb)
    slow_grad_wide = padded_2(grad_zb, (("ha", 2), ("wa", 3)), 1)
    fast_grad_wide = padded_2(grad_fzb, (("ha", 2), ("wa", 3)), 1)
    slow_first_grad = conv_space_back(slow_grad_wide, slow_b_weight)
    fast_first_grad = conv_space_back(fast_grad_wide, fast_b_weight)
    back_sa = slow_first_grad * slow_mask * smooth_slope(pre_sa)
    back_fa = fast_first_grad * fast_mask * smooth_slope(pre_fa)
    (shift_sa, gain_sa), (shift_fa, gain_fa) = back_sums(
        [(back_sa, normed_sa), (back_fa, normed_fa)]
    )
    grad_za = norm_back(
        back_sa, normed_sa, slow_gains[0], scale_sa, slow_mask, slow_total, shift_sa, gain_sa
    )
    grad_fza = norm_back(
        back_fa, normed_fa, fast_gains[0], scale_fa, fast_mask, fast_total, shift_fa, gain_fa
    )
    slow_a_grad = conv_time_weights(joined, grad_za)
    fast_a_grad = conv_time_weights(fast_zero, grad_fza)
    joined_grad = joined_grad + conv_time_back(grad_za, slow_a_weight)
    lateral_grad = joined_grad[..., C_IN:].astype(jnp.bfloat16)
    lateral_grads = jnp.stack([weight_sum(taps[k], lateral_grad) for k in range(5)])
    fast_in_grad = (
        fast_back
        + conv_time_back(grad_fza, fast_a_weight)
        + lateral_back(lateral_grad, lateral_weight)
    )
    slow_input_grad = (joined_grad[..., :C_IN] * slow_mask).astype(jnp.bfloat16)
    fast_input_grad = (fast_in_grad * fast_mask).astype(jnp.bfloat16)
    (
        lateral_grads,
        slow_a_grad,
        slow_b_grad,
        slow_c_grad,
        slow_proj_grad,
        fast_a_grad,
        fast_b_grad,
        fast_c_grad,
    ) = lax.psum(
        (
            lateral_grads,
            slow_a_grad,
            slow_b_grad,
            slow_c_grad,
            slow_proj_grad,
            fast_a_grad,
            fast_b_grad,
            fast_c_grad,
        ),
        ("clip", "ha", "wa"),
    )
    slow_gain_grad = jnp.concatenate([gain_sa, gain_sb, gain_sc, gain_sp])
    slow_shift_grad = jnp.concatenate([shift_sa, shift_sb, shift_sc, shift_sp])
    fast_gain_grad = jnp.concatenate([gain_fa, gain_fb, gain_fc])
    fast_shift_grad = jnp.concatenate([shift_fa, shift_fb, shift_fc])
    return (
        slow_output,
        fast_output,
        slow_input_grad,
        fast_input_grad,
        lateral_grads,
        slow_a_grad,
        slow_b_grad,
        slow_c_grad,
        slow_proj_grad,
        fast_a_grad,
        fast_b_grad,
        fast_c_grad,
        slow_gain_grad,
        slow_shift_grad,
        fast_gain_grad,
        fast_shift_grad,
    )


def solution(mesh):
    placed = (
        P("clip", None, "ha", "wa", None),
        P("clip", None, "ha", "wa", None),
        P(),
        P(),
        P(),
        P(),
        P(),
        P(),
        P(),
        P(),
        P(),
        P(),
        P(),
        P(),
        P(),
        P("clip", None, "ha", "wa", None),
        P("clip", None, "ha", "wa", None),
    )
    return jax.shard_map(
        on_device,
        mesh=mesh,
        in_specs=placed,
        out_specs=(
            P("clip", None, "ha", "wa", None),
            P("clip", None, "ha", "wa", None),
            P("clip", None, "ha", "wa", None),
            P("clip", None, "ha", "wa", None),
            P(),
            P(),
            P(),
            P(),
            P(),
            P(),
            P(),
            P(),
            P(),
            P(),
            P(),
            P(),
        ),
        check_vma=False,
    )
```

profile of v0, /device:TPU:0, one launch (start us, length us, event | category | flops | bytes accessed | tf_op | source)
XLA Modules:
  0.0 1269.7 jit_solution(5639538061457965492)
XLA Ops:
  45.1 8.3 multiply_reduce_fusion.14
  53.5 6.6 multiply_reduce_fusion.20
  60.2 42.0 %psum.140 = f32[288]{0:T(512)S(1)} all-reduce(f32[288]{0:T(512)S(1)} %pad_maximum_fusion.34), channel_id=1, replica_groups=mesh['clip'=8,'ha'=2,'wa'=2] {'clip','ha','wa'}, use_global_device_ids=true, to_apply=%region_2.3 | all-reduce | flops 288 | bytes 2304 | tf_op jit(solution)/shard_map/psum | solution.py:156
  107.1 40.2 %psum.141 = f32[288]{0:T(512)S(1)} all-reduce(f32[288]{0:T(512)S(1)} %pad_maximum_fusion.35), channel_id=1, replica_groups=mesh['clip'=8,'ha'=2,'wa'=2] {'clip','ha','wa'}, use_global_device_ids=true, to_apply=%region_6.7 | all-reduce | flops 288 | bytes 2304 | tf_op jit(solution)/shard_map/psum | solution.py:165
  169.6 13.3 %fusion.6 = f32[4,12,7,7,1024]{4,3,2,1,0:T(8,128)} fusion(bf16[1280,1024]{1,0:T(8,128)(2,1)S(1)} %copy-done, bf16[4,12,7,7,256]{4,3,2,1,0:T(8,128)(2,1)S(1)} %copy-done.66, bf16[4,12,7,7,1024]{4,3,2,1,0:T(8,128)(2,1)S(1)} %bitcast.626), kind=kOutput, calls=%fused_computation.85 | convolution fusion | flops 6177669120 | bytes 18276352 | tf_op jit(solution)/shard_map/dot_general | solution.py:45
  236.1 6.3 multiply_reduce_fusion.12
  255.6 39.3 %psum.142 = f32[288]{0:T(512)S(1)} all-reduce(f32[288]{0:T(512)S(1)} %pad_maximum_fusion.36), channel_id=1, replica_groups=mesh['clip'=8,'ha'=2,'wa'=2] {'clip','ha','wa'}, use_global_device_ids=true, to_apply=%region_9.10 | all-reduce | flops 288 | bytes 2304 | tf_op jit(solution)/shard_map/psum | solution.py:156
  298.6 40.9 %psum.143 = f32[288]{0:T(512)S(1)} all-reduce(f32[288]{0:T(512)S(1)} %pad_maximum_fusion.37), channel_id=1, replica_groups=mesh['clip'=8,'ha'=2,'wa'=2] {'clip','ha','wa'}, use_global_device_ids=true, to_apply=%region_12.13 | all-reduce | flops 288 | bytes 2304 | tf_op jit(solution)/shard_map/psum | solution.py:165
  347.4 9.4 multiply_reduce_fusion.5
  356.8 39.3 %psum.144 = f32[2176]{0:T(1024)S(1)} all-reduce(f32[2176]{0:T(1024)S(1)} %pad_maximum_fusion.27), channel_id=1, replica_groups=mesh['clip'=8,'ha'=2,'wa'=2] {'clip','ha','wa'}, use_global_device_ids=true, to_apply=%region_16.17 | all-reduce | flops 2176 | bytes 17408 | tf_op jit(solution)/shard_map/psum | solution.py:156
  399.8 9.0 multiply_reduce_fusion.3
  408.9 41.5 %psum.145 = f32[2176]{0:T(1024)S(1)} all-reduce(f32[2176]{0:T(1024)S(1)} %pad_maximum_fusion.29), channel_id=1, replica_groups=mesh['clip'=8,'ha'=2,'wa'=2] {'clip','ha','wa'}, use_global_device_ids=true, to_apply=%region_20.21 | all-reduce | flops 2176 | bytes 17408 | tf_op jit(solution)/shard_map/psum | solution.py:165
  450.6 8.2 fusion.316
  458.8 19.1 %fusion.315 = (f32[1024]{0:T(1024)S(1)}, f32[1024]{0:T(1024)S(1)}, f32[1024]{0:T(1024)S(1)}, f32[4,12,7,7,1024]{4,3,2,1,0:T(8,128)}, bf16[4,12,7,7,1024]{4,3,2,1,0:T(8,128)(2,1)}) fusion(f32[1024]{0:T(1024)S(1)} %get-tuple-element.123, f32[4,12,7,7,1024]{4,3,2,1,0:T(8,128)} %fusion.6, f32[1024]{0:T(1024)S(1)} %get-tuple-element.131, ...), kind=kLoop, calls=%fused_computation.460 | loop fusion | flops 65025024 | bytes 38580416 | tf_op jit(solution)/shard_map/reduce_sum | solution.py:172
  477.9 39.6 %all-reduce.11 = (f32[2176]{0:T(1024)S(1)}, f32[2176]{0:T(1024)S(1)}) all-reduce(f32[2176]{0:T(1024)S(1)} %get-tuple-element.165, f32[2176]{0:T(1024)S(1)} %get-tuple-element.164), channel_id=1, replica_groups=mesh['clip'=8,'ha'=2,'wa'=2] {'clip','ha','wa'}, use_global_device_ids=true, to_apply=%region_27.28 | all-reduce | flops 4352 | bytes 34816 | tf_op jit(solution)/shard_map/psum | solution.py:176
  531.4 13.3 %multiply_convert_fusion = (bf16[4,12,7,7,1024]{4,3,2,1,0:T(8,128)(2,1)S(1)}, bf16[4,12,7,7,1024]{4,3,2,1,0:T(8,128)(2,1)}) fusion(f32[4,12,7,7,1024]{4,3,2,1,0:T(8,128)} %get-tuple-element.79, f32[4,12,7,7,1024]{4,3,2,1,0:T(8,128)} %get-tuple-element.159, f32[1024]{0:T(1024)S(1)} %get-tuple-element.127, f32[1024]{0:T(1024)S(1)} %get-tuple-element.125, ...), kind=kLoop, calls=%fused_computation.3 | loop fusion | flops 43352064 | bytes 38576324 | tf_op jit(solution)/shard_map/convert_element_type | solution.py:183
  555.7 41.3 %all-reduce.10 = (f32[288]{0:T(512)S(1)}, f32[288]{0:T(512)S(1)}) all-reduce(f32[288]{0:T(512)S(1)} %pad_maximum_fusion.39, f32[288]{0:T(512)S(1)} %pad_maximum_fusion.38), channel_id=1, replica_groups=mesh['clip'=8,'ha'=2,'wa'=2] {'clip','ha','wa'}, use_global_device_ids=true, to_apply=%region_33.34 | all-reduce | flops 576 | bytes 4608 | tf_op jit(solution)/shard_map/psum | solution.py:176
  625.5 17.5 %convolution_bitcast_fusion = f32[1280,1024]{1,0:T(8,128)} fusion(bf16[4,12,7,7,1024]{4,3,2,1,0:T(8,128)(2,1)S(1)} %bitcast.632, bf16[4,12,7,7,256]{4,3,2,1,0:T(8,128)(2,1)} %copy-done.64, bf16[4,12,7,7,1024]{4,3,2,1,0:T(8,128)(2,1)S(1)} %bitcast.628), kind=kOutput, calls=%fused_computation.36 | convolution fusion | flops 6177669120 | bytes 16080896 | tf_op jit(solution)/shard_map/dot_general | solution.py:59
  643.1 12.6 fusion.4
  716.7 10.0 fusion.317
  739.4 7.2 fusion.319
  746.7 40.6 %all-reduce.9 = (f32[288]{0:T(512)S(1)}, f32[288]{0:T(512)S(1)}) all-reduce(f32[288]{0:T(512)S(1)} %pad_maximum_fusion.41, f32[288]{0:T(512)S(1)} %pad_maximum_fusion.40), channel_id=1, replica_groups=mesh['clip'=8,'ha'=2,'wa'=2] {'clip','ha','wa'}, use_global_device_ids=true, to_apply=%region_39.40 | all-reduce | flops 576 | bytes 4608 | tf_op jit(solution)/shard_map/psum | solution.py:176
  799.1 8.5 convolution_bitcast_fusion.1
  807.7 8.3 convolution_bitcast_fusion.3
  815.9 8.4 convolution_bitcast_fusion.2
  824.4 6.7 fusion.150
  831.1 6.7 fusion.146
  837.8 21.2 %add_add_fusion = f32[4,12,7,7,1280]{4,3,2,1,0:T(8,128)} fusion(f32[4,12,7,7,1280]{4,3,2,1,0:T(8,128)} %fusion.4, f32[4,12,7,7,1280]{4,3,2,1,0:T(8,128)} %fusion.150, f32[4,12,7,7,1280]{4,3,2,1,0:T(8,128)} %fusion.146, bf16[4,12,7,7,256]{4,3,2,1,0:T(8,128)(2,1)} %copy-done.22, bf16[3,1280,256]{2,1,0:T(8,128)(2,1)} %param.21), kind=kOutput, calls=%fused_computation | convolution fusion | flops 1421987840 | bytes 55361536 | tf_op jit(solution)/shard_map/dot_general | solution.py:51
  879.8 14.4 %copy.140 = bf16[4,12,7,7,1024]{4,0,3,2,1:T(4,128)(2,1)} copy(bf16[4,12,7,7,1024]{4,3,2,1,0:T(8,128)(2,1)} %get-tuple-element.83) | data formatting | bytes 9633792
  915.0 12.0 copy.141
  936.3 61.7 %all-reduce.16.cloned.1.call-done = (f32[3,128,32]{1,2,0:T(8,128)}, f32[3,3,32,32]{3,2,1,0:T(8,128)}, f32[32,128]{1,0:T(8,128)}) async-done(((f32[3,128,32]{1,2,0:T(8,128)}, f32[3,3,32,32]{3,2,1,0:T(8,128)}, f32[32,128]{1,0:T(8,128)}), (f32[3,128,32]{1,2,0:T(8,128)}, f32[3,3,32,32]{3,2,1,0:T(8,128)}, f32[32,128]{1,0:T(8,128)})) %all-reduce.16.cloned.1.call-update) | async-done | bytes 102416 | tf_op jit(solution)/shard_map/psum | solution.py:342
  998.0 250.8 %all-reduce.18.cloned.1.call-done = (f32[5,128,256]{2,1,0:T(8,128)}, f32[3,1280,256]{2,1,0:T(8,128)}, f32[3,3,256,256]{3,2,1,0:T(8,128)}, f32[256,1024]{1,0:T(8,128)}, f32[1280,1024]{1,0:T(8,128)}) async-done(((f32[5,128,256]{2,1,0:T(8,128)}, f32[3,1280,256]{2,1,0:T(8,128)}, f32[3,3,256,256]{3,2,1,0:T(8,128)}, f32[256,1024]{1,0:T(8,128)}, f32[1280,1024]{1,0:T(8,128)}), (f32[5,128,256]{2,1,0:T(8,128)}, ...) | async-done | bytes 13238288 | tf_op jit(solution)/shard_map/psum | solution.py:342
  (629 shorter events, 347.8 us)
Async XLA Ops:
  7.2 162.4 %copy-start = (bf16[1280,1024]{1,0:T(8,128)(2,1)S(1)}, bf16[1280,1024]{1,0:T(8,128)(2,1)}, u32[]{:S(2)}) copy-start(bf16[1280,1024]{1,0:T(8,128)(2,1)} %param.24) | copy-start | bytes 7864324
  7.2 990.8 %all-reduce.16.cloned.1.call-start = ((), (), s32[]{:S(2)}) async-start(), calls=%async_computation | async-start | bytes 425984 | tf_op jit(solution)/shard_map/psum | solution.py:342
  9.5 515.7 %copy-start.73 = (f32[4,48]{1,0:T(4,128)}, f32[4,48]{1,0:T(4,128)S(1)}, u32[]{:S(2)}) copy-start(f32[4,48]{1,0:T(4,128)S(1)} %get-tuple-element.147) | copy-start | bytes 2308
  53.5 49.6 %copy-start.135 = (f32[2560]{0:T(1024)S(1)}, f32[2560]{0:T(1024)}, u32[]{:S(2)}) copy-start(f32[2560]{0:T(1024)} %param.29) | copy-start | bytes 30724
  102.2 53.7 %copy-start.137 = (f32[32]{0:T(128)}, f32[32]{0:T(128)S(1)}, u32[]{:S(2)}) copy-start(f32[32]{0:T(128)S(1)} %split.96) | copy-start | bytes 388
  107.1 47.7 %copy-start.168 = (f32[192]{0:T(256)S(1)}, f32[192]{0:T(256)}, u32[]{:S(2)}) copy-start(f32[192]{0:T(256)} %param.31) | copy-start | bytes 2308
  107.1 48.3 %copy-start.146 = (f32[192]{0:T(256)S(1)}, f32[192]{0:T(256)}, u32[]{:S(2)}) copy-start(f32[192]{0:T(256)} %param.30) | copy-start | bytes 2308
  151.1 56.9 %collective-permute-start = (bf16[4,12,1,7,256]{4,3,2,1,0:T(8,128)(2,1)}, bf16[4,12,1,7,256]{4,3,2,1,0:T(8,128)(2,1)}, u32[]{:S(2)}, u32[]{:S(2)}) collective-permute-start(bf16[4,12,1,7,256]{4,3,2,1,0:T(8,128)(2,1)} %get-tuple-element.112), channel_id=1, source_target_pairs={{0,2},{1,3},{4,6},{5,7},{8,10},{9,11},{12,14},{13,15},{16,18},{17,... | collective-permute-start | bytes 516104 | tf_op jit(solution)/shard_map/ppermute | solution.py:26
  153.0 54.9 %collective-permute-start.1 = (bf16[4,12,1,7,256]{4,3,2,1,0:T(8,128)(2,1)}, bf16[4,12,1,7,256]{4,3,2,1,0:T(8,128)(2,1)}, u32[]{:S(2)}, u32[]{:S(2)}) collective-permute-start(bf16[4,12,1,7,256]{4,3,2,1,0:T(8,128)(2,1)} %get-tuple-element.113), channel_id=1, source_target_pairs={{2,0},{3,1},{6,4},{7,5},{10,8},{11,9},{14,12},{15,13},{18,16},{19,... | collective-permute-start | bytes 516104 | tf_op jit(solution)/shard_map/ppermute | solution.py:28
  158.0 40.3 %collective-permute-start.4 = (bf16[4,48,1,7,32]{1,4,3,2,0:T(8,128)(2,1)}, bf16[4,48,1,7,32]{1,4,3,2,0:T(8,128)(2,1)S(1)}, u32[]{:S(2)}, u32[]{:S(2)}) collective-permute-start(bf16[4,48,1,7,32]{1,4,3,2,0:T(8,128)(2,1)} %get-tuple-element.108), channel_id=1, source_target_pairs={{0,2},{1,3},{4,6},{5,7},{8,10},{9,11},{12,14},{13,15},{16,18},{17,... | collective-permute-start | bytes 258056 | tf_op jit(solution)/shard_map/ppermute | solution.py:26
  162.0 36.4 %collective-permute-start.5 = (bf16[4,48,1,7,32]{1,4,3,2,0:T(8,128)(2,1)}, bf16[4,48,1,7,32]{1,4,3,2,0:T(8,128)(2,1)}, u32[]{:S(2)}, u32[]{:S(2)}) collective-permute-start(bf16[4,48,1,7,32]{1,4,3,2,0:T(8,128)(2,1)} %get-tuple-element.109), channel_id=1, source_target_pairs={{2,0},{3,1},{6,4},{7,5},{10,8},{11,9},{14,12},{15,13},{18,16},{19,... | collective-permute-start | bytes 258056 | tf_op jit(solution)/shard_map/ppermute | solution.py:28
  199.7 25.3 %collective-permute-start.7 = (bf16[4,48,9,1,32]{1,4,3,2,0:T(8,128)(2,1)S(1)}, bf16[4,48,9,1,32]{1,4,3,2,0:T(8,128)(2,1)S(1)}, u32[]{:S(2)}, u32[]{:S(2)}) collective-permute-start(bf16[4,48,9,1,32]{1,4,3,2,0:T(8,128)(2,1)S(1)} %get-tuple-element.96), channel_id=1, source_target_pairs={{1,0},{3,2},{5,4},{7,6},{9,8},{11,10},{13,12},{15,14},{17,16},{19,... | collective-permute-start | bytes 331784 | tf_op jit(solution)/shard_map/ppermute | solution.py:28
  201.2 23.8 %collective-permute-start.6 = (bf16[4,48,9,1,32]{1,4,3,2,0:T(8,128)(2,1)S(1)}, bf16[4,48,9,1,32]{1,4,3,2,0:T(8,128)(2,1)S(1)}, u32[]{:S(2)}, u32[]{:S(2)}) collective-permute-start(bf16[4,48,9,1,32]{1,4,3,2,0:T(8,128)(2,1)S(1)} %get-tuple-element.97), channel_id=1, source_target_pairs={{0,1},{2,3},{4,5},{6,7},{8,9},{10,11},{12,13},{14,15},{16,17},{18,... | collective-permute-start | bytes 331784 | tf_op jit(solution)/shard_map/ppermute | solution.py:26
  211.4 30.9 %collective-permute-start.3 = (bf16[4,12,9,1,256]{4,3,2,1,0:T(2,128)(2,1)}, bf16[4,12,9,1,256]{4,3,2,1,0:T(2,128)(2,1)}, u32[]{:S(2)}, u32[]{:S(2)}) collective-permute-start(bf16[4,12,9,1,256]{4,3,2,1,0:T(2,128)(2,1)} %get-tuple-element.104), channel_id=1, source_target_pairs={{1,0},{3,2},{5,4},{7,6},{9,8},{11,10},{13,12},{15,14},{17,16},{19,... | collective-permute-start | bytes 663560 | tf_op jit(solution)/shard_map/ppermute | solution.py:28
  212.7 29.7 %collective-permute-start.2 = (bf16[4,12,9,1,256]{4,3,2,1,0:T(2,128)(2,1)}, bf16[4,12,9,1,256]{4,3,2,1,0:T(2,128)(2,1)}, u32[]{:S(2)}, u32[]{:S(2)}) collective-permute-start(bf16[4,12,9,1,256]{4,3,2,1,0:T(2,128)(2,1)} %get-tuple-element.105), channel_id=1, source_target_pairs={{0,1},{2,3},{4,5},{6,7},{8,9},{10,11},{12,13},{14,15},{16,17},{18,... | collective-permute-start | bytes 663560 | tf_op jit(solution)/shard_map/ppermute | solution.py:26
  295.0 230.2 %copy-start.139 = (f32[32]{0:T(128)}, f32[32]{0:T(128)S(1)}, u32[]{:S(2)}) copy-start(f32[32]{0:T(128)S(1)} %split.100) | copy-start | bytes 388
  295.0 45.7 %copy-start.154 = (f32[32]{0:T(128)S(1)}, f32[32]{0:T(128)}, u32[]{:S(2)}) copy-start(f32[32]{0:T(128)} %get-tuple-element.141) | copy-start | bytes 388
  295.0 45.7 %copy-start.157 = (f32[32]{0:T(128)S(1)}, f32[32]{0:T(128)}, u32[]{:S(2)}) copy-start(f32[32]{0:T(128)} %get-tuple-element.143) | copy-start | bytes 388
  298.6 45.3 %copy-start.136 = (bf16[32,128]{1,0:T(8,128)(2,1)S(1)}, bf16[32,128]{1,0:T(8,128)(2,1)}, u32[]{:S(2)}) copy-start(bf16[32,128]{1,0:T(8,128)(2,1)} %param.27) | copy-start | bytes 24580
  340.2 185.0 %copy-start.143 = (f32[32]{0:T(128)}, f32[32]{0:T(128)S(1)}, u32[]{:S(2)}) copy-start(f32[32]{0:T(128)S(1)} %get-tuple-element.139) | copy-start | bytes 388
  399.8 50.7 %copy-start.134 = (bf16[4,48]{1,0:T(4,128)(2,1)S(1)}, bf16[4,48]{1,0:T(4,128)(2,1)}, u32[]{:S(2)}) copy-start(bf16[4,48]{1,0:T(4,128)(2,1)} %copy-done.133) | copy-start | bytes 1156
  399.8 50.7 %copy-start.170 = (f32[128]{0:T(128)S(1)}, f32[128]{0:T(128)}, u32[]{:S(2)}) copy-start(f32[128]{0:T(128)} %slice.486) | copy-start | bytes 1540
  655.7 37.7 %collective-permute-start.9 = (bf16[4,12,1,7,256]{4,3,2,1,0:T(8,128)(2,1)S(1)}, bf16[4,12,1,7,256]{4,3,2,1,0:T(8,128)(2,1)S(1)}, u32[]{:S(2)}, u32[]{:S(2)}) collective-permute-start(bf16[4,12,1,7,256]{4,3,2,1,0:T(8,128)(2,1)S(1)} %copy-done.94), channel_id=1, source_target_pairs={{2,0},{3,1},{6,4},{7,5},{10,8},{11,9},{14,12},{15,13},{18,16},{19,... | collective-permute-start | bytes 516104 | tf_op jit(solution)/shard_map/ppermute | solution.py:28
  657.0 36.4 %collective-permute-start.8 = (bf16[4,12,1,7,256]{4,3,2,1,0:T(8,128)(2,1)S(1)}, bf16[4,12,1,7,256]{4,3,2,1,0:T(8,128)(2,1)S(1)}, u32[]{:S(2)}, u32[]{:S(2)}) collective-permute-start(bf16[4,12,1,7,256]{4,3,2,1,0:T(8,128)(2,1)S(1)} %copy-done.93), channel_id=1, source_target_pairs={{0,2},{1,3},{4,6},{5,7},{8,10},{9,11},{12,14},{13,15},{16,18},{17,... | collective-permute-start | bytes 516104 | tf_op jit(solution)/shard_map/ppermute | solution.py:26
  660.0 26.6 %collective-permute-start.13 = (bf16[4,48,1,7,32]{1,4,3,2,0:T(8,128)(2,1)S(1)}, bf16[4,48,1,7,32]{1,4,3,2,0:T(8,128)(2,1)S(1)}, u32[]{:S(2)}, u32[]{:S(2)}) collective-permute-start(bf16[4,48,1,7,32]{1,4,3,2,0:T(8,128)(2,1)S(1)} %copy-done.92), channel_id=1, source_target_pairs={{2,0},{3,1},{6,4},{7,5},{10,8},{11,9},{14,12},{15,13},{18,16},{19,... | collective-permute-start | bytes 258056 | tf_op jit(solution)/shard_map/ppermute | solution.py:28
  661.4 25.2 %collective-permute-start.12 = (bf16[4,48,1,7,32]{1,4,3,2,0:T(8,128)(2,1)S(1)}, bf16[4,48,1,7,32]{1,4,3,2,0:T(8,128)(2,1)S(1)}, u32[]{:S(2)}, u32[]{:S(2)}) collective-permute-start(bf16[4,48,1,7,32]{1,4,3,2,0:T(8,128)(2,1)S(1)} %copy-done.91), channel_id=1, source_target_pairs={{0,2},{1,3},{4,6},{5,7},{8,10},{9,11},{12,14},{13,15},{16,18},{17,... | collective-permute-start | bytes 258056 | tf_op jit(solution)/shard_map/ppermute | solution.py:26
  686.8 24.9 %collective-permute-start.15 = (bf16[4,48,9,1,32]{1,4,3,2,0:T(8,128)(2,1)S(1)}, bf16[4,48,9,1,32]{1,4,3,2,0:T(8,128)(2,1)S(1)}, u32[]{:S(2)}, u32[]{:S(2)}) collective-permute-start(bf16[4,48,9,1,32]{1,4,3,2,0:T(8,128)(2,1)S(1)} %get-tuple-element.92), channel_id=1, source_target_pairs={{0,1},{2,3},{4,5},{6,7},{8,9},{10,11},{12,13},{14,15},{16,17},{18,... | collective-permute-start | bytes 331784 | tf_op jit(solution)/shard_map/ppermute | solution.py:26
  691.0 14.0 %collective-permute-start.14 = (bf16[4,48,9,1,32]{1,4,3,2,0:T(8,128)(2,1)S(1)}, bf16[4,48,9,1,32]{1,4,3,2,0:T(8,128)(2,1)S(1)}, u32[]{:S(2)}, u32[]{:S(2)}) collective-permute-start(bf16[4,48,9,1,32]{1,4,3,2,0:T(8,128)(2,1)S(1)} %get-tuple-element.93), channel_id=1, source_target_pairs={{1,0},{3,2},{5,4},{7,6},{9,8},{11,10},{13,12},{15,14},{17,16},{19,... | collective-permute-start | bytes 331784 | tf_op jit(solution)/shard_map/ppermute | solution.py:28
  695.1 31.7 %collective-permute-start.11 = (bf16[4,12,9,1,256]{4,3,2,1,0:T(2,128)(2,1)}, bf16[4,12,9,1,256]{4,3,2,1,0:T(2,128)(2,1)}, u32[]{:S(2)}, u32[]{:S(2)}) collective-permute-start(bf16[4,12,9,1,256]{4,3,2,1,0:T(2,128)(2,1)} %get-tuple-element.100), channel_id=1, source_target_pairs={{0,1},{2,3},{4,5},{6,7},{8,9},{10,11},{12,13},{14,15},{16,17},{18,... | collective-permute-start | bytes 663560 | tf_op jit(solution)/shard_map/ppermute | solution.py:26
  700.4 26.4 %collective-permute-start.10 = (bf16[4,12,9,1,256]{4,3,2,1,0:T(2,128)(2,1)}, bf16[4,12,9,1,256]{4,3,2,1,0:T(2,128)(2,1)}, u32[]{:S(2)}, u32[]{:S(2)}) collective-permute-start(bf16[4,12,9,1,256]{4,3,2,1,0:T(2,128)(2,1)} %get-tuple-element.101), channel_id=1, source_target_pairs={{1,0},{3,2},{5,4},{7,6},{9,8},{11,10},{13,12},{15,14},{17,16},{19,... | collective-permute-start | bytes 663560 | tf_op jit(solution)/shard_map/ppermute | solution.py:28
  739.4 47.9 %copy-start.158 = (f32[32]{0:T(128)S(1)}, f32[32]{0:T(128)}, u32[]{:S(2)}) copy-start(f32[32]{0:T(128)} %get-tuple-element.136) | copy-start | bytes 388
  873.2 375.6 %all-reduce.18.cloned.1.call-start = ((), (), s32[]{:S(2)}) async-start(), calls=%async_computation.1 | async-start | bytes 26476544 | tf_op jit(solution)/shard_map/psum | solution.py:342
  (177 other events, 1514.6 us)
Sparse Core Ops, SparseCore 0:
  873.3 124.6 all-reduce.15
  1005.5 243.2 all-reduce.17
where the time goes:
time: 1280 us; the launch traced here: 1270 us
  blocking collectives  365 us (29%)
  matrix products  323 us (25%)
  waiting for transfers between devices  313 us (24%)
  other arithmetic  126 us (10%)
  local copies, waits for them, and re-layouts  81.5 us (6%)
  starting transfers between devices  44.2 us (3%)
  between operations  17.4 us (1%)
    psum x2, waiting for transfers between devices, on_device(): lax.psum((lateral_grads, slow_a_grad, slow_b_grad, slow_c_grad, slow_proj...  313 us
    dot_general x32, matrix products, product_back(): lax.dot_general(grads, weight, (((grads.ndim - 1,), (1,)), ((), ())), pre...  125 us
    psum x3, blocking collectives, moments(): spread = lax.psum(centred, ('clip', 'ha', 'wa')) / totals  123 us
    psum x3, blocking collectives, back_sums(): firsts, seconds = lax.psum((firsts, seconds), ('clip', 'ha', 'wa'))  121 us
    psum x3, blocking collectives, moments(): firsts = lax.psum(firsts, ('clip', 'ha', 'wa'))  121 us
    dot_general x32, matrix products, product(): lax.dot_general(values, weight, (((values.ndim - 1,), (0,)), ((), ())), p...  99.3 us
    dot_general x32, matrix products, weight_sum(): lax.dot_general(flat_values, flat_grads, (((0,), (0,)), ((), ())), prefer...  99.1 us
    unnamed x398, local copies, waits for them, and re-layouts  55.3 us
  transfers between devices with their start and end apart: 18, of which 2 were waited for; matrix products, arithmetic and copies ran while one was open for 14% of the time, Pallas kernels for 0%

commit v1 on v0

v1 whole, which is shorter than its diff:
```python
import functools

import jax
import jax.numpy as jnp
from jax import lax
from jax.experimental import pallas as pl
from jax.experimental.pallas import tpu as pltpu
from jax.sharding import PartitionSpec as P

ALPHA = 4
H = 14
W = 14
C_IN = 1024
C_LAT = 256
C_MID = 256
C_FAST = 128
C_FMID = 32
C_JOIN = C_IN + C_LAT
MIX = C_MID + ALPHA * C_FMID
WIDE_FAST = ALPHA * C_FAST

eps_norm = 1e-05
f32 = jnp.float32
bf16 = jnp.bfloat16
MESH = pl.DeviceIdType.MESH
MIB = 1 << 20


def dot(a, b):
    return lax.dot_general(a, b, (((1,), (0,)), ((), ())), preferred_element_type=f32)


def dot_nt(a, b):
    return lax.dot_general(a, b, (((1,), (1,)), ((), ())), preferred_element_type=f32)


def dot_tn(a, b):
    return lax.dot_general(a, b, (((0,), (0,)), ((), ())), preferred_element_type=f32)


def sigmoid(v):
    return 0.5 + 0.5 * jnp.tanh(0.5 * v)


def later(y, clips):
    return jnp.concatenate([jnp.zeros_like(y[:, :clips]), y[:, : y.shape[1] - clips]], axis=1)


def sooner(y, clips):
    return jnp.concatenate([y[:, clips:], jnp.zeros_like(y[:, :clips])], axis=1)


def rows_sum(v):
    return jnp.sum(jnp.sum(v, axis=0), axis=0, keepdims=True)


def phase_sum(v):
    out = v
    for k in range(1, ALPHA):
        out = out + pltpu.roll(v, k * C_FMID, 1)
    return out


def block_sum(v):
    return sum(v[:, p * C_FAST : (p + 1) * C_FAST] for p in range(ALPHA))


def spread(mask, width):
    return jnp.tile(mask, (1, width // 128))


def frames_matrix(wfa_ref, out_ref, ends_ref):
    out_ref[...] = jnp.zeros_like(out_ref)
    ends_ref[...] = jnp.zeros_like(ends_ref)
    for p in range(ALPHA):
        for s in range(max(p - 1, 0), min(p + 2, ALPHA)):
            out_ref[p * C_FMID : (p + 1) * C_FMID, s * C_FAST : (s + 1) * C_FAST] = wfa_ref[s - p + 1]
    ends_ref[0, 0:C_FMID] = wfa_ref[0]
    ends_ref[1, 3 * C_FMID :] = wfa_ref[2]


def expand_matrix(wfc_ref, out_ref):
    out_ref[...] = jnp.zeros_like(out_ref)
    for p in range(ALPHA):
        out_ref[p * C_FMID : (p + 1) * C_FMID, p * C_FAST : (p + 1) * C_FAST] = wfc_ref[...]


def first_convs(clips, xs, xf, m, perm, wl, wa, wp, wfa, x_out, f_out, z_out, zp_out, st, base_out,
                taps, ends, base, one, two):
    h = pl.program_id(0)
    cols = xs.shape[1]
    slab = m.shape[0]
    rows = cols * slab

    @pl.when(h == 0)
    def _():
        frames_matrix(wfa, taps, ends)

    mask_in = spread(m[...], C_IN).astype(bf16)
    for w in range(cols):
        x_out[w, :, :C_IN] = xs[:, w].reshape(slab, C_IN) * mask_in
        phases = dot(perm[...], xf[:, w].reshape(ALPHA * slab, C_FAST)).astype(bf16)
        for p in range(ALPHA):
            f_out[w, :, p * C_FAST : (p + 1) * C_FAST] = phases[p * slab : (p + 1) * slab]
    fast = f_out[...].reshape(rows, WIDE_FAST)
    lat = dot(fast[:, : 3 * C_FAST], wl[2:5].reshape(3 * C_FAST, C_LAT)).reshape(cols, slab, C_LAT)
    back = dot(fast[:, 2 * C_FAST :], wl[0:2].reshape(2 * C_FAST, C_LAT)).reshape(cols, slab, C_LAT)
    x_out[:, :, C_IN:] = (lat + later(back, clips)).astype(bf16)
    joined = x_out[...].reshape(rows, C_JOIN)
    za = dot(joined, wa[1]).reshape(cols, slab, C_MID)
    za = za + later(dot(joined, wa[0]).reshape(cols, slab, C_MID), clips)
    za = za + sooner(dot(joined, wa[2]).reshape(cols, slab, C_MID), clips)
    fa = dot_nt(fast, taps[...]).reshape(cols, slab, 128)
    fa = fa + later(dot_nt(fast[:, 3 * C_FAST :], ends[0]).reshape(cols, slab, 128), clips)
    fa = fa + sooner(dot_nt(fast[:, :C_FAST], ends[1]).reshape(cols, slab, 128), clips)
    zp = dot(joined, wp[...]).reshape(cols, slab, C_IN)
    z_out[:, :, :C_MID] = za
    z_out[:, :, C_MID:] = fa
    parts = ((0, za), (C_MID, fa), (MIX, zp))
    here = cols * jnp.sum(m[...], axis=0, keepdims=True)

    @pl.when(h == 0)
    def _():
        for at, z in parts:
            width = z.shape[-1]
            mean = rows_sum(z * spread(m[...], width)) / spread(here, width)
            if at == C_MID:
                mean = phase_sum(mean) * 0.25
            base[:, at : at + width] = mean
        one[...] = jnp.zeros_like(one)
        two[...] = jnp.zeros_like(two)

    for at, z in parts:
        width = z.shape[-1]
        off = z - base[:, at : at + width]
        if at == MIX:
            zp_out[...] = off.astype(bf16)
        off = off * spread(m[...], width)
        one[:, at : at + width] += rows_sum(off)
        two[:, at : at + width] += rows_sum(off * off)

    @pl.when(h == pl.num_programs(0) - 1)
    def _():
        count = pl.num_programs(0) * here
        base_out[...] = base[:, MIX:]
        finish_moments(st, base[...], one[...], two[...], count, ((0, C_MID, 0), (C_MID, 128, 1), (MIX, C_IN, 0)))


def finish_moments(st, base, one, two, count, parts):
    for at, width, fast in parts:
        s1 = one[:, at : at + width]
        s2 = two[:, at : at + width]
        if fast:
            s1 = phase_sum(s1) * 0.25
            s2 = phase_sum(s2) * 0.25
        n = spread(count.astype(f32), width)
        s1 = s1 / n
        st[0:1, at : at + width] = base[:, at : at + width] + s1
        st[1:2, at : at + width] = s2 / n - s1 * s1


def affine(moments, gain, shift, at, width):
    mean = moments[0:1, at : at + width]
    scale = lax.rsqrt(moments[1:2, at : at + width] + eps_norm)
    return mean, scale, gain[...], shift[...]


def space_convs(place, z1, row, col, corner, mom, gain, shift, m, wb, wfb, a_out, z_out, st, one, two):
    ha, wa = place[0], place[1]
    high, cols, slab, _ = z1.shape
    rows = cols * slab
    mean, scale, g, b = affine(mom, gain, shift, 0, MIX)
    mult = scale * g
    mask = spread(m[...], MIX)

    def act(z):
        v = (z - mean) * mult + b
        return (v * sigmoid(v) * mask).astype(bf16)

    far = high + 1
    a_out[far * ha] = jnp.zeros((cols + 2, slab, MIX), bf16)
    a_out[:, far * wa] = jnp.zeros((high + 2, slab, MIX), bf16)
    a_out[far * (1 - ha), 1 : 1 + cols] = act(row[...])
    a_out[1 : 1 + high, far * (1 - wa)] = act(col[...])
    a_out[far * (1 - ha), far * (1 - wa)] = act(corner[...])

    def fill(h, carry):
        a_out[h + 1, 1 : 1 + cols] = act(z1[h])
        return carry

    lax.fori_loop(0, high, fill, 0)

    def line(h, carry):
        slow = jnp.zeros((rows, C_MID), f32)
        fast = jnp.zeros((rows, 128), f32)
        for i in range(3):
            for j in range(3):
                v = a_out[h + i, j : j + cols].reshape(rows, MIX)
                slow = slow + dot(v[:, :C_MID], wb[i, j])
                fast = fast + dot(v[:, C_MID:], wfb[3 * i + j])
        z_out[h, :, :, :C_MID] = slow.reshape(cols, slab, C_MID)
        z_out[h, :, :, C_MID:] = fast.reshape(cols, slab, 128)
        return carry

    lax.fori_loop(0, high, line, 0)
    here = cols * jnp.sum(m[...], axis=0, keepdims=True)
    base = rows_sum(z_out[0] * mask) / spread(here, MIX)
    base = jnp.concatenate([base[:, :C_MID], phase_sum(base[:, C_MID:]) * 0.25], axis=1)
    one[...] = jnp.zeros_like(one)
    two[...] = jnp.zeros_like(two)

    def gather(h, carry):
        off = (z_out[h] - base) * mask
        one[...] += rows_sum(off)
        two[...] += rows_sum(off * off)
        return carry

    lax.fori_loop(0, high, gather, 0)
    finish_moments(st, base, one[...], two[...], high * here, ((0, C_MID, 0), (C_MID, 128, 1)))


def expand_moments(z2, mom, gain, shift, m, wc, wfc, a_out, st, big, base, one, two):
    h = pl.program_id(0)
    cols, slab, _ = z2.shape
    rows = cols * slab

    @pl.when(h == 0)
    def _():
        expand_matrix(wfc, big)

    mean, scale, g, b = affine(mom, gain, shift, 0, MIX)
    v = (z2[...] - mean) * (scale * g) + b
    a_out[...] = (v * sigmoid(v) * spread(m[...], MIX)).astype(bf16)
    a2 = a_out[...].reshape(rows, MIX)
    zc = dot(a2[:, :C_MID], wc[...]).reshape(cols, slab, C_IN)
    fc = dot(a2[:, C_MID:], big[...]).reshape(cols, slab, WIDE_FAST)
    here = cols * jnp.sum(m[...], axis=0, keepdims=True)

    @pl.when(h == 0)
    def _():
        base[:, :C_IN] = rows_sum(zc * spread(m[...], C_IN)) / spread(here, C_IN)
        base[:, C_IN:] = block_sum(rows_sum(fc * spread(m[...], WIDE_FAST))) / (4.0 * here)
        one[...] = jnp.zeros_like(one)
        two[...] = jnp.zeros_like(two)

    off = (zc - base[:, :C_IN]) * spread(m[...], C_IN)
    one[:, :C_IN] += rows_sum(off)
    two[:, :C_IN] += rows_sum(off * off)
    off = (fc - jnp.tile(base[:, C_IN:], (1, ALPHA))) * spread(m[...], WIDE_FAST)
    one[:, C_IN:] += block_sum(rows_sum(off)) * 0.25
    two[:, C_IN:] += block_sum(rows_sum(off * off)) * 0.25

    @pl.when(h == pl.num_programs(0) - 1)
    def _():
        count = pl.num_programs(0) * here
        finish_moments(st, base[...], one[...], two[...], count, ((0, C_IN + C_FAST, 0),))


def outputs(a2, zp, base, mom1, mom3, sgain, sshift, fgain, fshift, cot, fcot, fast_in, m, perm, wc, wfc,
            so, fo, gs, gf, sums, big):
    h = pl.program_id(0)
    cols, slab, _ = a2.shape

    @pl.when(h == 0)
    def _():
        expand_matrix(wfc, big)
        sums[...] = jnp.zeros_like(sums)

    mask = spread(m[...], C_IN)
    mean_c = mom3[0:1, :C_IN]
    scale_c = lax.rsqrt(mom3[1:2, :C_IN] + eps_norm)
    mean_p = mom1[0:1, MIX:] - base[...]
    scale_p = lax.rsqrt(mom1[1:2, MIX:] + eps_norm)
    mean_f = jnp.tile(mom3[0:1, C_IN:], (1, ALPHA))
    scale_f = jnp.tile(lax.rsqrt(mom3[1:2, C_IN:] + eps_norm), (1, ALPHA))
    gain_c, gain_p = sgain[:, :C_IN], sgain[:, C_IN:]
    shift_cp = sshift[:, :C_IN] + sshift[:, C_IN:]
    gain_f = jnp.tile(fgain[...], (1, ALPHA))
    shift_f = jnp.tile(fshift[...], (1, ALPHA))

    def tile_sum(v):
        return jnp.sum(v.reshape(slab // 8, 8, v.shape[-1]), axis=0)

    totals = [jnp.zeros((8, C_IN), f32)] * 3 + [jnp.zeros((8, WIDE_FAST), f32)] * 2
    for w in range(cols):
        zc = (dot(a2[w, :, :C_MID], wc[...]) - mean_c) * scale_c
        zq = (zp[w].astype(f32) - mean_p) * scale_p
        ps = gain_c * zc + gain_p * zq + shift_cp
        sig = sigmoid(ps)
        so[:, w] = (ps * sig * mask).astype(bf16).reshape(slab // cot.shape[2], cot.shape[2], C_IN)
        back = cot[:, w].reshape(slab, C_IN).astype(f32) * (sig * (1.0 + ps * (1.0 - sig)) * mask)
        gs[w] = back
        totals[0] += tile_sum(back)
        totals[1] += tile_sum(back * zc)
        totals[2] += tile_sum(back * zq)
        fc = (dot(a2[w, :, C_MID:], big[...]) - mean_f) * scale_f
        pf = gain_f * fc + shift_f + fast_in[w].astype(f32)
        sig = sigmoid(pf)
        res = (pf * sig).astype(bf16)
        stacked = jnp.concatenate([res[:, p * C_FAST : (p + 1) * C_FAST] for p in range(ALPHA)], axis=0)
        fo[:, w] = dot_tn(perm[...], stacked).astype(bf16).reshape(fo.shape[0], slab, C_FAST)
        phases = dot(perm[...], fcot[:, w].reshape(ALPHA * slab, C_FAST))
        wide = jnp.concatenate([phases[p * slab : (p + 1) * slab] for p in range(ALPHA)], axis=1)
        fback = wide * (sig * (1.0 + pf * (1.0 - sig)))
        gf[w] = fback
        totals[3] += tile_sum(fback)
        totals[4] += tile_sum(fback * fc)
    for k in range(3):
        sums[:, k * C_IN : (k + 1) * C_IN] += jnp.sum(totals[k], axis=0, keepdims=True)
    for k in range(2):
        at = 3 * C_IN + k * C_FAST
        sums[:, at : at + C_FAST] += block_sum(jnp.sum(totals[3 + k], axis=0, keepdims=True))


def expand_back(gs, gf, a2, zp, base, z2, mom1, mom2, mom3, tot, inv, sgain, fgain, gain2, shift2, m, wc, wfc,
                dzc_out, dzp_out, dfc_out, q_out, sums, big):
    h = pl.program_id(0)
    cols, slab, _ = a2.shape
    rows = cols * slab

    @pl.when(h == 0)
    def _():
        expand_matrix(wfc, big)
        sums[...] = jnp.zeros_like(sums)

    mask = spread(m[...], C_IN)
    inv_s = spread(inv[...], C_IN)
    inv_f = 0.25 * inv[...]
    mean_c = mom3[0:1, :C_IN]
    scale_c = lax.rsqrt(mom3[1:2, :C_IN] + eps_norm)
    mean_p = mom1[0:1, MIX:] - base[...]
    scale_p = lax.rsqrt(mom1[1:2, MIX:] + eps_norm)
    mean_f = jnp.tile(mom3[0:1, C_IN:], (1, ALPHA))
    scale_f = jnp.tile(lax.rsqrt(mom3[1:2, C_IN:] + eps_norm), (1, ALPHA))
    mult_c = sgain[:, :C_IN] * scale_c
    mult_p = sgain[:, C_IN:] * scale_p
    mult_f = jnp.tile(fgain[...], (1, ALPHA)) * scale_f
    first_s = tot[:, :C_IN] * inv_s
    second_c = tot[:, C_IN : 2 * C_IN] * inv_s
    second_p = tot[:, 2 * C_IN : 3 * C_IN] * inv_s
    first_f = jnp.tile(tot[:, 3 * C_IN : 3 * C_IN + C_FAST] * inv_f, (1, ALPHA))
    second_f = jnp.tile(tot[:, 3 * C_IN + C_FAST :] * inv_f, (1, ALPHA))
    mask_f = spread(m[...], WIDE_FAST)
    for w in range(cols):
        zc = (dot(a2[w, :, :C_MID], wc[...]) - mean_c) * scale_c
        zq = (zp[w].astype(f32) - mean_p) * scale_p
        g = gs[w].astype(f32)
        dzc_out[w] = (mult_c * (g - mask * (first_s + zc * second_c))).astype(bf16)
        dzp_out[w] = (mult_p * (g - mask * (first_s + zq * second_p))).astype(bf16)
        fc = (dot(a2[w, :, C_MID:], big[...]) - mean_f) * scale_f
        dfc_out[w] = (mult_f * (gf[w].astype(f32) - mask_f * (first_f + fc * second_f))).astype(bf16)
    da = dot_nt(dzc_out[...].reshape(rows, C_IN), wc[...]).reshape(cols, slab, C_MID)
    df = dot_nt(dfc_out[...].reshape(rows, WIDE_FAST), big[...]).reshape(cols, slab, 128)
    grads = jnp.concatenate([da, df], axis=2)
    slope_back(grads, z2[...], mom2, gain2, shift2, m, q_out, sums)


def slope_back(grads, z, mom, gain, shift, m, q_out, sums):
    mean, scale, g, b = affine(mom, gain, shift, 0, MIX)
    zhat = (z - mean) * scale
    v = g * zhat + b
    sig = sigmoid(v)
    q = grads * (sig * (1.0 + v * (1.0 - sig)) * spread(m[...], MIX))
    q_out[...] = q
    for k, s in enumerate((rows_sum(q), rows_sum(q * zhat))):
        at = k * MIX
        sums[:, at : at + C_MID] += s[:, :C_MID]
        sums[:, at + C_MID : at + MIX] += phase_sum(s[:, C_MID:])


def expand_weights(x, a2, dzp, dzc, dfc, wp_out, wc_out, wfc_out):
    i = pl.program_id(0)
    n, slab, _ = x.shape
    rows = n * slab
    wp_out[...] = dot_tn(x[...].reshape(rows, C_MID), dzp[...].reshape(rows, C_IN))

    @pl.when(i == pl.num_programs(0) - 1)
    def _():
        a = a2[...].reshape(rows, MIX)
        wc_out[...] = dot_tn(a[:, :C_MID], dzc[...].reshape(rows, C_IN))
        wide = dot_tn(a[:, C_MID:], dfc[...].reshape(rows, WIDE_FAST))
        wfc_out[...] = sum(
            wide[p * C_FMID : (p + 1) * C_FMID, p * C_FAST : (p + 1) * C_FAST] for p in range(ALPHA)
        )


def norm_terms(mom, gain, tot, inv):
    mean = mom[0:1, :MIX]
    scale = lax.rsqrt(mom[1:2, :MIX] + eps_norm)
    share = jnp.concatenate([spread(inv[...], C_MID), 0.25 * inv[...]], axis=1)
    return mean, scale, gain[...] * scale, tot[:, :MIX] * share, tot[:, MIX:] * share


def space_back(place, q2, z2, qrow, qcol, qcorner, zrow, zcol, zcorner, a1, z1, mom1, mom2, tot, inv, gain1, shift1,
               gain2, m, wb, wfb, q_out, sums, wb_out, wfb_out, wide, keep, keep_f):
    ha, wa = place[0], place[1]
    high, cols, slab, _ = z1.shape
    rows = cols * slab
    mean, scale, mult, first, second = norm_terms(mom2, gain2, tot, inv)
    mask = spread(m[...], MIX)

    def grad(q, z):
        return (mult * (q - mask * (first + (z - mean) * scale * second))).astype(bf16)

    far = high + 1
    wide[far * ha] = jnp.zeros((cols + 2, slab, MIX), bf16)
    wide[:, far * wa] = jnp.zeros((high + 2, slab, MIX), bf16)
    wide[far * (1 - ha), 1 : 1 + cols] = grad(qrow[...], zrow[...])
    wide[1 : 1 + high, far * (1 - wa)] = grad(qcol[...], zcol[...])
    wide[far * (1 - ha), far * (1 - wa)] = grad(qcorner[...], zcorner[...])

    def fill(h, carry):
        wide[h + 1, 1 : 1 + cols] = grad(q2[h], z2[h])
        return carry

    lax.fori_loop(0, high, fill, 0)
    sums[...] = jnp.zeros_like(sums)
    keep[...] = jnp.zeros_like(keep)
    keep_f[...] = jnp.zeros_like(keep_f)

    def line(h, carry):
        slow = jnp.zeros((rows, C_MID), f32)
        fast = jnp.zeros((rows, 128), f32)
        for i in range(3):
            for j in range(3):
                v = wide[h + 2 - i, 2 - j : 2 - j + cols].reshape(rows, MIX)
                slow = slow + dot_nt(v[:, :C_MID], wb[i, j])
                fast = fast + dot_nt(v[:, C_MID:], wfb[3 * i + j])
        grads = jnp.concatenate([slow, fast], axis=1).reshape(cols, slab, MIX)
        slope_back(grads, z1[h], mom1, gain1, shift1, m, q_out.at[h], sums)
        d = wide[h + 1, 1 : 1 + cols].reshape(rows, MIX)
        for i in range(3):
            for j in range(3):
                v = a1[h + i, j : j + cols].reshape(rows, MIX)
                keep[i, j] += dot_tn(v[:, :C_MID], d[:, :C_MID])
                keep_f[3 * i + j] += dot_tn(v[:, C_MID:], d[:, C_MID:])
        return carry

    lax.fori_loop(0, high, line, 0)
    wb_out[...] = keep[...]
    for k in range(9):
        wfb_out[k] = sum(
            keep_f[k, p * C_FMID : (p + 1) * C_FMID, p * C_FMID : (p + 1) * C_FMID] for p in range(ALPHA)
        )


def first_back(clips, q1, z1, mom1, tot, inv, gain1, m, perm, dzp, gf, wl, wa, wp, wfa, sx, fx, da_out, dl_out, df_out,
               taps, ends):
    h = pl.program_id(0)
    cols, slab, _ = q1.shape
    rows = cols * slab

    @pl.when(h == 0)
    def _():
        frames_matrix(wfa, taps, ends)

    mean, scale, mult, first, second = norm_terms(mom1, gain1, tot, inv)
    zhat = (z1[...] - mean) * scale
    dz = mult * (q1[...] - spread(m[...], MIX) * (first + zhat * second))
    up, down = sooner(dz, clips), later(dz, clips)
    for k, v in enumerate((up, dz, down)):
        da_out[:, :, k * C_MID : (k + 1) * C_MID] = v[:, :, :C_MID].astype(bf16)
        df_out[:, :, k * 128 : (k + 1) * 128] = v[:, :, C_MID:].astype(bf16)
    dj = dot_nt(dzp[...].reshape(rows, C_IN), wp[...])
    for k in range(3):
        dj = dj + dot_nt(da_out[:, :, k * C_MID : (k + 1) * C_MID].reshape(rows, C_MID), wa[k])
    mask = spread(m[...], C_IN)
    dj = dj.reshape(cols, slab, C_JOIN)
    for w in range(cols):
        sx[:, w] = (dj[w, :, :C_IN] * mask).astype(bf16).reshape(slab // clips, clips, C_IN)
    dlat = dj[:, :, C_IN:].astype(bf16).astype(f32)
    dl_out[:, :, :C_LAT] = dlat.astype(bf16)
    dl_out[:, :, C_LAT:] = sooner(dlat, clips).astype(bf16)
    df = df_out[...].reshape(rows, 3 * 128)
    dl = dl_out[...].reshape(rows, 2 * C_LAT)
    total = gf[...].reshape(rows, WIDE_FAST).astype(f32) + dot(df[:, 128:256], taps[...])
    head = dot_nt(dl[:, :C_LAT], wl[2:5].reshape(3 * C_FAST, C_LAT))
    tail = dot_nt(dl[:, C_LAT:], wl[0:2].reshape(2 * C_FAST, C_LAT))
    blocks = [total[:, p * C_FAST : (p + 1) * C_FAST] for p in range(ALPHA)]
    for p in range(3):
        blocks[p] = blocks[p] + head[:, p * C_FAST : (p + 1) * C_FAST]
    for p in range(2):
        blocks[2 + p] = blocks[2 + p] + tail[:, p * C_FAST : (p + 1) * C_FAST]
    blocks[3] = blocks[3] + dot(df[:, :128], ends[0])
    blocks[0] = blocks[0] + dot(df[:, 256:], ends[1])
    blocks = [v.astype(bf16) for v in blocks]
    for w in range(cols):
        stacked = jnp.concatenate([v[w * slab : (w + 1) * slab] for v in blocks], axis=0)
        fx[:, w] = dot_tn(perm[...], stacked).astype(bf16).reshape(clips, slab, C_FAST)


def first_weights(x, f, da, dl, df, wa_out, wl_out, wfa_out):
    i = pl.program_id(0)
    n, slab, _ = x.shape
    rows = n * slab
    for k in range(3):
        wa_out[k] = dot_tn(x[...].reshape(rows, C_MID), da[:, :, k * C_MID : (k + 1) * C_MID].reshape(rows, C_MID))

    @pl.when(i == pl.num_programs(0) - 1)
    def _():
        fast = f[...].reshape(rows, WIDE_FAST)
        d = dl[...].reshape(rows, 2 * C_LAT)
        wl_out[2:5] = dot_tn(fast[:, : 3 * C_FAST], d[:, :C_LAT]).reshape(3, C_FAST, C_LAT)
        wl_out[0:2] = dot_tn(fast[:, 2 * C_FAST :], d[:, C_LAT:]).reshape(2, C_FAST, C_LAT)
        g = df[...].reshape(rows, 3 * 128)
        mid = dot_tn(g[:, 128:256], fast)
        sums = [jnp.zeros((C_FMID, C_FAST), f32) for _ in range(3)]
        for p in range(ALPHA):
            for s in range(max(p - 1, 0), min(p + 2, ALPHA)):
                sums[s - p + 1] += mid[p * C_FMID : (p + 1) * C_FMID, s * C_FAST : (s + 1) * C_FAST]
        sums[0] += dot_tn(g[:, :128], fast[:, 3 * C_FAST :])[:C_FMID]
        sums[2] += dot_tn(g[:, 256:], fast[:, :C_FAST])[3 * C_FMID :]
        for k in range(3):
            wfa_out[k] = sums[k]


def exchange(n_clip, moments, edges, *refs):
    refs = list(refs)
    part, weight = refs.pop(0), refs.pop(0)
    source = refs.pop(0) if edges else None
    out = refs.pop(0)
    rims = [refs.pop(0) for _ in range(3)] if edges else None
    near, mid, far, near_send, near_recv, far_send, far_recv = refs[:7]
    refs = refs[7:]
    clip, ha, wa = lax.axis_index("clip"), lax.axis_index("ha"), lax.axis_index("wa")
    me = 2 * ha + wa
    peers = [(1 - ha, wa), (ha, 1 - wa), (1 - ha, 1 - wa)]
    if edges:
        line, side, packs, lands, local_sem, rim_send, rim_recv = refs
        high, cols = source.shape[0], source.shape[1]
        first = pltpu.make_async_copy(source.at[(high - 1) * (1 - ha)], line, local_sem.at[0])
        second = pltpu.make_async_copy(source.at[:, (cols - 1) * (1 - wa)], side, local_sem.at[1])
        first.start()
        second.start()
    barrier = pltpu.get_barrier_semaphore()
    for a, b in peers:
        pl.semaphore_signal(barrier, inc=1, device_id=(clip, a, b), device_id_type=MESH)
    for d in range(1, n_clip):
        other = lax.rem(clip + d, n_clip)
        pl.semaphore_signal(barrier, inc=1, device_id=(other, ha, wa), device_id_type=MESH)
    pl.semaphore_wait(barrier, 3 + n_clip - 1)
    copies = []
    for k, (a, b) in enumerate(peers):
        copy = pltpu.make_async_remote_copy(
            src_ref=part, dst_ref=near.at[me], send_sem=near_send.at[k], recv_sem=near_recv.at[me],
            device_id=(clip, a, b), device_id_type=MESH,
        )
        copy.start()
        copies.append(copy)
    if edges:
        first.wait()
        second.wait()
        centre = part[0:1, :MIX] if moments else jnp.zeros((1, MIX), f32)
        packs[0, : cols] = (line[...] - centre).astype(bf16)
        packs[1, : high] = (side[...] - centre).astype(bf16)
        packs[2, 0] = packs[0, (cols - 1) * (1 - wa)]
        for k, (a, b) in enumerate(peers):
            size = 1 if k == 2 else cols
            copy = pltpu.make_async_remote_copy(
                src_ref=packs.at[k, pl.ds(0, size)], dst_ref=lands.at[k, pl.ds(0, size)],
                send_sem=rim_send.at[k], recv_sem=rim_recv.at[k], device_id=(clip, a, b), device_id_type=MESH,
            )
            copy.start()
            copies.append(copy)
    near[me] = part[...]
    for a, b in peers:
        other = 2 * a + b
        pltpu.make_async_remote_copy(
            src_ref=part, dst_ref=near.at[other], send_sem=near_send.at[0], recv_sem=near_recv.at[other],
            device_id=(clip, a, b), device_id_type=MESH,
        ).wait_recv()
    if moments:
        mean = (near[0, 0:1] + near[1, 0:1] + near[2, 0:1] + near[3, 0:1]) * 0.25
        var = sum(near[k, 1:2] + (near[k, 0:1] - mean) ** 2 for k in range(4)) * 0.25
        mid[0:1] = mean
        mid[1:2] = var
    else:
        mid[...] = near[0] + near[1] + near[2] + near[3]
    for d in range(1, n_clip):
        other = lax.rem(clip + d, n_clip)
        copy = pltpu.make_async_remote_copy(
            src_ref=mid, dst_ref=far.at[clip], send_sem=far_send.at[d], recv_sem=far_recv.at[clip],
            device_id=(other, ha, wa), device_id_type=MESH,
        )
        copy.start()
        copies.append(copy)
    far[clip] = mid[...]
    for d in range(1, n_clip):
        other = lax.rem(clip + d, n_clip)
        pltpu.make_async_remote_copy(
            src_ref=mid, dst_ref=far.at[other], send_sem=far_send.at[0], recv_sem=far_recv.at[other],
            device_id=(other, ha, wa), device_id_type=MESH,
        ).wait_recv()
    width = out.shape[1]
    if moments:
        mean = sum(far[k, 0:1] * spread(weight[k], width) for k in range(n_clip))
        var = sum((far[k, 1:2] + (far[k, 0:1] - mean) ** 2) * spread(weight[k], width) for k in range(n_clip))
        out[0:1] = mean
        out[1:2] = var
    else:
        out[...] = sum(far[k] for k in range(n_clip))
    if edges:
        for k, (a, b) in enumerate(peers):
            size = 1 if k == 2 else cols
            pltpu.make_async_remote_copy(
                src_ref=packs.at[k, pl.ds(0, size)], dst_ref=lands.at[k, pl.ds(0, size)],
                send_sem=rim_send.at[k], recv_sem=rim_recv.at[k], device_id=(clip, a, b), device_id_type=MESH,
            ).wait_recv()
            centre = near[2 * a + b, 0:1, :MIX] if moments else jnp.zeros((1, MIX), f32)
            land = lands[k, 0].astype(f32) if k == 2 else lands[k, 0:cols].astype(f32)
            rims[k][...] = land + centre
    for copy in copies:
        copy.wait_send()


def vmem_spec():
    return pl.BlockSpec(memory_space=pltpu.VMEM)


def run_exchange(ident, n_clip, part, weight, moments, source=None):
    edges = source is not None
    count, width = part.shape
    out_shape = [jax.ShapeDtypeStruct((count, width), f32)]
    ins = [part, weight]
    in_specs = [vmem_spec(), vmem_spec()]
    scratch = [
        pltpu.VMEM((4, count, width), f32),
        pltpu.VMEM((count, width), f32),
        pltpu.VMEM((n_clip, count, width), f32),
        pltpu.SemaphoreType.DMA((3,)),
        pltpu.SemaphoreType.DMA((4,)),
        pltpu.SemaphoreType.DMA((n_clip,)),
        pltpu.SemaphoreType.DMA((n_clip,)),
    ]
    if edges:
        high, cols, slab, _ = source.shape
        ins.append(source)
        in_specs.append(pl.BlockSpec(memory_space=pl.ANY))
        out_shape += [
            jax.ShapeDtypeStruct((cols, slab, MIX), f32),
            jax.ShapeDtypeStruct((high, slab, MIX), f32),
            jax.ShapeDtypeStruct((slab, MIX), f32),
        ]
        scratch += [
            pltpu.VMEM((cols, slab, MIX), f32),
            pltpu.VMEM((high, slab, MIX), f32),
            pltpu.VMEM((3, cols, slab, MIX), bf16),
            pltpu.VMEM((3, cols, slab, MIX), bf16),
            pltpu.SemaphoreType.DMA((2,)),
            pltpu.SemaphoreType.DMA((3,)),
            pltpu.SemaphoreType.DMA((3,)),
        ]
    return pl.pallas_call(
        functools.partial(exchange, n_clip, moments, edges),
        out_shape=tuple(out_shape),
        in_specs=in_specs,
        out_specs=tuple(vmem_spec() for _ in out_shape),
        scratch_shapes=scratch,
        compiler_params=pltpu.CompilerParams(
            collective_id=ident, has_side_effects=True, vmem_limit_bytes=16 * MIB
        ),
        name=f"exchange{ident}",
    )(*ins)


def whole(shape):
    return pl.BlockSpec(shape, lambda h: (0,) * len(shape))


def per_line(shape):
    return pl.BlockSpec((None,) + tuple(shape), lambda h: (h,) + (0,) * len(shape))


def params(limit):
    return pltpu.CompilerParams(vmem_limit_bytes=limit * MIB)


def shaped(shape, kind):
    return jax.ShapeDtypeStruct(shape, kind)


def on_device(
    slow_input,
    fast_input,
    frame_counts,
    lateral_weight,
    slow_a_weight,
    slow_b_weight,
    slow_c_weight,
    slow_proj_weight,
    fast_a_weight,
    fast_b_weight,
    fast_c_weight,
    slow_gain,
    slow_shift,
    fast_gain,
    fast_shift,
    slow_cotangent,
    fast_cotangent,
):
    n_clip = lax.axis_size("clip")
    clips, frames, high, cols, _ = slow_input.shape
    slab = clips * frames
    own = lax.dynamic_slice_in_dim(frame_counts, lax.axis_index("clip") * clips, clips)
    row_t = jnp.arange(slab) // clips
    row_c = jnp.arange(slab) % clips
    real = row_t < own[row_c]
    m = jnp.broadcast_to(real.astype(f32)[:, None], (slab, 128))
    col_c = jnp.arange(ALPHA * slab) // (ALPHA * frames)
    col_f = jnp.arange(ALPHA * slab) % (ALPHA * frames)
    want_f = (ALPHA * row_t[None, :] + jnp.arange(ALPHA)[:, None]).reshape(-1)
    want_c = jnp.tile(row_c, ALPHA)
    perm = (
        (want_f[:, None] == col_f[None, :]) & (want_c[:, None] == col_c[None, :]) & jnp.tile(real, ALPHA)[:, None]
    ).astype(bf16)
    real_total = jnp.sum(frame_counts).astype(f32)
    weight = jnp.broadcast_to(
        (jnp.sum(frame_counts.reshape(n_clip, clips), axis=1).astype(f32) / real_total)[:, None, None], (n_clip, 1, 128)
    )
    inv = jnp.full((1, 128), 1.0, f32) / (real_total * (H * W))
    place = jnp.stack([lax.axis_index("ha"), lax.axis_index("wa")]).astype(jnp.int32)

    def mixed(slow, fast, k):
        lo = fast[k * C_FMID : (k + 1) * C_FMID]
        return jnp.concatenate([slow[k * C_MID : (k + 1) * C_MID], jnp.tile(lo, ALPHA)])[None]

    gain1, shift1 = mixed(slow_gain, fast_gain, 0), mixed(slow_shift, fast_shift, 0)
    gain2, shift2 = mixed(slow_gain, fast_gain, 1), mixed(slow_shift, fast_shift, 1)
    sgain, sshift = slow_gain[None, 2 * C_MID :], slow_shift[None, 2 * C_MID :]
    fgain, fshift = fast_gain[None, 2 * C_FMID :], fast_shift[None, 2 * C_FMID :]
    wfa = fast_a_weight.transpose(0, 2, 1)
    eye = jnp.eye(ALPHA, dtype=bf16)
    wfb = (eye[None, :, None, :, None] * fast_b_weight.reshape(9, 1, C_FMID, 1, C_FMID)).reshape(9, 128, 128)

    xs = slow_input.transpose(1, 2, 3, 0, 4)
    xf = fast_input.transpose(0, 2, 3, 1, 4)
    cot = slow_cotangent.transpose(1, 2, 3, 0, 4)
    fcot = fast_cotangent.transpose(0, 2, 3, 1, 4)
    slow_block = pl.BlockSpec((frames, None, cols, clips, C_IN), lambda h: (0, h, 0, 0, 0))
    fast_block = pl.BlockSpec((clips, None, cols, ALPHA * frames, C_FAST), lambda h: (0, h, 0, 0, 0))

    def lines(c, kind):
        return shaped((high, cols, slab, c), kind)

    m_spec = whole((slab, 128))
    perm_spec = whole((ALPHA * slab, ALPHA * slab))
    L1 = MIX + C_IN
    x, f, z1, zp, st1, base = pl.pallas_call(
        functools.partial(first_convs, clips),
        grid=(high,),
        in_specs=[
            slow_block, fast_block, m_spec, perm_spec, whole((5, C_FAST, C_LAT)), whole((3, C_JOIN, C_MID)),
            whole((C_JOIN, C_IN)), whole((3, C_FMID, C_FAST)),
        ],
        out_specs=(
            per_line((cols, slab, C_JOIN)), per_line((cols, slab, WIDE_FAST)), per_line((cols, slab, MIX)),
            per_line((cols, slab, C_IN)), whole((2, L1)), whole((1, C_IN)),
        ),
        out_shape=(
            lines(C_JOIN, bf16), lines(WIDE_FAST, bf16), lines(MIX, f32), lines(C_IN, bf16), shaped((2, L1), f32),
            shaped((1, C_IN), f32),
        ),
        scratch_shapes=[
            pltpu.VMEM((128, WIDE_FAST), bf16), pltpu.VMEM((2, 128, C_FAST), bf16), pltpu.VMEM((1, L1), f32),
            pltpu.VMEM((1, L1), f32), pltpu.VMEM((1, L1), f32),
        ],
        compiler_params=params(40),
        name="first_convs",
    )(xs, xf, m, perm, lateral_weight, slow_a_weight, slow_proj_weight, wfa)

    mom1, row1, col1, corner1 = run_exchange(1, n_clip, st1, weight, True, z1)
    smem = pl.BlockSpec(memory_space=pltpu.SMEM)
    vm = vmem_spec()
    a1, z2, st2 = pl.pallas_call(
        space_convs,
        in_specs=[smem] + [vm] * 10,
        out_specs=(vm, vm, vm),
        out_shape=(
            shaped((high + 2, cols + 2, slab, MIX), bf16), lines(MIX, f32), shaped((2, MIX), f32),
        ),
        scratch_shapes=[pltpu.VMEM((1, MIX), f32), pltpu.VMEM((1, MIX), f32)],
        compiler_params=params(32),
        name="space_convs",
    )(place, z1, row1, col1, corner1, mom1, gain1, shift1, m, slow_b_weight, wfb)
    mom2, zrow, zcol, zcorner = run_exchange(2, n_clip, st2, weight, True, z2)

    L3 = C_IN + C_FAST
    a2, st3 = pl.pallas_call(
        expand_moments,
        grid=(high,),
        in_specs=[
            per_line((cols, slab, MIX)), whole((2, MIX)), whole((1, MIX)), whole((1, MIX)), m_spec, whole((C_MID, C_IN)),
            whole((C_FMID, C_FAST)),
        ],
        out_specs=(per_line((cols, slab, MIX)), whole((2, L3))),
        out_shape=(lines(MIX, bf16), shaped((2, L3), f32)),
        scratch_shapes=[pltpu.VMEM((128, WIDE_FAST), bf16)] + [pltpu.VMEM((1, L3), f32)] * 3,
        compiler_params=params(24),
        name="expand_moments",
    )(z2, mom2, gain2, shift2, m, slow_c_weight, fast_c_weight)
    (mom3,) = run_exchange(3, n_clip, st3, weight, True)

    L4 = 3 * C_IN + 2 * C_FAST
    so, fo, gs, gf, part4 = pl.pallas_call(
        outputs,
        grid=(high,),
        in_specs=[
            per_line((cols, slab, MIX)), per_line((cols, slab, C_IN)), whole((1, C_IN)), whole((2, L1)), whole((2, L3)),
            whole((1, 2 * C_IN)), whole((1, 2 * C_IN)), whole((1, C_FAST)), whole((1, C_FAST)), slow_block, fast_block,
            per_line((cols, slab, WIDE_FAST)), m_spec, perm_spec, whole((C_MID, C_IN)), whole((C_FMID, C_FAST)),
        ],
        out_specs=(
            slow_block, fast_block, per_line((cols, slab, C_IN)), per_line((cols, slab, WIDE_FAST)), whole((1, L4)),
        ),
        out_shape=(
            shaped(xs.shape, bf16), shaped(xf.shape, bf16), lines(C_IN, f32), lines(WIDE_FAST, f32),
            shaped((1, L4), f32),
        ),
        scratch_shapes=[pltpu.VMEM((128, WIDE_FAST), bf16)],
        compiler_params=params(32),
        name="outputs",
    )(a2, zp, base, mom1, mom3, sgain, sshift, fgain, fshift, cot, fcot, f, m, perm, slow_c_weight, fast_c_weight)
    (tot4,) = run_exchange(4, n_clip, part4, weight, False)

    dzc, dzp, dfc, q2, part5 = pl.pallas_call(
        expand_back,
        grid=(high,),
        in_specs=[
            per_line((cols, slab, C_IN)), per_line((cols, slab, WIDE_FAST)), per_line((cols, slab, MIX)),
            per_line((cols, slab, C_IN)), whole((1, C_IN)), per_line((cols, slab, MIX)), whole((2, L1)), whole((2, MIX)),
            whole((2, L3)), whole((1, L4)), whole((1, 128)), whole((1, 2 * C_IN)), whole((1, C_FAST)), whole((1, MIX)),
            whole((1, MIX)), m_spec, whole((C_MID, C_IN)), whole((C_FMID, C_FAST)),
        ],
        out_specs=(
            per_line((cols, slab, C_IN)), per_line((cols, slab, C_IN)), per_line((cols, slab, WIDE_FAST)),
            per_line((cols, slab, MIX)), whole((1, 2 * MIX)),
        ),
        out_shape=(
            lines(C_IN, bf16), lines(C_IN, bf16), lines(WIDE_FAST, bf16), lines(MIX, f32), shaped((1, 2 * MIX), f32),
        ),
        scratch_shapes=[pltpu.VMEM((128, WIDE_FAST), bf16)],
        compiler_params=params(32),
        name="expand_back",
    )(gs, gf, a2, zp, base, z2, mom1, mom2, mom3, tot4, inv, sgain, fgain, gain2, shift2, m, slow_c_weight, fast_c_weight)
    tot5, qrow, qcol, qcorner = run_exchange(5, n_clip, part5, weight, False, q2)

    n = high * cols

    def flat(v):
        return v.reshape((n,) + v.shape[2:])

    dwp, dwc, dwfc = pl.pallas_call(
        expand_weights,
        grid=(C_JOIN // C_MID,),
        in_specs=[
            pl.BlockSpec((n, slab, C_MID), lambda i: (0, 0, i)), whole((n, slab, MIX)), whole((n, slab, C_IN)),
            whole((n, slab, C_IN)), whole((n, slab, WIDE_FAST)),
        ],
        out_specs=(
            pl.BlockSpec((C_MID, C_IN), lambda i: (i, 0)), whole((C_MID, C_IN)), whole((C_FMID, C_FAST)),
        ),
        out_shape=(shaped((C_JOIN, C_IN), f32), shaped((C_MID, C_IN), f32), shaped((C_FMID, C_FAST), f32)),
        compiler_params=params(56),
        name="expand_weights",
    )(flat(x), flat(a2), flat(dzp), flat(dzc), flat(dfc))

    q1, part6, dwb, dwfb = pl.pallas_call(
        space_back,
        in_specs=[smem] + [vm] * 20,
        out_specs=(vm, vm, vm, vm),
        out_shape=(
            lines(MIX, f32), shaped((1, 2 * MIX), f32), shaped((3, 3, C_MID, C_MID), f32),
            shaped((9, C_FMID, C_FMID), f32),
        ),
        scratch_shapes=[
            pltpu.VMEM((high + 2, cols + 2, slab, MIX), bf16), pltpu.VMEM((3, 3, C_MID, C_MID), f32),
            pltpu.VMEM((9, 128, 128), f32),
        ],
        compiler_params=params(48),
        name="space_back",
    )(
        place, q2, z2, qrow, qcol, qcorner, zrow, zcol, zcorner, a1, z1, mom1, mom2, tot5, inv, gain1, shift1, gain2, m,
        slow_b_weight, wfb,
    )
    (tot6,) = run_exchange(6, n_clip, part6, weight, False)

    sx, fx, da, dl, df = pl.pallas_call(
        functools.partial(first_back, clips),
        grid=(high,),
        in_specs=[
            per_line((cols, slab, MIX)), per_line((cols, slab, MIX)), whole((2, L1)), whole((1, 2 * MIX)),
            whole((1, 128)), whole((1, MIX)), m_spec, perm_spec, per_line((cols, slab, C_IN)),
            per_line((cols, slab, WIDE_FAST)), whole((5, C_FAST, C_LAT)), whole((3, C_JOIN, C_MID)),
            whole((C_JOIN, C_IN)), whole((3, C_FMID, C_FAST)),
        ],
        out_specs=(
            slow_block, fast_block, per_line((cols, slab, 3 * C_MID)), per_line((cols, slab, 2 * C_LAT)),
            per_line((cols, slab, 3 * 128)),
        ),
        out_shape=(
            shaped(xs.shape, bf16), shaped(xf.shape, bf16), lines(3 * C_MID, bf16), lines(2 * C_LAT, bf16),
            lines(3 * 128, bf16),
        ),
        scratch_shapes=[pltpu.VMEM((128, WIDE_FAST), bf16), pltpu.VMEM((2, 128, C_FAST), bf16)],
        compiler_params=params(40),
        name="first_back",
    )(q1, z1, mom1, tot6, inv, gain1, m, perm, dzp, gf, lateral_weight, slow_a_weight, slow_proj_weight, wfa)

    dwa, dwl, dwfa = pl.pallas_call(
        first_weights,
        grid=(C_JOIN // C_MID,),
        in_specs=[
            pl.BlockSpec((n, slab, C_MID), lambda i: (0, 0, i)), whole((n, slab, WIDE_FAST)),
            whole((n, slab, 3 * C_MID)), whole((n, slab, 2 * C_LAT)), whole((n, slab, 3 * 128)),
        ],
        out_specs=(
            pl.BlockSpec((3, C_MID, C_MID), lambda i: (0, i, 0)), whole((5, C_FAST, C_LAT)), whole((3, C_FMID, C_FAST)),
        ),
        out_shape=(
            shaped((3, C_JOIN, C_MID), f32), shaped((5, C_FAST, C_LAT), f32), shaped((3, C_FMID, C_FAST), f32),
        ),
        compiler_params=params(48),
        name="first_weights",
    )(flat(x), flat(f), flat(da), flat(dl), flat(df))

    axes = ("clip", "ha", "wa")
    dwp, dwc, dwb, dwa, dwl = [
        v.astype(f32) for v in lax.psum(tuple(v.astype(bf16) for v in (dwp, dwc, dwb, dwa, dwl)), axes)
    ]
    dwfc, dwfb, dwfa = lax.psum((dwfc, dwfb, dwfa), axes)

    def joined_sums(k):
        first = [tot6[0, k * MIX : (k + 1) * MIX], tot5[0, k * MIX : (k + 1) * MIX]]
        last = tot4[0, :C_IN] if k == 0 else tot4[0, C_IN : 2 * C_IN]
        proj = tot4[0, :C_IN] if k == 0 else tot4[0, 2 * C_IN : 3 * C_IN]
        at = 3 * C_IN + k * C_FAST
        slow = jnp.concatenate([first[0][:C_MID], first[1][:C_MID], last, proj])
        lo = C_MID + C_FMID
        fast = jnp.concatenate([first[0][C_MID:lo], first[1][C_MID:lo], tot4[0, at : at + C_FAST]])
        return slow, fast

    slow_shift_grad, fast_shift_grad = joined_sums(0)
    slow_gain_grad, fast_gain_grad = joined_sums(1)
    return (
        so.transpose(3, 0, 1, 2, 4),
        fo.transpose(0, 3, 1, 2, 4),
        sx.transpose(3, 0, 1, 2, 4),
        fx.transpose(0, 3, 1, 2, 4),
        dwl,
        dwa,
        dwb,
        dwc,
        dwp,
        dwfa.transpose(0, 2, 1),
        dwfb.reshape(3, 3, C_FMID, C_FMID),
        dwfc,
        slow_gain_grad,
        slow_shift_grad,
        fast_gain_grad,
        fast_shift_grad,
    )


def solution(mesh):
    tiles = P("clip", None, "ha", "wa", None)
    return jax.shard_map(
        on_device,
        mesh=mesh,
        in_specs=(tiles, tiles) + (P(),) * 13 + (tiles, tiles),
        out_specs=(tiles,) * 4 + (P(),) * 12,
        check_vma=False,
    )
```

time: 1280 us -> 592 us (0.46)
  blocking collectives: 365 us -> 0 us
  matrix products: 323 us -> 0 us
  Pallas kernels: 0 us -> 221 us
  other arithmetic: 126 us -> 30.4 us
  starting transfers between devices: 44.2 us -> 0.08 us
  local copies, waits for them, and re-layouts: 81.5 us -> 45.9 us
  waiting for transfers between devices: 313 us -> 278 us
    psum x9 -> x0, blocking collectives: 365 us -> none  [the longest x3 123 us: moments(): spread = lax.psum(centred, ('clip', 'ha', 'wa')) / totals]
    dot_general x96 -> x0, matrix products: 323 us -> none  [the longest x32 125 us: product_back(): lax.dot_general(grads, weight, (((grads.ndim - 1,), (1,)), ((), ())), pre...]
    pallas_call x0 -> x15, Pallas kernels: none -> 221 us  [the longest x6 65.1 us: run_exchange(): pl.pallas_call(functools.partial(exchange, n_clip, moments, edges), out_s...]
    reduce_sum x9 -> x2, other arithmetic: 48.4 us -> 1.41 us  [the longest x1 1.3 us: on_device(): real_total = jnp.sum(frame_counts).astype(f32)]
    ppermute x16 -> x0, starting transfers between devices: 43.7 us -> none  [the longest x8 32.6 us: padded_2(): lax.ppermute(tail, axis, [(i, (i + 1) % count) for i in range(ends)])]
    psum x2, waiting for transfers between devices: 313 us -> 277 us  [the longest x1 158 us: on_device(): lax.psum(tuple((v.astype(bf16) for v in (dwp, dwc, dwb, dwa, dwl))), axes)]
    unnamed x398 -> x141, local copies, waits for them, and re-layouts: 55.3 us -> 31.2 us
    convert_element_type x12 -> x13, other arithmetic: 42.2 us -> 26.3 us  [the longest x5 12.1 us: on_device(): v.astype(bf16)]
  transfers between devices with their start and end apart: 18 -> 2, of which waited for: 2 -> 2; matrix products, arithmetic and copies ran while one was open for 14% -> 2% of each run, Pallas kernels for 0% -> 0%
where the time goes in v1:
time: 592 us; the launch traced here: 590 us
  waiting for transfers between devices  278 us (47%)
  Pallas kernels  221 us (37%)
  local copies, waits for them, and re-layouts  45.9 us (8%)
  other arithmetic  30.4 us (5%)
  between operations  15.6 us (3%)
    psum x1, waiting for transfers between devices, on_device(): lax.psum(tuple((v.astype(bf16) for v in (dwp, dwc, dwb, dwa, dwl))), axes)  158 us
    psum x1, waiting for transfers between devices, on_device(): dwfc, dwfb, dwfa = lax.psum((dwfc, dwfb, dwfa), axes)  119 us
    pallas_call x6, Pallas kernels, run_exchange(): pl.pallas_call(functools.partial(exchange, n_clip, moments, edges), out_s...  65.1 us
    unnamed x141, local copies, waits for them, and re-layouts  31.2 us
    pallas_call x1, Pallas kernels, on_device(): pl.pallas_call(outputs, grid=(high,), in_specs=[per_line((cols, slab, MIX...  24.8 us
    pallas_call x1, Pallas kernels, on_device(): pl.pallas_call(functools.partial(first_back, clips), grid=(high,), in_spe...  23.3 us
    pallas_call x1, Pallas kernels, on_device(): pl.pallas_call(space_back, in_specs=[smem] + [vm] * 20, out_specs=(vm, vm...  22.8 us
    pallas_call x1, Pallas kernels, on_device(): pl.pallas_call(functools.partial(first_convs, clips), grid=(high,), in_sp...  21.8 us
  transfers between devices with their start and end apart: 2, of which 2 were waited for; matrix products, arithmetic and copies ran while one was open for 2% of the time, Pallas kernels for 0%

profile of v1, /device:TPU:0, one launch (start us, length us, event | category | flops | bytes accessed | tf_op | source)
XLA Modules:
  0.0 590.2 jit_solution(6146638008987261922)
XLA Ops:
  18.0 2.6 fusion.4
  21.9 2.4 mul.46
  24.3 2.0 mul.47
  30.3 21.8 %first_convs.1 = (bf16[7,7,48,1280]{3,2,1,0:T(8,128)(2,1)}, bf16[7,7,48,512]{3,2,1,0:T(8,128)(2,1)S(1)}, f32[7,7,48,384]{3,2,1,0:T(8,128)S(1)}, bf16[7,7,48,1024...) custom-call(bf16[12,7,7,4,1024]{4,3,2,1,0:T(4,128)(2,1)} %bitcast.77, ...), custom_call_target="tpu_custom_call" | custom-call | tf_op jit(solution)/shard_map/first_convs/pallas_call | solution.py:748
  52.1 15.1 %exchange1.1 = (f32[2,1408]{1,0:T(2,128)S(1)}, f32[7,48,384]{2,1,0:T(8,128)S(1)}, f32[7,48,384]{2,1,0:T(8,128)S(1)}, f32[48,384]{1,0:T(8,128)S(1)}) custom-call(f32[2,1408]{1,0:T(2,128)S(1)} %get-tuple-element.65.refs_0_, f32[8,1,128]{2,1,0:T(1,128)S(1)} %broadcast_in_dim.46.refs_1_, f32[7,7,48,384]{3,2,1,0:T(8,128)S(1)} %get-tuple-element.64.refs_2_.z1), custom_call_target="tpu_custom_call" | custom-call | tf_op jit(solution)/shard_map/exchange1/pallas_call | solution.py:653
  67.3 10.0 %space_convs.1 = (bf16[9,9,48,384]{3,2,1,0:T(8,128)(2,1)S(1)}, f32[7,7,48,384]{3,2,1,0:T(8,128)S(1)}, f32[2,384]{1,0:T(2,128)S(1)}) custom-call(s32[2]{0:T(128)S(1)} %pad_add_fusion.place, f32[7,7,48,384]{3,2,1,0:T(8,128)S(1)} %get-tuple-element.64.refs_2_.z1, f32[7,48,384]{2,1,0:T(8,128)S(1)} %get-tuple-element.66.row, ...), custom_call_target="tpu_custom_call" | custom-call | tf_op jit(solution)/shard_map/space_convs/pallas_call | solution.py:774
  77.3 10.3 %exchange2.1 = (f32[2,384]{1,0:T(2,128)S(1)}, f32[7,48,384]{2,1,0:T(8,128)S(1)}, f32[7,48,384]{2,1,0:T(8,128)S(1)}, f32[48,384]{1,0:T(8,128)S(1)}) custom-call(f32[2,384]{1,0:T(2,128)S(1)} %get-tuple-element.71.refs_0_, f32[8,1,128]{2,1,0:T(1,128)S(1)} %broadcast_in_dim.46.refs_1_, f32[7,7,48,384]{3,2,1,0:T(8,128)S(1)} %get-tuple-element.70.refs_2_.z2), custom_call_target="tpu_custom_call" | custom-call | tf_op jit(solution)/shard_map/exchange2/pallas_call | solution.py:653
  89.2 7.9 %expand_moments.1 = (bf16[7,7,48,384]{3,2,1,0:T(8,128)(2,1)S(1)}, f32[2,1152]{1,0:T(2,128)S(1)}) custom-call(f32[7,7,48,384]{3,2,1,0:T(8,128)S(1)} %get-tuple-element.70.refs_2_.z2, f32[2,384]{1,0:T(2,128)S(1)} %get-tuple-element.72.mom.mom2, f32[1,384]{1,0:T(1,128)S(1)} %broadcast_in_dim.49.gain.gain2, f32[1,384]{1,0:T(1,128)S(1)} %broadcast_in_dim.50.shift.shift2, ...), custom_call_target="tpu_custom_call" | custom-call | tf_op jit(solution)/shard_map/expand_moments/pallas_call | solution.py:788
  97.2 9.2 %exchange3.1.mom3 = f32[2,1152]{1,0:T(2,128)S(1)} custom-call(f32[2,1152]{1,0:T(2,128)S(1)} %get-tuple-element.76.refs_0_, f32[8,1,128]{2,1,0:T(1,128)S(1)} %broadcast_in_dim.46.refs_1_), custom_call_target="tpu_custom_call" | custom-call | tf_op jit(solution)/shard_map/exchange3/pallas_call | solution.py:653
  106.6 2.4 copy-done.14
  108.9 24.8 %outputs.1 = (bf16[12,7,7,4,1024]{4,3,2,1,0:T(4,128)(2,1)}, bf16[4,7,7,48,128]{4,3,2,1,0:T(8,128)(2,1)}, f32[7,7,48,1024]{3,2,1,0:T(8,128)}, f32[7,7,48,512]{3,2,1,0:T(8,128)S(1)}, f32[1,3328]{1,0:T(1,128)S(1)}) custom-call(bf16[7,7,48,384]{3,2,1,0:T(8,128)(2,1)S(1)} %get-tuple-element.73.a2, bf16[7,7,48,1024]{3,2,1,0:T(8,128)(2,1)S(1)} %bitcast.59, ...), custom_call_target="tpu_custom_call" | custom-call | tf_op jit(solution)/shard_map/outputs/pallas_call | solution.py:804
  133.7 2.2 copy-done.4
  135.9 9.6 %exchange4.1.tot = f32[1,3328]{1,0:T(1,128)S(1)} custom-call(f32[1,3328]{1,0:T(1,128)S(1)} %get-tuple-element.82.refs_0_, f32[8,1,128]{2,1,0:T(1,128)S(1)} %broadcast_in_dim.46.refs_1_), custom_call_target="tpu_custom_call" | custom-call | tf_op jit(solution)/shard_map/exchange4/pallas_call | solution.py:653
  146.2 2.0 copy-done.1
  153.7 15.5 %expand_back.1 = (bf16[7,7,48,1024]{3,2,1,0:T(8,128)(2,1)S(1)}, bf16[7,7,48,1024]{3,2,1,0:T(8,128)(2,1)S(1)}, bf16[7,7,48,512]{3,2,1,0:T(8,128)(2,1)S(1)}, f32[7,7,48,384]{3,2,1,0:T(8,128)S(1)}, f32[1,768]{1,0:T(1,128)S(1)}) custom-call(f32[7,7,48,1024]{3,2,1,0:T(8,128)} %get-tuple-element.80.gs, f32[7,7,48,512]{3,2,1,0:T(8,128)} %copy-done.4, ...), custom_call_target="tpu_custom_call" | custom-call | tf_op jit(solution)/shard_map/expand_back/pallas_call | solution.py:825
  169.2 2.2 copy-done.3
  171.4 2.2 copy-done.13
  175.2 12.3 %exchange5.1 = (f32[1,768]{1,0:T(1,128)S(1)}, f32[7,48,384]{2,1,0:T(8,128)S(1)}, f32[7,48,384]{2,1,0:T(8,128)S(1)}, f32[48,384]{1,0:T(8,128)S(1)}) custom-call(f32[1,768]{1,0:T(1,128)S(1)} %get-tuple-element.84.refs_0_, f32[8,1,128]{2,1,0:T(1,128)S(1)} %broadcast_in_dim.46.refs_1_, f32[7,7,48,384]{3,2,1,0:T(8,128)S(1)} %get-tuple-element.83.refs_2_.q2), custom_call_target="tpu_custom_call" | custom-call | tf_op jit(solution)/shard_map/exchange5/pallas_call | solution.py:653
  187.6 22.8 %space_back.1 = (f32[7,7,48,384]{3,2,1,0:T(8,128)}, f32[1,768]{1,0:T(1,128)S(1)}, f32[3,3,256,256]{3,2,1,0:T(8,128)}, f32[9,32,32]{2,1,0:T(8,128)}) custom-call(s32[2]{0:T(128)S(1)} %copy-done.62, f32[7,7,48,384]{3,2,1,0:T(8,128)} %copy-done.6, f32[7,7,48,384]{3,2,1,0:T(8,128)} %copy-done, f32[7,48,384]{2,1,0:T(8,128)S(1)} %get-tuple-element.85.qrow, ...), custom_call_target="tpu_custom_call" | custom-call | tf_op jit(solution)/shard_map/space_back/pallas_call | solution.py:867
  210.4 8.6 %exchange6.1.tot = f32[1,768]{1,0:T(1,128)S(1)} custom-call(f32[1,768]{1,0:T(1,128)S(1)} %get-tuple-element.94.refs_0_, f32[8,1,128]{2,1,0:T(1,128)S(1)} %broadcast_in_dim.46.refs_1_), custom_call_target="tpu_custom_call" | custom-call | tf_op jit(solution)/shard_map/exchange6/pallas_call | solution.py:653
  219.2 23.3 %first_back.1 = (bf16[12,7,7,4,1024]{4,3,2,1,0:T(4,128)(2,1)}, bf16[4,7,7,48,128]{4,3,2,1,0:T(8,128)(2,1)}, bf16[7,7,48,768]{3,2,1,0:T(8,128)(2,1)S(1)}, bf16[7,...) custom-call(f32[7,7,48,384]{3,2,1,0:T(8,128)} %get-tuple-element.93.q1, f32[7,7,48,384]{3,2,1,0:T(8,128)} %copy-done.2, ...), custom_call_target="tpu_custom_call" | custom-call | tf_op jit(solution)/shard_map/first_back/pallas_call | solution.py:887
  242.5 1.8 copy-done.17
  245.7 12.7 %first_weights.1 = (f32[3,1280,256]{2,1,0:T(8,128)}, f32[5,128,256]{2,1,0:T(8,128)S(1)}, f32[3,32,128]{2,1,0:T(8,128)}) custom-call(bf16[49,48,1280]{2,1,0:T(8,128)(2,1)} %bitcast.75, bf16[49,48,512]{2,1,0:T(8,128)(2,1)S(1)} %bitcast.61, bf16[49,48,768]{2,1,0:T(8,128)(2,1)} %bitcast.64, bf16[49,48,512]{2,1,0:T(8,128)(2,1)} %bitcast.68, ...), custom_call_target="tpu_custom_call" | custom-call | tf_op jit(solution)/shard_map/first_weights/pallas_call | solution.py:909
  259.2 3.7 convert_element_type.64
  264.1 16.6 %expand_weights.1 = (f32[1280,1024]{1,0:T(8,128)}, f32[256,1024]{1,0:T(8,128)}, f32[32,128]{1,0:T(8,128)}) custom-call(bf16[49,48,1280]{2,1,0:T(8,128)(2,1)} %bitcast.76, bf16[49,48,384]{2,1,0:T(8,128)(2,1)} %bitcast.60, bf16[49,48,1024]{2,1,0:T(8,128)(2,1)} %bitcast.57, bf16[49,48,1024]{2,1,0:T(8,128)(2,1)} %bitcast.62, bf16[49,48,512]{2,1,0:T(8,128)(2,1)} %bitcast.65), custom_call_target="tpu_custom_call" | custom-call | tf_op jit(solution)/shard_map/expand_weights/pallas_call | solution.py:852
  280.7 2.1 convert_element_type.68
  282.8 4.4 convert_element_type.70
  290.5 158.0 %all-reduce.7.cloned.1.call-done = (bf16[5,128,256]{2,1,0:T(8,128)(2,1)}, bf16[3,1280,256]{2,1,0:T(8,128)(2,1)}, bf16[3,3,256,256]{3,2,1,0:T(8,128)(2,1)}, bf16[256,1024]{1,0:T(8,128)(2,1)}, bf16[1280,1024]{1,0:T(8,128)(2,1)}) async-done(((bf16[5,128,256]{2,1,0:T(8,128)(2,1)}, bf16[3,1280,256]{2,1,0:T(8,128)(2,1)}, bf16[3,3,256,256]{3,2,1,0:T(8,128)(2,1)}, bf16[256,1024]{1,0:T(8,128)(2,1)}, ...) | async-done | bytes 6619152 | tf_op jit(solution)/shard_map/psum | solution.py:928
  448.5 1.9 convert_element_type.63
  450.4 3.9 convert_element_type.65
  457.1 3.0 convert_element_type.71
  460.1 118.9 %all-reduce.5.cloned.1.call-done = (f32[3,128,32]{1,2,0:T(8,128)}, f32[3,3,32,32]{3,2,1,0:T(8,128)}, f32[32,128]{1,0:T(8,128)}) async-done(((f32[3,128,32]{1,2,0:T(8,128)}, f32[3,3,32,32]{3,2,1,0:T(8,128)}, f32[32,128]{1,0:T(8,128)}), (f32[3,128,32]{1,2,0:T(8,128)}, f32[3,3,32,32]{3,2,1,0:T(8,128)}, f32[32,128]{1,0:T(8,128)})) %all-reduce.5.cloned.1.call-update) | async-done | bytes 102416 | tf_op jit(solution)/shard_map/psum | solution.py:930
  (199 shorter events, 38.2 us)
Async XLA Ops:
  7.2 19.8 %copy-start.27 = (bf16[5,128,256]{2,1,0:T(8,128)(2,1)S(1)}, bf16[5,128,256]{2,1,0:T(8,128)(2,1)}, u32[]{:S(2)}) copy-start(bf16[5,128,256]{2,1,0:T(8,128)(2,1)} %wl.3) | copy-start | bytes 983044
  7.2 19.8 %copy-start.7 = (bf16[1280,1024]{1,0:T(8,128)(2,1)S(1)}, bf16[1280,1024]{1,0:T(8,128)(2,1)}, u32[]{:S(2)}) copy-start(bf16[1280,1024]{1,0:T(8,128)(2,1)} %wp.3) | copy-start | bytes 7864324
  7.2 19.8 %copy-start.36 = (bf16[3,128,32]{1,2,0:T(8,128)(2,1)S(1)}, bf16[3,128,32]{1,2,0:T(8,128)(2,1)}, u32[]{:S(2)}) copy-start(bf16[3,128,32]{1,2,0:T(8,128)(2,1)} %param.25) | copy-start | bytes 73732
  7.2 441.3 %all-reduce.7.cloned.1.call-start = ((), (), s32[]{:S(2)}) async-start(), calls=%async_computation.1 | async-start | bytes 13238272 | tf_op jit(solution)/shard_map/psum | solution.py:928
  21.7 45.5 %copy-start.50 = (f32[1,384]{1,0:T(1,128)}, f32[1,384]{1,0:T(1,128)S(1)}, u32[]{:S(2)}) copy-start(f32[1,384]{1,0:T(1,128)S(1)} %broadcast_in_dim.47.gain.gain1) | copy-start | bytes 4612
  21.9 45.3 %copy-start.56 = (f32[1,384]{1,0:T(1,128)}, f32[1,384]{1,0:T(1,128)S(1)}, u32[]{:S(2)}) copy-start(f32[1,384]{1,0:T(1,128)S(1)} %broadcast_in_dim.48.shift.shift1) | copy-start | bytes 4612
  26.6 62.6 %copy-start.47 = (f32[1,384]{1,0:T(1,128)}, f32[1,384]{1,0:T(1,128)S(1)}, u32[]{:S(2)}) copy-start(f32[1,384]{1,0:T(1,128)S(1)} %broadcast_in_dim.49.gain.gain2) | copy-start | bytes 4612
  26.6 62.6 %copy-start.54 = (f32[1,384]{1,0:T(1,128)}, f32[1,384]{1,0:T(1,128)S(1)}, u32[]{:S(2)}) copy-start(f32[1,384]{1,0:T(1,128)S(1)} %broadcast_in_dim.50.shift.shift2) | copy-start | bytes 4612
  26.7 40.5 %copy-start.61 = (s32[2]{0:T(128)}, s32[2]{0:T(128)S(1)}, u32[]{:S(2)}) copy-start(s32[2]{0:T(128)S(1)} %pad_add_fusion.place) | copy-start | bytes 28
  26.8 40.5 %copy-start.19 = (bf16[9,128,128]{2,1,0:T(8,128)(2,1)}, bf16[9,128,128]{2,1,0:T(8,128)(2,1)S(1)}, u32[]{:S(2)}) copy-start(bf16[9,128,128]{2,1,0:T(8,128)(2,1)S(1)} %broadcast_multiply_fusion.wfb) | copy-start | bytes 884740
  26.9 79.5 %copy-start.25 = (bf16[192,192]{1,0:T(8,128)(2,1)}, bf16[192,192]{1,0:T(8,128)(2,1)S(1)}, u32[]{:S(2)}) copy-start(bf16[192,192]{1,0:T(8,128)(2,1)S(1)} %and_convert_fusion.perm) | copy-start | bytes 221188
  52.0 25.2 %copy-start.2 = (f32[7,7,48,384]{3,2,1,0:T(8,128)}, f32[7,7,48,384]{3,2,1,0:T(8,128)S(1)}, u32[]{:S(2)}) copy-start(f32[7,7,48,384]{3,2,1,0:T(8,128)S(1)} %get-tuple-element.64.refs_2_.z1) | copy-start | bytes 10838020
  52.0 54.4 %copy-start.9 = (bf16[7,7,48,512]{3,2,1,0:T(8,128)(2,1)}, bf16[7,7,48,512]{3,2,1,0:T(8,128)(2,1)S(1)}, u32[]{:S(2)}) copy-start(bf16[7,7,48,512]{3,2,1,0:T(8,128)(2,1)S(1)} %get-tuple-element.77.fast_in) | copy-start | bytes 7225348
  52.0 54.4 %copy-start.52 = (f32[1,1024]{1,0:T(1,128)}, f32[1,1024]{1,0:T(1,128)S(1)}, u32[]{:S(2)}) copy-start(f32[1,1024]{1,0:T(1,128)S(1)} %get-tuple-element.75.base) | copy-start | bytes 12292
  67.3 39.2 %slice-start = ((s8[4816896]{0:T(1024)(128)(4,1)}), s8[622592]{0:T(1024)(128)(4,1)S(1)}, s32[]{:S(2)}) async-start(s8[4816896]{0:T(1024)(128)(4,1)} %bitcast.58), calls=%async_computation.2 | async-start | bytes 1245184
  77.3 19.9 %copy-start = (f32[7,7,48,384]{3,2,1,0:T(8,128)}, f32[7,7,48,384]{3,2,1,0:T(8,128)S(1)}, u32[]{:S(2)}) copy-start(f32[7,7,48,384]{3,2,1,0:T(8,128)S(1)} %get-tuple-element.70.refs_2_.z2) | copy-start | bytes 10838020
  77.3 19.9 %copy-start.18 = (bf16[9,9,48,384]{3,2,1,0:T(8,128)(2,1)}, bf16[9,9,48,384]{3,2,1,0:T(8,128)(2,1)S(1)}, u32[]{:S(2)}) copy-start(bf16[9,9,48,384]{3,2,1,0:T(8,128)(2,1)S(1)} %get-tuple-element.91.a1) | copy-start | bytes 8957956
  77.3 29.2 %slice-start.1 = ((s8[4816896]{0:T(1024)(128)(4,1)}), s8[4194304]{0:T(1024)(128)(4,1)S(1)}, s32[]{:S(2)}) async-start(s8[4816896]{0:T(1024)(128)(4,1)} %bitcast.58), calls=%async_computation.3 | async-start | bytes 8388608
  89.2 44.5 %copy-start.40 = (f32[48,384]{1,0:T(8,128)}, f32[48,384]{1,0:T(8,128)S(1)}, u32[]{:S(2)}) copy-start(f32[48,384]{1,0:T(8,128)S(1)} %get-tuple-element.90.zcorner) | copy-start | bytes 221188
  89.2 17.3 %copy-start.44 = (f32[2048]{0:T(1024)S(1)}, f32[2048]{0:T(1024)}, u32[]{:S(2)}) copy-start(f32[2048]{0:T(1024)} %slice.120) | copy-start | bytes 24580
  89.2 17.3 %copy-start.46 = (f32[2048]{0:T(1024)S(1)}, f32[2048]{0:T(1024)}, u32[]{:S(2)}) copy-start(f32[2048]{0:T(1024)} %slice.121) | copy-start | bytes 24580
  89.2 17.3 %copy-start.58 = (f32[1,128]{1,0:T(1,128)S(1)}, f32[1,128]{1,0:T(1,128)}, u32[]{:S(2)}) copy-start(f32[1,128]{1,0:T(1,128)} %get-tuple-element.154.fgain) | copy-start | bytes 1540
  89.2 17.3 %copy-start.60 = (f32[1,128]{1,0:T(1,128)S(1)}, f32[1,128]{1,0:T(1,128)}, u32[]{:S(2)}) copy-start(f32[1,128]{1,0:T(1,128)} %get-tuple-element.153.fshift) | copy-start | bytes 1540
  97.2 49.0 %copy-start.5 = (bf16[7,7,48,384]{3,2,1,0:T(8,128)(2,1)}, bf16[7,7,48,384]{3,2,1,0:T(8,128)(2,1)S(1)}, u32[]{:S(2)}) copy-start(bf16[7,7,48,384]{3,2,1,0:T(8,128)(2,1)S(1)} %get-tuple-element.73.a2) | copy-start | bytes 5419012
  106.4 27.3 %copy-start.38 = (f32[2,1152]{1,0:T(2,128)}, f32[2,1152]{1,0:T(2,128)S(1)}, u32[]{:S(2)}) copy-start(f32[2,1152]{1,0:T(2,128)S(1)} %exchange3.1.mom3) | copy-start | bytes 27652
  187.6 31.5 %copy-start.8 = (bf16[1280,1024]{1,0:T(8,128)(2,1)S(1)}, bf16[1280,1024]{1,0:T(8,128)(2,1)}, u32[]{:S(2)}) copy-start(bf16[1280,1024]{1,0:T(8,128)(2,1)} %wp.3) | copy-start | bytes 7864324
  187.6 31.5 %copy-start.12 = (bf16[3,1280,256]{2,1,0:T(8,128)(2,1)S(1)}, bf16[3,1280,256]{2,1,0:T(8,128)(2,1)}, u32[]{:S(2)}) copy-start(bf16[3,1280,256]{2,1,0:T(8,128)(2,1)} %wa.3) | copy-start | bytes 5898244
  187.6 31.5 %copy-start.26 = (bf16[192,192]{1,0:T(8,128)(2,1)S(1)}, bf16[192,192]{1,0:T(8,128)(2,1)}, u32[]{:S(2)}) copy-start(bf16[192,192]{1,0:T(8,128)(2,1)} %copy-done.25) | copy-start | bytes 221188
  187.6 31.5 %copy-start.28 = (bf16[5,128,256]{2,1,0:T(8,128)(2,1)S(1)}, bf16[5,128,256]{2,1,0:T(8,128)(2,1)}, u32[]{:S(2)}) copy-start(bf16[5,128,256]{2,1,0:T(8,128)(2,1)} %wl.3) | copy-start | bytes 983044
  187.6 31.5 %copy-start.37 = (bf16[3,128,32]{1,2,0:T(8,128)(2,1)S(1)}, bf16[3,128,32]{1,2,0:T(8,128)(2,1)}, u32[]{:S(2)}) copy-start(bf16[3,128,32]{1,2,0:T(8,128)(2,1)} %param.25) | copy-start | bytes 73732
  219.1 26.6 %copy-start.10 = (bf16[7,7,48,512]{3,2,1,0:T(8,128)(2,1)S(1)}, bf16[7,7,48,512]{3,2,1,0:T(8,128)(2,1)}, u32[]{:S(2)}) copy-start(bf16[7,7,48,512]{3,2,1,0:T(8,128)(2,1)} %copy-done.9) | copy-start | bytes 7225348
  287.2 291.9 %all-reduce.5.cloned.1.call-start = ((), (), s32[]{:S(2)}) async-start(), calls=%async_computation | async-start | bytes 425984 | tf_op jit(solution)/shard_map/psum | solution.py:930
  (39 other events, 207.4 us)
Sparse Core Ops, SparseCore 0:
  287.3 161.1 all-reduce.6
  455.0 123.9 all-reduce.4

commit v2 on v1

--- a/solution.py
+++ b/solution.py
@@ -372,12 +372,12 @@
     i = pl.program_id(0)
     n, slab, _ = x.shape
     rows = n * slab
-    wp_out[...] = dot_tn(x[...].reshape(rows, C_MID), dzp[...].reshape(rows, C_IN))
+    wp_out[...] = dot_tn(x[...].reshape(rows, C_MID), dzp[...].reshape(rows, C_IN)).astype(bf16)
 
     @pl.when(i == pl.num_programs(0) - 1)
     def _():
         a = a2[...].reshape(rows, MIX)
-        wc_out[...] = dot_tn(a[:, :C_MID], dzc[...].reshape(rows, C_IN))
+        wc_out[...] = dot_tn(a[:, :C_MID], dzc[...].reshape(rows, C_IN)).astype(bf16)
         wide = dot_tn(a[:, C_MID:], dfc[...].reshape(rows, WIDE_FAST))
         wfc_out[...] = sum(
             wide[p * C_FMID : (p + 1) * C_FMID, p * C_FAST : (p + 1) * C_FAST] for p in range(ALPHA)
@@ -437,7 +437,7 @@
         return carry
 
     lax.fori_loop(0, high, line, 0)
-    wb_out[...] = keep[...]
+    wb_out[...] = keep[...].astype(bf16)
     for k in range(9):
         wfb_out[k] = sum(
             keep_f[k, p * C_FMID : (p + 1) * C_FMID, p * C_FMID : (p + 1) * C_FMID] for p in range(ALPHA)
@@ -489,19 +489,19 @@
         fx[:, w] = dot_tn(perm[...], stacked).astype(bf16).reshape(clips, slab, C_FAST)
 
 
-def first_weights(x, f, da, dl, df, wa_out, wl_out, wfa_out):
+def first_weights(x, f, da, dl, df, dwfc, dwfb, wa_out, wl_out, small_out):
     i = pl.program_id(0)
     n, slab, _ = x.shape
     rows = n * slab
     for k in range(3):
-        wa_out[k] = dot_tn(x[...].reshape(rows, C_MID), da[:, :, k * C_MID : (k + 1) * C_MID].reshape(rows, C_MID))
+        wa_out[k] = dot_tn(x[...].reshape(rows, C_MID), da[:, :, k * C_MID : (k + 1) * C_MID].reshape(rows, C_MID)).astype(bf16)
 
     @pl.when(i == pl.num_programs(0) - 1)
     def _():
         fast = f[...].reshape(rows, WIDE_FAST)
         d = dl[...].reshape(rows, 2 * C_LAT)
-        wl_out[2:5] = dot_tn(fast[:, : 3 * C_FAST], d[:, :C_LAT]).reshape(3, C_FAST, C_LAT)
-        wl_out[0:2] = dot_tn(fast[:, 2 * C_FAST :], d[:, C_LAT:]).reshape(2, C_FAST, C_LAT)
+        wl_out[2:5] = dot_tn(fast[:, : 3 * C_FAST], d[:, :C_LAT]).reshape(3, C_FAST, C_LAT).astype(bf16)
+        wl_out[0:2] = dot_tn(fast[:, 2 * C_FAST :], d[:, C_LAT:]).reshape(2, C_FAST, C_LAT).astype(bf16)
         g = df[...].reshape(rows, 3 * 128)
         mid = dot_tn(g[:, 128:256], fast)
         sums = [jnp.zeros((C_FMID, C_FAST), f32) for _ in range(3)]
@@ -510,8 +510,13 @@
                 sums[s - p + 1] += mid[p * C_FMID : (p + 1) * C_FMID, s * C_FAST : (s + 1) * C_FAST]
         sums[0] += dot_tn(g[:, :128], fast[:, 3 * C_FAST :])[:C_FMID]
         sums[2] += dot_tn(g[:, 256:], fast[:, :C_FAST])[3 * C_FMID :]
+        small_out[...] = jnp.zeros_like(small_out)
         for k in range(3):
-            wfa_out[k] = sums[k]
+            small_out[k * C_FMID : (k + 1) * C_FMID] = sums[k].astype(bf16)
+        small_out[3 * C_FMID : 4 * C_FMID] = dwfc[...].astype(bf16)
+        for k in range(9):
+            at = (4 + k) * C_FMID
+            small_out[at : at + C_FMID, :C_FMID] = dwfb[k].astype(bf16)
 
 
 def exchange(n_clip, moments, edges, *refs):
@@ -613,8 +618,240 @@
         copy.wait_send()
 
 
+UNIT = 512
+
+
+def bit_of(axis, power):
+    return lax.rem(lax.axis_index(axis) // (1 << power), 2)
+
+
+def partner_of(axis, power, bit):
+    where = {name: lax.axis_index(name) for name in ("clip", "ha", "wa")}
+    where[axis] = where[axis] + (1 - 2 * bit) * (1 << power)
+    return (where["clip"], where["ha"], where["wa"])
+
+
+def stage_orders(n_clip, sets):
+    rest = [("wa", 0)] + [("clip", b) for b in range(n_clip.bit_length() - 1)]
+    turn, last = rest[:3], rest[3:]
+    return [[("ha", 0)] + turn[s % len(turn) :] + turn[: s % len(turn)] + last for s in range(sets)]
+
+
+def chunk_of(rows):
+    best = 16
+    for k in range(16, min(rows, 256) + 1, 16):
+        if rows % k == 0:
+            best = k
+    return best
+
+
+def land_plan(n_clip, sizes):
+    stages = len(stage_orders(n_clip, 1)[0])
+    starts, total = [], 0
+    for size in sizes:
+        starts.append(total)
+        for _ in range(stages):
+            size = size // 2 if size % 32 == 0 else size
+            total += size
+    return starts, total
+
+
+def reduce_sets(n_clip, starts, sizes, mine, land, done, rs_send, rs_recv, ag_send, ag_recv):
+    orders = stage_orders(n_clip, len(starts))
+    stages = len(orders[0])
+    low = [jnp.int32(v) for v in starts]
+    size = list(sizes)
+    at = land_plan(n_clip, sizes)[0]
+    trail = [[] for _ in starts]
+    sent = []
+
+    def rows(ref, begin, count):
+        return ref.at[pl.ds(pl.multiple_of(begin, 16), count)]
+
+    def send(s, k):
+        axis, power = orders[s][k]
+        bit = bit_of(axis, power)
+        halve = size[s] % 32 == 0
+        count = size[s] // 2 if halve else size[s]
+        begin = low[s] + (1 - bit) * count if halve else low[s]
+        copy = pltpu.make_async_remote_copy(
+            src_ref=rows(mine, begin, count), dst_ref=rows(land, at[s], count),
+            send_sem=rs_send.at[s, k], recv_sem=rs_recv.at[s, k],
+            device_id=partner_of(axis, power, bit), device_id_type=MESH,
+        )
+        copy.start()
+        trail[s].append((copy, low[s], count, halve, axis, power, bit, at[s]))
+        if halve:
+            low[s] = low[s] + bit * count
+            size[s] = count
+        at[s] += count
+
+    def gather(s, k):
+        copy, _, count, halve, axis, power, bit, begin = trail[s][k]
+        copy.wait_recv()
+        if not halve:
+            copy.wait_send()
+        step = chunk_of(count)
+
+        def add(i, carry):
+            own = pl.ds(pl.multiple_of(low[s] + i * step, 16), step)
+            came = pl.ds(pl.multiple_of(begin + i * step, 16), step)
+            mine[own, :] = (mine[own, :].astype(f32) + land[came, :].astype(f32)).astype(bf16)
+            return carry
+
+        lax.fori_loop(0, count // step, add, 0)
+        if halve:
+            sent.append(copy)
+
+    for s in range(len(starts)):
+        send(s, 0)
+    for k in range(stages):
+        for s in range(len(starts)):
+            gather(s, k)
+            if k + 1 < stages:
+                send(s, k + 1)
+    for copy in sent:
+        copy.wait_send()
+
+    for s in range(len(starts)):
+        step = chunk_of(size[s])
+
+        def keep(i, carry):
+            own = pl.ds(pl.multiple_of(low[s] + i * step, 16), step)
+            done[own, :] = mine[own, :]
+            return carry
+
+        lax.fori_loop(0, size[s] // step, keep, 0)
+
+    copies = []
+    pending = [None] * len(starts)
+
+    def spread_out(s, k):
+        _, before, count, halve, axis, power, bit, _ = trail[s][k]
+        if not halve:
+            return
+        copy = pltpu.make_async_remote_copy(
+            src_ref=rows(done, low[s], count), dst_ref=rows(done, low[s], count),
+            send_sem=ag_send.at[s, k], recv_sem=ag_recv.at[s, k],
+            device_id=partner_of(axis, power, bit), device_id_type=MESH,
+        )
+        copy.start()
+        other = before + (1 - bit) * count
+        pending[s] = pltpu.make_async_remote_copy(
+            src_ref=rows(done, other, count), dst_ref=rows(done, other, count),
+            send_sem=ag_send.at[s, k], recv_sem=ag_recv.at[s, k],
+            device_id=partner_of(axis, power, bit), device_id_type=MESH,
+        )
+        low[s] = before
+        copies.append(copy)
+
+    for s in range(len(starts)):
+        spread_out(s, stages - 1)
+    for k in range(stages - 1, -1, -1):
+        for s in range(len(starts)):
+            if pending[s] is not None:
+                pending[s].wait_recv()
+                pending[s] = None
+            if k > 0:
+                spread_out(s, k - 1)
+    for copy in copies:
+        copy.wait_send()
+
+
+def greet(n_clip):
+    barrier = pltpu.get_barrier_semaphore()
+    stages = stage_orders(n_clip, 1)[0]
+    for axis, power in stages:
+        bit = bit_of(axis, power)
+        pl.semaphore_signal(barrier, inc=1, device_id=partner_of(axis, power, bit), device_id_type=MESH)
+    pl.semaphore_wait(barrier, len(stages))
+
+
+def weight_pieces(dws_rows):
+    pieces = []
+    row = 0
+    for which, count in ((0, C_JOIN), (1, C_MID)):
+        for b in range(C_IN // 256):
+            pieces.append((row, count, which, (slice(None), slice(b * 256, (b + 1) * 256))))
+            row += count
+    for i in range(3):
+        for j in range(3):
+            pieces.append((row, C_MID, 2, (i, j)))
+            row += C_MID
+    for k in range(3):
+        pieces.append((row, C_JOIN, 3, (k,)))
+        row += C_JOIN
+    for k in range(5):
+        pieces.append((row, C_FAST, 4, (k,)))
+        row += C_FAST
+    return pieces, row
+
+
+def reduce_weights(n_clip, starts, sizes, dwp, dwc, dwb, dwa, dwl, dws, done,
+                   mine, land, rs_send, rs_recv, ag_send, ag_recv):
+    sources = (dwp, dwc, dwb, dwa, dwl)
+    pieces, row = weight_pieces(dws.shape[0])
+    for begin, count, which, at in pieces:
+        mine[begin : begin + count, :] = sources[which].at[at][...]
+    half = dws.shape[0] // 2
+    mine[row : row + half, :128] = dws[:half]
+    mine[row : row + half, 128:] = dws[half:]
+    end = row + half
+    if end < mine.shape[0]:
+        mine[end:, :] = jnp.zeros((mine.shape[0] - end, 256), bf16)
+    greet(n_clip)
+    reduce_sets(n_clip, starts, sizes, mine, land, done, rs_send, rs_recv, ag_send, ag_recv)
+
+
+def unpack_weights(done, wp_out, wc_out, wb_out, wa_out, wl_out, ws_out):
+    targets = (wp_out, wc_out, wb_out, wa_out, wl_out)
+    pieces, row = weight_pieces(ws_out.shape[0])
+    for begin, count, which, at in pieces:
+        targets[which].at[at][...] = done[begin : begin + count, :].astype(f32)
+    half = ws_out.shape[0] // 2
+    ws_out[:half] = done[row : row + half, :128].astype(f32)
+    ws_out[half:] = done[row : row + half, 128:].astype(f32)
+
+
 def vmem_spec():
     return pl.BlockSpec(memory_space=pltpu.VMEM)
+
+
+def shaped(shape, kind):
+    return jax.ShapeDtypeStruct(shape, kind)
+
+
+def run_reduce(ident, n_clip, arrays):
+    total = sum(v.size for v in arrays) // 256
+    units = -(-total // UNIT)
+    share = [-(-units // 3), -(-(units - units // 3) // 2), units // 3]
+    share[1] = units - share[0] - share[2]
+    sizes = [v * UNIT for v in share]
+    starts = [0, sizes[0], sizes[0] + sizes[1]]
+    rows = units * UNIT
+    land_rows = land_plan(n_clip, sizes)[1]
+    stages = len(stage_orders(n_clip, 1)[0])
+    sems = [pltpu.SemaphoreType.DMA((3, stages))] * 4
+    vm = vmem_spec()
+    done = pl.pallas_call(
+        functools.partial(reduce_weights, n_clip, starts, sizes),
+        in_specs=[vm] * len(arrays),
+        out_specs=vm,
+        out_shape=shaped((rows, 256), bf16),
+        scratch_shapes=[pltpu.VMEM((v, 256), bf16) for v in (rows, land_rows)] + sems,
+        compiler_params=pltpu.CompilerParams(
+            collective_id=ident, has_side_effects=True, vmem_limit_bytes=60 * MIB
+        ),
+        name=f"reduce{ident}",
+    )(*arrays)
+    return pl.pallas_call(
+        unpack_weights,
+        in_specs=[vm],
+        out_specs=(vm,) * len(arrays),
+        out_shape=tuple(shaped(v.shape, f32) for v in arrays),
+        compiler_params=params(60),
+        name="unpack_weights",
+    )(done)
 
 
 def run_exchange(ident, n_clip, part, weight, moments, source=None):
@@ -657,7 +894,7 @@
         out_specs=tuple(vmem_spec() for _ in out_shape),
         scratch_shapes=scratch,
         compiler_params=pltpu.CompilerParams(
-            collective_id=ident, has_side_effects=True, vmem_limit_bytes=16 * MIB
+            collective_id=ident, has_side_effects=True, vmem_limit_bytes=60 * MIB
         ),
         name=f"exchange{ident}",
     )(*ins)
@@ -672,11 +909,7 @@
 
 
 def params(limit):
-    return pltpu.CompilerParams(vmem_limit_bytes=limit * MIB)
-
-
-def shaped(shape, kind):
-    return jax.ShapeDtypeStruct(shape, kind)
+    return pltpu.CompilerParams(vmem_limit_bytes=60 * MIB)
 
 
 def on_device(
@@ -859,7 +1092,7 @@
         out_specs=(
             pl.BlockSpec((C_MID, C_IN), lambda i: (i, 0)), whole((C_MID, C_IN)), whole((C_FMID, C_FAST)),
         ),
-        out_shape=(shaped((C_JOIN, C_IN), f32), shaped((C_MID, C_IN), f32), shaped((C_FMID, C_FAST), f32)),
+        out_shape=(shaped((C_JOIN, C_IN), bf16), shaped((C_MID, C_IN), bf16), shaped((C_FMID, C_FAST), f32)),
         compiler_params=params(56),
         name="expand_weights",
     )(flat(x), flat(a2), flat(dzp), flat(dzc), flat(dfc))
@@ -869,7 +1102,7 @@
         in_specs=[smem] + [vm] * 20,
         out_specs=(vm, vm, vm, vm),
         out_shape=(
-            lines(MIX, f32), shaped((1, 2 * MIX), f32), shaped((3, 3, C_MID, C_MID), f32),
+            lines(MIX, f32), shaped((1, 2 * MIX), f32), shaped((3, 3, C_MID, C_MID), bf16),
             shaped((9, C_FMID, C_FMID), f32),
         ),
         scratch_shapes=[
@@ -906,28 +1139,28 @@
         name="first_back",
     )(q1, z1, mom1, tot6, inv, gain1, m, perm, dzp, gf, lateral_weight, slow_a_weight, slow_proj_weight, wfa)
 
-    dwa, dwl, dwfa = pl.pallas_call(
+    dwa, dwl, dws = pl.pallas_call(
         first_weights,
         grid=(C_JOIN // C_MID,),
         in_specs=[
             pl.BlockSpec((n, slab, C_MID), lambda i: (0, 0, i)), whole((n, slab, WIDE_FAST)),
             whole((n, slab, 3 * C_MID)), whole((n, slab, 2 * C_LAT)), whole((n, slab, 3 * 128)),
+            whole((C_FMID, C_FAST)), whole((9, C_FMID, C_FMID)),
         ],
         out_specs=(
-            pl.BlockSpec((3, C_MID, C_MID), lambda i: (0, i, 0)), whole((5, C_FAST, C_LAT)), whole((3, C_FMID, C_FAST)),
+            pl.BlockSpec((3, C_MID, C_MID), lambda i: (0, i, 0)), whole((5, C_FAST, C_LAT)), whole((512, C_FAST)),
         ),
         out_shape=(
-            shaped((3, C_JOIN, C_MID), f32), shaped((5, C_FAST, C_LAT), f32), shaped((3, C_FMID, C_FAST), f32),
+            shaped((3, C_JOIN, C_MID), bf16), shaped((5, C_FAST, C_LAT), bf16), shaped((512, C_FAST), bf16),
         ),
         compiler_params=params(48),
         name="first_weights",
-    )(flat(x), flat(f), flat(da), flat(dl), flat(df))
-
-    axes = ("clip", "ha", "wa")
-    dwp, dwc, dwb, dwa, dwl = [
-        v.astype(f32) for v in lax.psum(tuple(v.astype(bf16) for v in (dwp, dwc, dwb, dwa, dwl)), axes)
-    ]
-    dwfc, dwfb, dwfa = lax.psum((dwfc, dwfb, dwfa), axes)
+    )(flat(x), flat(f), flat(da), flat(dl), flat(df), dwfc, dwfb)
+
+    dwp, dwc, dwb, dwa, dwl, dws = run_reduce(7, n_clip, (dwp, dwc, dwb, dwa, dwl, dws))
+    dwfa = dws[: 3 * C_FMID].reshape(3, C_FMID, C_FAST)
+    dwfc = dws[3 * C_FMID : 4 * C_FMID]
+    dwfb = dws[4 * C_FMID : 13 * C_FMID, :C_FMID]
 
     def joined_sums(k):
         first = [tot6[0, k * MIX : (k + 1) * MIX], tot5[0, k * MIX : (k + 1) * MIX]]

time: 592 us -> 365 us (0.62)
  waiting for transfers between devices: 278 us -> 0 us
  Pallas kernels: 221 us -> 341 us
  local copies, waits for them, and re-layouts: 45.9 us -> 13.9 us
  other arithmetic: 30.4 us -> 8.08 us
  between operations: 15.6 us -> 1.62 us
    psum x2 -> x0, waiting for transfers between devices: 277 us -> none  [the longest x1 158 us: on_device(): lax.psum(tuple((v.astype(bf16) for v in (dwp, dwc, dwb, dwa, dwl))), axes)]
    pallas_call x0 -> x2, Pallas kernels: none -> 95.9 us  [the longest x1 88.1 us: run_reduce(): pl.pallas_call(functools.partial(reduce_weights, n_clip, starts, sizes),...]
    unnamed x141 -> x18, local copies, waits for them, and re-layouts: 31.2 us -> 0.05 us
    convert_element_type x10 -> x0, other arithmetic: 23.6 us -> none  [the longest x5 12.1 us: on_device(): v.astype(bf16)]
    pallas_call x6, Pallas kernels: 65.1 us -> 72.8 us  [run_exchange(): pl.pallas_call(functools.partial(exchange, n_clip, moments, edges), out_s...]
  transfers between devices with their start and end apart: 2 -> 0, of which waited for: 2 -> 0; matrix products, arithmetic and copies ran while one was open for 2% -> 0% of each run, Pallas kernels for 0% -> 0%
where the time goes in v2:
time: 365 us; the launch traced here: 364 us
  Pallas kernels  341 us (93%)
  local copies, waits for them, and re-layouts  13.9 us (4%)
  other arithmetic  8.08 us (2%)
    pallas_call x1, Pallas kernels, run_reduce(): pl.pallas_call(functools.partial(reduce_weights, n_clip, starts, sizes),...  88.1 us
    pallas_call x6, Pallas kernels, run_exchange(): pl.pallas_call(functools.partial(exchange, n_clip, moments, edges), out_s...  72.8 us
    pallas_call x1, Pallas kernels, on_device(): pl.pallas_call(outputs, grid=(high,), in_specs=[per_line((cols, slab, MIX...  25.8 us
    pallas_call x1, Pallas kernels, on_device(): pl.pallas_call(functools.partial(first_back, clips), grid=(high,), in_spe...  25.4 us
    pallas_call x1, Pallas kernels, on_device(): pl.pallas_call(functools.partial(first_convs, clips), grid=(high,), in_sp...  23.8 us
    pallas_call x1, Pallas kernels, on_device(): pl.pallas_call(space_back, in_specs=[smem] + [vm] * 20, out_specs=(vm, vm...  23.3 us
    pallas_call x1, Pallas kernels, on_device(): pl.pallas_call(expand_back, grid=(high,), in_specs=[per_line((cols, slab,...  19.2 us
    pallas_call x1, Pallas kernels, on_device(): pl.pallas_call(expand_weights, grid=(C_JOIN // C_MID,), in_specs=[pl.Bloc...  16.2 us

profile of v2, /device:TPU:0, one launch (start us, length us, event | category | flops | bytes accessed | tf_op | source)
XLA Modules:
  0.0 364.4 jit_solution(13750136466274364335)
XLA Ops:
  0.7 0.7 pad_add_fusion.place
  1.3 0.7 dynamic_slice.3
  2.6 2.6 fusion.4
  5.2 0.7 broadcast_in_dim.22.m
  6.2 0.8 and_convert_fusion.perm
  7.0 23.8 %first_convs.1 = (bf16[7,7,48,1280]{3,2,1,0:T(8,128)(2,1)}, bf16[7,7,48,512]{3,2,1,0:T(8,128)(2,1)}, f32[7,7,48,384]{3,2,1,0:T(8,128)}, bf16[7,7,48,1024]{3,2,1,...) custom-call(bf16[12,7,7,4,1024]{4,3,2,1,0:T(4,128)(2,1)} %bitcast.65, bf16[4,7,7,48,128]{4,3,2,1,0:T(8,128)(2,1)} %bitcast.69, ...), custom_call_target="tpu_custom_call" | custom-call | tf_op jit(solution)/shard_map/first_convs/pallas_call | solution.py:981
  31.0 0.6 reduce_sum.19
  32.3 0.7 broadcast_in_dim.46.refs_1_
  33.0 16.4 %exchange1.1 = (f32[2,1408]{1,0:T(2,128)}, f32[7,48,384]{2,1,0:T(8,128)}, f32[7,48,384]{2,1,0:T(8,128)}, f32[48,384]{1,0:T(8,128)}) custom-call(f32[2,1408]{1,0:T(2,128)} %get-tuple-element.71.refs_0_, f32[8,1,128]{2,1,0:T(1,128)} %broadcast_in_dim.46.refs_1_, f32[7,7,48,384]{3,2,1,0:T(8,128)} %get-tuple-element.70.refs_2_.z1), custom_call_target="tpu_custom_call" | custom-call | tf_op jit(solution)/shard_map/exchange1/pallas_call | solution.py:890
  52.6 0.7 broadcast_multiply_fusion.wfb
  53.3 14.8 %space_convs.1 = (bf16[9,9,48,384]{3,2,1,0:T(8,128)(2,1)}, f32[7,7,48,384]{3,2,1,0:T(8,128)}, f32[2,384]{1,0:T(2,128)}) custom-call(s32[2]{0:T(128)} %pad_add_fusion.place, f32[7,7,48,384]{3,2,1,0:T(8,128)} %get-tuple-element.70.refs_2_.z1, f32[7,48,384]{2,1,0:T(8,128)} %get-tuple-element.72.row, f32[7,48,384]{2,1,0:T(8,128)} %get-tuple-element.73.col, ...), custom_call_target="tpu_custom_call" | custom-call | tf_op jit(solution)/shard_map/space_convs/pallas_call | solution.py:1007
  68.1 11.5 %exchange2.1 = (f32[2,384]{1,0:T(2,128)}, f32[7,48,384]{2,1,0:T(8,128)}, f32[7,48,384]{2,1,0:T(8,128)}, f32[48,384]{1,0:T(8,128)}) custom-call(f32[2,384]{1,0:T(2,128)} %get-tuple-element.77.refs_0_, f32[8,1,128]{2,1,0:T(1,128)} %broadcast_in_dim.46.refs_1_, f32[7,7,48,384]{3,2,1,0:T(8,128)} %get-tuple-element.76.refs_2_.z2), custom_call_target="tpu_custom_call" | custom-call | tf_op jit(solution)/shard_map/exchange2/pallas_call | solution.py:890
  80.8 9.9 %expand_moments.1 = (bf16[7,7,48,384]{3,2,1,0:T(8,128)(2,1)}, f32[2,1152]{1,0:T(2,128)}) custom-call(f32[7,7,48,384]{3,2,1,0:T(8,128)} %get-tuple-element.76.refs_2_.z2, f32[2,384]{1,0:T(2,128)} %get-tuple-element.78.mom.mom2, f32[1,384]{1,0:T(1,128)} %broadcast_in_dim.49.gain.gain2, f32[1,384]{1,0:T(1,128)} %broadcast_in_dim.50.shift.shift2, ...), custom_call_target="tpu_custom_call" | custom-call | tf_op jit(solution)/shard_map/expand_moments/pallas_call | solution.py:1021
  90.7 10.6 %exchange3.1.mom3 = f32[2,1152]{1,0:T(2,128)} custom-call(f32[2,1152]{1,0:T(2,128)} %get-tuple-element.82.refs_0_, f32[8,1,128]{2,1,0:T(1,128)} %broadcast_in_dim.46.refs_1_), custom_call_target="tpu_custom_call" | custom-call | tf_op jit(solution)/shard_map/exchange3/pallas_call | solution.py:890
  103.2 25.8 %outputs.1 = (bf16[12,7,7,4,1024]{4,3,2,1,0:T(4,128)(2,1)}, bf16[4,7,7,48,128]{4,3,2,1,0:T(8,128)(2,1)}, f32[7,7,48,1024]{3,2,1,0:T(8,128)}, f32[7,7,48,512]{3,2,1,0:T(8,128)}, f32[1,3328]{1,0:T(1,128)}) custom-call(bf16[7,7,48,384]{3,2,1,0:T(8,128)(2,1)} %get-tuple-element.79.a2, bf16[7,7,48,1024]{3,2,1,0:T(8,128)(2,1)} %get-tuple-element.80.zp, ...), custom_call_target="tpu_custom_call" | custom-call | tf_op jit(solution)/shard_map/outputs/pallas_call | solution.py:1037
  129.0 10.7 %exchange4.1.tot = f32[1,3328]{1,0:T(1,128)} custom-call(f32[1,3328]{1,0:T(1,128)} %get-tuple-element.88.refs_0_, f32[8,1,128]{2,1,0:T(1,128)} %broadcast_in_dim.46.refs_1_), custom_call_target="tpu_custom_call" | custom-call | tf_op jit(solution)/shard_map/exchange4/pallas_call | solution.py:890
  140.3 19.2 %expand_back.1 = (bf16[7,7,48,1024]{3,2,1,0:T(8,128)(2,1)}, bf16[7,7,48,1024]{3,2,1,0:T(8,128)(2,1)}, bf16[7,7,48,512]{3,2,1,0:T(8,128)(2,1)}, f32[7,7,48,384]{3,2,1,0:T(8,128)}, f32[1,768]{1,0:T(1,128)}) custom-call(f32[7,7,48,1024]{3,2,1,0:T(8,128)} %get-tuple-element.86.gs, f32[7,7,48,512]{3,2,1,0:T(8,128)} %get-tuple-element.87.gf, ...), custom_call_target="tpu_custom_call" | custom-call | tf_op jit(solution)/shard_map/expand_back/pallas_call | solution.py:1058
  159.4 13.5 %exchange5.1 = (f32[1,768]{1,0:T(1,128)}, f32[7,48,384]{2,1,0:T(8,128)}, f32[7,48,384]{2,1,0:T(8,128)}, f32[48,384]{1,0:T(8,128)}) custom-call(f32[1,768]{1,0:T(1,128)} %get-tuple-element.90.refs_0_, f32[8,1,128]{2,1,0:T(1,128)} %broadcast_in_dim.46.refs_1_, f32[7,7,48,384]{3,2,1,0:T(8,128)} %get-tuple-element.89.refs_2_.q2), custom_call_target="tpu_custom_call" | custom-call | tf_op jit(solution)/shard_map/exchange5/pallas_call | solution.py:890
  173.0 23.3 %space_back.1 = (f32[7,7,48,384]{3,2,1,0:T(8,128)}, f32[1,768]{1,0:T(1,128)}, bf16[3,3,256,256]{3,2,1,0:T(8,128)(2,1)}, f32[9,32,32]{2,1,0:T(8,128)}) custom-call(s32[2]{0:T(128)} %pad_add_fusion.place, f32[7,7,48,384]{3,2,1,0:T(8,128)} %get-tuple-element.89.refs_2_.q2, f32[7,7,48,384]{3,2,1,0:T(8,128)} %get-tuple-element.76.refs_2_.z2, ...), custom_call_target="tpu_custom_call" | custom-call | tf_op jit(solution)/shard_map/space_back/pallas_call | solution.py:1100
  196.2 9.9 %exchange6.1.tot = f32[1,768]{1,0:T(1,128)} custom-call(f32[1,768]{1,0:T(1,128)} %get-tuple-element.100.refs_0_, f32[8,1,128]{2,1,0:T(1,128)} %broadcast_in_dim.46.refs_1_), custom_call_target="tpu_custom_call" | custom-call | tf_op jit(solution)/shard_map/exchange6/pallas_call | solution.py:890
  206.2 25.4 %first_back.1 = (bf16[12,7,7,4,1024]{4,3,2,1,0:T(4,128)(2,1)}, bf16[4,7,7,48,128]{4,3,2,1,0:T(8,128)(2,1)}, bf16[7,7,48,768]{3,2,1,0:T(8,128)(2,1)}, bf16[7,7,48...) custom-call(f32[7,7,48,384]{3,2,1,0:T(8,128)} %get-tuple-element.99.q1, f32[7,7,48,384]{3,2,1,0:T(8,128)} %get-tuple-element.70.refs_2_.z1, ...), custom_call_target="tpu_custom_call" | custom-call | tf_op jit(solution)/shard_map/first_back/pallas_call | solution.py:1120
  231.5 16.2 %expand_weights.1 = (bf16[1280,1024]{1,0:T(8,128)(2,1)}, bf16[256,1024]{1,0:T(8,128)(2,1)}, f32[32,128]{1,0:T(8,128)}) custom-call(bf16[49,48,1280]{2,1,0:T(8,128)(2,1)} %bitcast.59, bf16[49,48,384]{2,1,0:T(8,128)(2,1)} %bitcast.62, bf16[49,48,1024]{2,1,0:T(8,128)(2,1)} %bitcast.61, bf16[49,48,1024]{2,1,0:T(8,128)(2,1)} %bitcast.64, ...), custom_call_target="tpu_custom_call" | custom-call | tf_op jit(solution)/shard_map/expand_weights/pallas_call | solution.py:1085
  247.7 13.8 %first_weights.1 = (bf16[3,1280,256]{2,1,0:T(8,128)(2,1)}, bf16[5,128,256]{2,1,0:T(8,128)(2,1)}, bf16[512,128]{1,0:T(8,128)(2,1)}) custom-call(bf16[49,48,1280]{2,1,0:T(8,128)(2,1)} %bitcast.60, bf16[49,48,512]{2,1,0:T(8,128)(2,1)} %bitcast.63, bf16[49,48,768]{2,1,0:T(8,128)(2,1)} %bitcast.67, bf16[49,48,512]{2,1,0:T(8,128)(2,1)} %bitcast.71, ...), custom_call_target="tpu_custom_call" | custom-call | tf_op jit(solution)/shard_map/first_weights/pallas_call | solution.py:1142
  261.5 88.1 %reduce7.1.done = bf16[13312,256]{1,0:T(8,128)(2,1)} custom-call(bf16[1280,1024]{1,0:T(8,128)(2,1)} %get-tuple-element.107.dwp, bf16[256,1024]{1,0:T(8,128)(2,1)} %get-tuple-element.108.dwc, bf16[3,3,256,256]{3,2,1,0:T(8,128)(2,1)} %get-tuple-element.109.dwb, bf16[3,1280,256]{2,1,0:T(8,128)(2,1)} %get-tuple-element.115.dwa, ...), custom_call_target="tpu_custom_call" | custom-call | tf_op jit(solution)/shard_map/reduce7/pallas_call | solution.py:836
  349.7 7.8 %unpack_weights.1 = (f32[1280,1024]{1,0:T(8,128)}, f32[256,1024]{1,0:T(8,128)}, f32[3,3,256,256]{3,2,1,0:T(8,128)}, f32[3,1280,256]{2,1,0:T(8,128)}, f32[5,128,256]{2,1,0:T(8,128)}, /*index=5*/f32[512,128]{1,0:T(8,128)}) custom-call(bf16[13312,256]{1,0:T(8,128)(2,1)} %reduce7.1.done), custom_call_target="tpu_custom_call" | custom-call | tf_op jit(solution)/shard_map/unpack_weights/pallas_call | solution.py:847
  357.5 1.4 slice.133
  358.9 1.6 slice.134
  360.5 1.3 slice.135
  361.9 0.6 pad_maximum_fusion
  362.5 0.6 pad_maximum_fusion.1
  363.1 0.6 pad_maximum_fusion.6
  363.7 0.6 pad_maximum_fusion.7
  (64 shorter events, 7.7 us)
Async XLA Ops:
  7.0 23.8 %copy-start.8 = (s32[32]{0:T(128)S(1)}, s32[32]{0:T(128)}, u32[]{:S(2)}) copy-start(s32[32]{0:T(128)} %param.19) | copy-start | bytes 388
  30.8 18.7 %copy-start.6 = (f32[192]{0:T(256)S(1)}, f32[192]{0:T(256)}, u32[]{:S(2)}) copy-start(f32[192]{0:T(256)} %param.30) | copy-start | bytes 2308
  30.8 18.8 %copy-start.4 = (f32[2560]{0:T(1024)S(1)}, f32[2560]{0:T(1024)}, u32[]{:S(2)}) copy-start(f32[2560]{0:T(1024)} %param.28) | copy-start | bytes 30724
  30.8 19.5 %copy-start.7 = (f32[192]{0:T(256)S(1)}, f32[192]{0:T(256)}, u32[]{:S(2)}) copy-start(f32[192]{0:T(256)} %param.31) | copy-start | bytes 2308
  30.8 19.7 %copy-start.5 = (f32[2560]{0:T(1024)S(1)}, f32[2560]{0:T(1024)}, u32[]{:S(2)}) copy-start(f32[2560]{0:T(1024)} %param.29) | copy-start | bytes 30724
  30.8 20.4 %copy-start.1 = (bf16[3,3,32,32]{3,2,1,0:T(8,128)(2,1)S(1)}, bf16[3,3,32,32]{3,2,1,0:T(8,128)(2,1)}, u32[]{:S(2)}) copy-start(bf16[3,3,32,32]{3,2,1,0:T(8,128)(2,1)} %param.26) | copy-start | bytes 55300
  349.6 12.2 %copy-start = (f32[1,3328]{1,0:T(1,128)S(1)}, f32[1,3328]{1,0:T(1,128)}, u32[]{:S(2)}) copy-start(f32[1,3328]{1,0:T(1,128)} %exchange4.1.tot) | copy-start | bytes 39940
  349.6 12.2 %copy-start.3 = (f32[1,768]{1,0:T(1,128)S(1)}, f32[1,768]{1,0:T(1,128)}, u32[]{:S(2)}) copy-start(f32[1,768]{1,0:T(1,128)} %get-tuple-element.98.tot) | copy-start | bytes 9220
  349.7 12.2 %copy-start.2 = (f32[1,768]{1,0:T(1,128)S(1)}, f32[1,768]{1,0:T(1,128)}, u32[]{:S(2)}) copy-start(f32[1,768]{1,0:T(1,128)} %exchange6.1.tot) | copy-start | bytes 9220

commit v3 on v2

v3 whole, which is shorter than its diff:
```python
import functools

import jax
import jax.numpy as jnp
from jax import lax
from jax.experimental import pallas as pl
from jax.experimental.pallas import tpu as pltpu
from jax.sharding import PartitionSpec as P

ALPHA = 4
H = 14
W = 14
C_IN = 1024
C_LAT = 256
C_MID = 256
C_FAST = 128
C_FMID = 32
C_JOIN = C_IN + C_LAT
MIX = C_MID + ALPHA * C_FMID
WIDE_FAST = ALPHA * C_FAST

eps_norm = 1e-05
f32 = jnp.float32
bf16 = jnp.bfloat16
MESH = pl.DeviceIdType.MESH
MIB = 1 << 20


def dot(a, b):
    return lax.dot_general(a, b, (((1,), (0,)), ((), ())), preferred_element_type=f32)


def dot_nt(a, b):
    return lax.dot_general(a, b, (((1,), (1,)), ((), ())), preferred_element_type=f32)


def dot_tn(a, b):
    return lax.dot_general(a, b, (((0,), (0,)), ((), ())), preferred_element_type=f32)


def sigmoid(v):
    return 0.5 + 0.5 * jnp.tanh(0.5 * v)


def later(y, clips):
    return jnp.concatenate([jnp.zeros_like(y[:, :clips]), y[:, : y.shape[1] - clips]], axis=1)


def sooner(y, clips):
    return jnp.concatenate([y[:, clips:], jnp.zeros_like(y[:, :clips])], axis=1)


def rows_sum(v):
    return jnp.sum(jnp.sum(v, axis=0), axis=0, keepdims=True)


def phase_sum(v):
    out = v
    for k in range(1, ALPHA):
        out = out + pltpu.roll(v, k * C_FMID, 1)
    return out


def block_sum(v):
    return sum(v[:, p * C_FAST : (p + 1) * C_FAST] for p in range(ALPHA))


def spread(mask, width):
    return jnp.tile(mask, (1, width // 128))


def frames_matrix(wfa_ref, out_ref, ends_ref):
    out_ref[...] = jnp.zeros_like(out_ref)
    ends_ref[...] = jnp.zeros_like(ends_ref)
    for p in range(ALPHA):
        for s in range(max(p - 1, 0), min(p + 2, ALPHA)):
            out_ref[p * C_FMID : (p + 1) * C_FMID, s * C_FAST : (s + 1) * C_FAST] = wfa_ref[s - p + 1]
    ends_ref[0, 0:C_FMID] = wfa_ref[0]
    ends_ref[1, 3 * C_FMID :] = wfa_ref[2]


def expand_matrix(wfc_ref, out_ref):
    out_ref[...] = jnp.zeros_like(out_ref)
    for p in range(ALPHA):
        out_ref[p * C_FMID : (p + 1) * C_FMID, p * C_FAST : (p + 1) * C_FAST] = wfc_ref[...]


class Exchange:
    def __init__(self, n_clip, moments, refs, rim_refs=None):
        self.n = n_clip
        self.moments = moments
        self.part, self.near, self.mid, self.far, self.near_send, self.near_recv, self.far_send, self.far_recv = refs
        self.clip, self.ha, self.wa = lax.axis_index("clip"), lax.axis_index("ha"), lax.axis_index("wa")
        self.me = 2 * self.ha + self.wa
        self.peers = [(1 - self.ha, self.wa), (self.ha, 1 - self.wa), (1 - self.ha, 1 - self.wa)]
        self.others = [lax.rem(self.clip + d, n_clip) for d in range(1, n_clip)]
        if rim_refs is not None:
            self.packs, self.lands, self.rim_send, self.rim_recv = rim_refs

    def signal(self):
        barrier = pltpu.get_barrier_semaphore()
        for a, b in self.peers:
            pl.semaphore_signal(barrier, inc=1, device_id=(self.clip, a, b), device_id_type=MESH)
        for other in self.others:
            pl.semaphore_signal(barrier, inc=1, device_id=(other, self.ha, self.wa), device_id_type=MESH)

    def meet(self):
        pl.semaphore_wait(pltpu.get_barrier_semaphore(), 3 + self.n - 1)

    def near_copy(self, k, slot):
        a, b = self.peers[k]
        return pltpu.make_async_remote_copy(
            src_ref=self.part, dst_ref=self.near.at[slot], send_sem=self.near_send.at[k],
            recv_sem=self.near_recv.at[slot], device_id=(self.clip, a, b), device_id_type=MESH,
        )

    def far_copy(self, d, slot):
        return pltpu.make_async_remote_copy(
            src_ref=self.mid, dst_ref=self.far.at[slot], send_sem=self.far_send.at[d],
            recv_sem=self.far_recv.at[slot], device_id=(self.others[d], self.ha, self.wa), device_id_type=MESH,
        )

    def rim_copy(self, k):
        a, b = self.peers[k]
        size = 1 if k == 2 else self.packs.shape[1]
        return pltpu.make_async_remote_copy(
            src_ref=self.packs.at[k, pl.ds(0, size)], dst_ref=self.lands.at[k, pl.ds(0, size)],
            send_sem=self.rim_send.at[k], recv_sem=self.rim_recv.at[k], device_id=(self.clip, a, b),
            device_id_type=MESH,
        )

    def send_near(self):
        for k in range(3):
            self.near_copy(k, self.me).start()
        self.near[self.me] = self.part[...]

    def send_rims(self, line, side):
        count = self.packs.shape[1]
        centre = self.part[0:1, :MIX] if self.moments else jnp.zeros((1, MIX), f32)
        self.packs[0] = (line[...] - centre).astype(bf16)
        self.packs[1] = (side[...] - centre).astype(bf16)
        self.packs[2, 0] = self.packs[0, (count - 1) * (1 - self.wa)]
        for k in range(3):
            self.rim_copy(k).start()

    def send_far(self):
        for k, (a, b) in enumerate(self.peers):
            self.near_copy(k, 2 * a + b).wait_recv()
        near = self.near
        if self.moments:
            mean = (near[0, 0:1] + near[1, 0:1] + near[2, 0:1] + near[3, 0:1]) * 0.25
            self.mid[0:1] = mean
            self.mid[1:2] = sum(near[k, 1:2] + (near[k, 0:1] - mean) ** 2 for k in range(4)) * 0.25
        else:
            self.mid[...] = near[0] + near[1] + near[2] + near[3]
        for d in range(self.n - 1):
            self.far_copy(d, self.clip).start()
        self.far[self.clip] = self.mid[...]

    def finish(self, out, weight):
        for d, other in enumerate(self.others):
            self.far_copy(d, other).wait_recv()
        width = out.shape[1]
        far = self.far
        if self.moments:
            mean = sum(far[k, 0:1] * spread(weight[k], width) for k in range(self.n))
            out[0:1] = mean
            out[1:2] = sum((far[k, 1:2] + (far[k, 0:1] - mean) ** 2) * spread(weight[k], width) for k in range(self.n))
        else:
            out[...] = sum(far[k] for k in range(self.n))
        for k in range(3):
            self.near_copy(k, self.me).wait_send()
        for d in range(self.n - 1):
            self.far_copy(d, self.clip).wait_send()

    def finish_rims(self, rims):
        for k, (a, b) in enumerate(self.peers):
            self.rim_copy(k).wait_recv()
            centre = self.near[2 * a + b, 0:1, :MIX] if self.moments else jnp.zeros((1, MIX), f32)
            land = self.lands[k, 0] if k == 2 else self.lands[k]
            rims[k][...] = land.astype(f32) + centre
        for k in range(3):
            self.rim_copy(k).wait_send()


def exchange_scratch(n_clip, count, width):
    return [
        pltpu.VMEM((count, width), f32),
        pltpu.VMEM((4, count, width), f32),
        pltpu.VMEM((count, width), f32),
        pltpu.VMEM((n_clip, count, width), f32),
        pltpu.SemaphoreType.DMA((3,)),
        pltpu.SemaphoreType.DMA((4,)),
        pltpu.SemaphoreType.DMA((n_clip,)),
        pltpu.SemaphoreType.DMA((n_clip,)),
    ]


def rim_scratch(side, slab):
    return [
        pltpu.VMEM((3, side, slab, MIX), bf16),
        pltpu.VMEM((3, side, slab, MIX), bf16),
        pltpu.SemaphoreType.DMA((3,)),
        pltpu.SemaphoreType.DMA((3,)),
    ]


def first_pass(clips, n_clip, xs, xf, m, perm, wl, wa, wp, wfa, weight,
               x_out, f_out, z_out, zp_out, st_out, base_out, mom, row, col, corner,
               keep, taps, ends, base, one, two, line, side, *refs):
    i = pl.program_id(0)
    cols = xs.shape[1]
    slab = m.shape[0]
    rows = cols * slab
    high = keep.shape[0]
    ex = Exchange(n_clip, True, refs[:8], refs[8:])
    here = cols * jnp.sum(m[...], axis=0, keepdims=True)
    count = high * here

    @pl.when(i == 0)
    def _():
        ex.signal()
        frames_matrix(wfa, taps, ends)

    @pl.when(i < high)
    def _():
        mask_in = spread(m[...], C_IN).astype(bf16)
        for w in range(cols):
            keep[i, w, :, :C_IN] = xs[:, w].reshape(slab, C_IN) * mask_in
            phases = dot(perm[...], xf[:, w].reshape(ALPHA * slab, C_FAST)).astype(bf16)
            for p in range(ALPHA):
                f_out[w, :, p * C_FAST : (p + 1) * C_FAST] = phases[p * slab : (p + 1) * slab]
        fast = f_out[...].reshape(rows, WIDE_FAST)
        lat = dot(fast[:, : 3 * C_FAST], wl[2:5].reshape(3 * C_FAST, C_LAT)).reshape(cols, slab, C_LAT)
        back = dot(fast[:, 2 * C_FAST :], wl[0:2].reshape(2 * C_FAST, C_LAT)).reshape(cols, slab, C_LAT)
        keep[i, :, :, C_IN:] = (lat + later(back, clips)).astype(bf16)
        x_out[...] = keep[i]
        joined = keep[i].reshape(rows, C_JOIN)
        za = dot(joined, wa[1]).reshape(cols, slab, C_MID)
        za = za + later(dot(joined, wa[0]).reshape(cols, slab, C_MID), clips)
        za = za + sooner(dot(joined, wa[2]).reshape(cols, slab, C_MID), clips)
        fa = dot_nt(fast, taps[...]).reshape(cols, slab, 128)
        fa = fa + later(dot_nt(fast[:, 3 * C_FAST :], ends[0]).reshape(cols, slab, 128), clips)
        fa = fa + sooner(dot_nt(fast[:, :C_FAST], ends[1]).reshape(cols, slab, 128), clips)
        z_out[:, :, :C_MID] = za
        z_out[:, :, C_MID:] = fa
        keep_rims(ex, i, high, z_out, line, side)
        add_moments(i == 0, ((0, za, 0), (C_MID, fa, 1)), m, here, base, one, two)

    @pl.when(i == high)
    def _():
        finish_moments(ex.part, base[...], one[...], two[...], count, ((0, C_MID, 0), (C_MID, 128, 1)))
        ex.meet()
        ex.send_near()
        ex.send_rims(line, side)

    @pl.when(i == high + 2)
    def _():
        ex.send_far()

    @pl.when(i >= high)
    def _():
        joined = keep[i - high].reshape(rows, C_JOIN)
        zp = dot(joined, wp[...]).reshape(cols, slab, C_IN)
        add_moments(i == high, ((MIX, zp, 0),), m, here, base, one, two)
        zp_out[...] = (zp - base[:, MIX:]).astype(bf16)

    @pl.when(i == 2 * high - 1)
    def _():
        s1 = one[:, MIX:] / spread(count, C_IN)
        st_out[0:1] = base[:, MIX:] + s1
        st_out[1:2] = two[:, MIX:] / spread(count, C_IN) - s1 * s1
        base_out[...] = base[:, MIX:]
        ex.finish(mom, weight)
        ex.finish_rims((row, col, corner))


def keep_rims(ex, i, high, block, line, side):
    side[i] = block[(block.shape[0] - 1) * (1 - ex.wa)]

    @pl.when(i == (high - 1) * (1 - ex.ha))
    def _():
        line[...] = block[...]


def add_moments(first, parts, m, here, base, one, two):
    @pl.when(first)
    def _():
        for at, z, fast in parts:
            width = z.shape[-1]
            mean = rows_sum(z * spread(m[...], width)) / spread(here, width)
            if fast:
                mean = phase_sum(mean) * 0.25
            base[:, at : at + width] = mean
            one[:, at : at + width] = jnp.zeros((1, width), f32)
            two[:, at : at + width] = jnp.zeros((1, width), f32)

    for at, z, _ in parts:
        width = z.shape[-1]
        off = (z - base[:, at : at + width]) * spread(m[...], width)
        one[:, at : at + width] += rows_sum(off)
        two[:, at : at + width] += rows_sum(off * off)


def finish_moments(st, base, one, two, count, parts):
    for at, width, fast in parts:
        s1 = one[:, at : at + width]
        s2 = two[:, at : at + width]
        if fast:
            s1 = phase_sum(s1) * 0.25
            s2 = phase_sum(s2) * 0.25
        n = spread(count.astype(f32), width)
        s1 = s1 / n
        st[0:1, at : at + width] = base[:, at : at + width] + s1
        st[1:2, at : at + width] = s2 / n - s1 * s1


def affine(moments, gain, shift, at, width):
    mean = moments[0:1, at : at + width]
    scale = lax.rsqrt(moments[1:2, at : at + width] + eps_norm)
    return mean, scale, gain[...], shift[...]


def second_pass(n_clip, z1_hbm, row, col, corner, mom, gain, shift, m, wb, wfb, stp, weight, cot,
                a_out, z_out, mom_out, zrow, zcol, zcorner, cot_out, z1, z1_sem, one, two, *refs):
    i = pl.program_id(0)
    high, cols, slab, _ = z1.shape
    rows = cols * slab
    ex = Exchange(n_clip, True, refs[:8], refs[8:])

    def fetch(h):
        return pltpu.make_async_copy(z1_hbm.at[h], z1.at[h], z1_sem.at[h])

    @pl.when(i == 0)
    def _():
        for h in range(high):
            fetch(h).start()
        ex.signal()
        mean, scale, g, b = affine(mom, gain, shift, 0, MIX)
        mult = scale * g
        mask = spread(m[...], MIX)

        def act(z):
            v = (z - mean) * mult + b
            return (v * sigmoid(v) * mask).astype(bf16)

        far = high + 1
        a_out[far * ex.ha] = jnp.zeros((cols + 2, slab, MIX), bf16)
        a_out[:, far * ex.wa] = jnp.zeros((high + 2, slab, MIX), bf16)
        a_out[far * (1 - ex.ha), 1 : 1 + cols] = act(row[...])
        a_out[1 : 1 + high, far * (1 - ex.wa)] = act(col[...])
        a_out[far * (1 - ex.ha), far * (1 - ex.wa)] = act(corner[...])

        def fill(h, carry):
            fetch(h).wait()
            a_out[h + 1, 1 : 1 + cols] = act(z1[h])
            return carry

        lax.fori_loop(0, high, fill, 0)

        def space(h, carry):
            slow = jnp.zeros((rows, C_MID), f32)
            fast = jnp.zeros((rows, 128), f32)
            for a in range(3):
                for c in range(3):
                    v = a_out[h + a, c : c + cols].reshape(rows, MIX)
                    slow = slow + dot(v[:, :C_MID], wb[a, c])
                    fast = fast + dot(v[:, C_MID:], wfb[3 * a + c])
            z_out[h, :, :, :C_MID] = slow.reshape(cols, slab, C_MID)
            z_out[h, :, :, C_MID:] = fast.reshape(cols, slab, 128)
            return carry

        lax.fori_loop(0, high, space, 0)
        here = cols * jnp.sum(m[...], axis=0, keepdims=True)
        base = rows_sum(z_out[0] * mask) / spread(here, MIX)
        base = jnp.concatenate([base[:, :C_MID], phase_sum(base[:, C_MID:]) * 0.25], axis=1)
        one[...] = jnp.zeros_like(one)
        two[...] = jnp.zeros_like(two)

        def gather(h, carry):
            off = (z_out[h] - base) * mask
            one[...] += rows_sum(off)
            two[...] += rows_sum(off * off)
            return carry

        lax.fori_loop(0, high, gather, 0)
        finish_moments(ex.part, base, one[...], two[...], high * here, ((0, C_MID, 0), (C_MID, 128, 1)))
        ex.part[:, MIX:] = stp[...]
        ex.meet()
        ex.send_near()
        ex.send_rims(z_out.at[(high - 1) * (1 - ex.ha)], z_out.at[:, (cols - 1) * (1 - ex.wa)])

    @pl.when(i == 3)
    def _():
        ex.send_far()

    @pl.when(i > 0)
    def _():
        for w in range(cols):
            cot_out[w] = cot[:, w].reshape(slab, C_IN)

    @pl.when(i == high)
    def _():
        ex.finish(mom_out, weight)
        ex.finish_rims((zrow, zcol, zcorner))


def third_pass(n_clip, z2, mom, gain, shift, m, wc, wfc, weight, fcot, perm,
               a_out, mom_out, fcot_out, big, base, one, two, *refs):
    i = pl.program_id(0)
    high = pl.num_programs(0) // 2
    cols, slab, _ = z2.shape
    rows = cols * slab
    ex = Exchange(n_clip, True, refs)
    here = cols * jnp.sum(m[...], axis=0, keepdims=True)

    @pl.when(i == 0)
    def _():
        ex.signal()
        expand_matrix(wfc, big)

    @pl.when(i < high)
    def _():
        mean, scale, g, b = affine(mom, gain, shift, 0, MIX)
        v = (z2[...] - mean) * (scale * g) + b
        a_out[...] = (v * sigmoid(v) * spread(m[...], MIX)).astype(bf16)
        a2 = a_out[...].reshape(rows, MIX)
        zc = dot(a2[:, :C_MID], wc[...]).reshape(cols, slab, C_IN)
        fc = dot(a2[:, C_MID:], big[...]).reshape(cols, slab, WIDE_FAST)

        @pl.when(i == 0)
        def _():
            base[:, :C_IN] = rows_sum(zc * spread(m[...], C_IN)) / spread(here, C_IN)
            base[:, C_IN:] = block_sum(rows_sum(fc * spread(m[...], WIDE_FAST))) / (4.0 * here)
            one[...] = jnp.zeros_like(one)
            two[...] = jnp.zeros_like(two)

        off = (zc - base[:, :C_IN]) * spread(m[...], C_IN)
        one[:, :C_IN] += rows_sum(off)
        two[:, :C_IN] += rows_sum(off * off)
        off = (fc - jnp.tile(base[:, C_IN:], (1, ALPHA))) * spread(m[...], WIDE_FAST)
        one[:, C_IN:] += block_sum(rows_sum(off)) * 0.25
        two[:, C_IN:] += block_sum(rows_sum(off * off)) * 0.25

    @pl.when(i == high)
    def _():
        finish_moments(ex.part, base[...], one[...], two[...], high * here, ((0, C_IN + C_FAST, 0),))
        ex.meet()
        ex.send_near()

    @pl.when(i == high + 2)
    def _():
        ex.send_far()

    @pl.when(i >= high)
    def _():
        for w in range(cols):
            phases = dot(perm[...], fcot[:, w].reshape(ALPHA * slab, C_FAST)).astype(bf16)
            for p in range(ALPHA):
                fcot_out[w, :, p * C_FAST : (p + 1) * C_FAST] = phases[p * slab : (p + 1) * slab]

    @pl.when(i == 2 * high - 1)
    def _():
        ex.finish(mom_out, weight)


def fourth_pass(n_clip, clips, a2, zp, base, mom2, mom3, sgain, sshift, fgain, fshift, cot, fcot, fast_in, m, perm, wc,
                wfc, weight, so, fo, gs, gf, tot, so_keep, fo_keep, sums, big, *refs):
    i = pl.program_id(0)
    high = pl.num_programs(0) // 2
    cols, slab, _ = a2.shape
    ex = Exchange(n_clip, False, refs)

    @pl.when(i == 0)
    def _():
        ex.signal()
        expand_matrix(wfc, big)
        sums[...] = jnp.zeros_like(sums)

    def tile_sum(v):
        return jnp.sum(v.reshape(slab // 8, 8, v.shape[-1]), axis=0)

    @pl.when(i < high)
    def _():
        mask = spread(m[...], C_IN)
        mask_f = spread(m[...], WIDE_FAST)
        mean_c = mom3[0:1, :C_IN]
        scale_c = lax.rsqrt(mom3[1:2, :C_IN] + eps_norm)
        mean_p = mom2[0:1, MIX:] - base[...]
        scale_p = lax.rsqrt(mom2[1:2, MIX:] + eps_norm)
        mean_f = jnp.tile(mom3[0:1, C_IN:], (1, ALPHA))
        scale_f = jnp.tile(lax.rsqrt(mom3[1:2, C_IN:] + eps_norm), (1, ALPHA))
        gain_c, gain_p = sgain[:, :C_IN], sgain[:, C_IN:]
        shift_cp = sshift[:, :C_IN] + sshift[:, C_IN:]
        gain_f = jnp.tile(fgain[...], (1, ALPHA))
        shift_f = jnp.tile(fshift[...], (1, ALPHA))
        totals = [jnp.zeros((8, C_IN), f32)] * 3 + [jnp.zeros((8, WIDE_FAST), f32)] * 2
        for w in range(cols):
            zc = (dot(a2[w, :, :C_MID], wc[...]) - mean_c) * scale_c
            zq = (zp[w].astype(f32) - mean_p) * scale_p
            ps = gain_c * zc + gain_p * zq + shift_cp
            sig = sigmoid(ps)
            so_keep[i, w] = (ps * sig * mask).astype(bf16)
            back = cot[w].astype(f32) * (sig * (1.0 + ps * (1.0 - sig)) * mask)
            gs[w] = back
            totals[0] += tile_sum(back)
            totals[1] += tile_sum(back * zc)
            totals[2] += tile_sum(back * zq)
            fc = (dot(a2[w, :, C_MID:], big[...]) - mean_f) * scale_f
            pf = gain_f * fc + shift_f + fast_in[w].astype(f32)
            sig = sigmoid(pf)
            fo_keep[i, w] = (pf * sig).astype(bf16)
            fback = fcot[w].astype(f32) * (sig * (1.0 + pf * (1.0 - sig)))
            gf[w] = fback
            totals[3] += tile_sum(fback)
            totals[4] += tile_sum(fback * fc)
        for k in range(3):
            sums[:, k * C_IN : (k + 1) * C_IN] += jnp.sum(totals[k], axis=0, keepdims=True)
        for k in range(2):
            at = 3 * C_IN + k * C_FAST
            sums[:, at : at + C_FAST] += block_sum(jnp.sum(totals[3 + k], axis=0, keepdims=True))

    @pl.when(i == high)
    def _():
        ex.part[...] = sums[...]
        ex.meet()
        ex.send_near()

    @pl.when(i == high + 2)
    def _():
        ex.send_far()

    @pl.when(i >= high)
    def _():
        for w in range(cols):
            so[:, w] = so_keep[i - high, w].reshape(slab // clips, clips, C_IN)
            wide = fo_keep[i - high, w]
            stacked = jnp.concatenate([wide[:, p * C_FAST : (p + 1) * C_FAST] for p in range(ALPHA)], axis=0)
            fo[:, w] = dot_tn(perm[...], stacked).astype(bf16).reshape(clips, slab, C_FAST)

    @pl.when(i == 2 * high - 1)
    def _():
        ex.finish(tot, weight)


def fifth_pass(n_clip, gs, gf, a2, zp, base, z2, mom2, mom3, tot4, inv, sgain, fgain, gain2, shift2, m, wc, wfc, x, weight,
               dzp_out, q_out, tot, row, col, corner, wp_out, wc_out, wfc_out,
               dzc_keep, dzp_keep, dfc_keep, a_keep, sums, big, line, side, *refs):
    i = pl.program_id(0)
    high, cols, slab, _ = dzc_keep.shape
    n = high * cols
    rows = cols * slab
    ex = Exchange(n_clip, False, refs[:8], refs[8:])

    @pl.when(i == 0)
    def _():
        ex.signal()
        expand_matrix(wfc, big)
        sums[...] = jnp.zeros_like(sums)

    @pl.when(i < high)
    def _():
        mask = spread(m[...], C_IN)
        inv_s = spread(inv[...], C_IN)
        inv_f = 0.25 * inv[...]
        mean_c = mom3[0:1, :C_IN]
        scale_c = lax.rsqrt(mom3[1:2, :C_IN] + eps_norm)
        mean_p = mom2[0:1, MIX:] - base[...]
        scale_p = lax.rsqrt(mom2[1:2, MIX:] + eps_norm)
        mean_f = jnp.tile(mom3[0:1, C_IN:], (1, ALPHA))
        scale_f = jnp.tile(lax.rsqrt(mom3[1:2, C_IN:] + eps_norm), (1, ALPHA))
        mult_c = sgain[:, :C_IN] * scale_c
        mult_p = sgain[:, C_IN:] * scale_p
        mult_f = jnp.tile(fgain[...], (1, ALPHA)) * scale_f
        first_s = tot4[:, :C_IN] * inv_s
        second_c = tot4[:, C_IN : 2 * C_IN] * inv_s
        second_p = tot4[:, 2 * C_IN : 3 * C_IN] * inv_s
        first_f = jnp.tile(tot4[:, 3 * C_IN : 3 * C_IN + C_FAST] * inv_f, (1, ALPHA))
        second_f = jnp.tile(tot4[:, 3 * C_IN + C_FAST :] * inv_f, (1, ALPHA))
        mask_f = spread(m[...], WIDE_FAST)
        a_keep[i] = a2[...]
        for w in range(cols):
            zc = (dot(a2[w, :, :C_MID], wc[...]) - mean_c) * scale_c
            zq = (zp[w].astype(f32) - mean_p) * scale_p
            g = gs[w]
            dzc_keep[i, w] = (mult_c * (g - mask * (first_s + zc * second_c))).astype(bf16)
            dzp = (mult_p * (g - mask * (first_s + zq * second_p))).astype(bf16)
            dzp_keep[i, w] = dzp
            dzp_out[w] = dzp
            fc = (dot(a2[w, :, C_MID:], big[...]) - mean_f) * scale_f
            dfc_keep[i, w] = (mult_f * (gf[w] - mask_f * (first_f + fc * second_f))).astype(bf16)
        da = dot_nt(dzc_keep[i].reshape(rows, C_IN), wc[...]).reshape(cols, slab, C_MID)
        df = dot_nt(dfc_keep[i].reshape(rows, WIDE_FAST), big[...]).reshape(cols, slab, 128)
        grads = jnp.concatenate([da, df], axis=2)
        slope_back(grads, z2[...], mom2, gain2, shift2, m, q_out, sums)
        keep_rims(ex, i, high, q_out, line, side)

    @pl.when(i == high)
    def _():
        ex.part[...] = sums[...]
        ex.meet()
        ex.send_near()
        ex.send_rims(line, side)

    @pl.when(i == high + 2)
    def _():
        ex.send_far()

    @pl.when(i >= high)
    def _():
        wp_out[...] = dot_tn(
            x[...].reshape(n * slab, C_MID), dzp_keep[...].reshape(n * slab, C_IN)
        ).astype(bf16)

    @pl.when(i == pl.num_programs(0) - 1)
    def _():
        a = a_keep[...].reshape(n * slab, MIX)
        wc_out[...] = dot_tn(a[:, :C_MID], dzc_keep[...].reshape(n * slab, C_IN)).astype(bf16)
        wide = dot_tn(a[:, C_MID:], dfc_keep[...].reshape(n * slab, WIDE_FAST))
        wfc_out[...] = sum(
            wide[p * C_FMID : (p + 1) * C_FMID, p * C_FAST : (p + 1) * C_FAST] for p in range(ALPHA)
        )
        ex.finish(tot, weight)
        ex.finish_rims((row, col, corner))


def slope_back(grads, z, mom, gain, shift, m, q_out, sums):
    mean, scale, g, b = affine(mom, gain, shift, 0, MIX)
    zhat = (z - mean) * scale
    v = g * zhat + b
    sig = sigmoid(v)
    q = grads * (sig * (1.0 + v * (1.0 - sig)) * spread(m[...], MIX))
    q_out[...] = q
    for k, s in enumerate((rows_sum(q), rows_sum(q * zhat))):
        at = k * MIX
        sums[:, at : at + C_MID] += s[:, :C_MID]
        sums[:, at + C_MID : at + MIX] += phase_sum(s[:, C_MID:])


def norm_terms(mom, gain, tot, inv):
    mean = mom[0:1, :MIX]
    scale = lax.rsqrt(mom[1:2, :MIX] + eps_norm)
    share = jnp.concatenate([spread(inv[...], C_MID), 0.25 * inv[...]], axis=1)
    return mean, scale, gain[...] * scale, tot[:, :MIX] * share, tot[:, MIX:] * share


def sixth_pass(n_clip, q2_hbm, z2_hbm, z1_hbm, a1_hbm, qrow, qcol, qcorner, zrow, zcol, zcorner, mom1, mom2, tot5, inv,
               gain1, shift1, gain2, m, wb, wfb, weight, q_out, tot, wb_out, wfb_out,
               wide, q2, z2, z1, a1, q2_sem, z2_sem, z1_sem, a1_sem, sums, *refs):
    i = pl.program_id(0)
    high, cols, slab, _ = z1.shape
    rows = cols * slab
    ex = Exchange(n_clip, False, refs)

    moved = ((q2_hbm, q2, q2_sem), (z2_hbm, z2, z2_sem), (z1_hbm, z1, z1_sem))

    def fetch(k, h):
        a, b, s = moved[k]
        return pltpu.make_async_copy(a.at[h], b.at[h], s.at[h])

    def fetch_a1():
        return pltpu.make_async_copy(a1_hbm, a1, a1_sem.at[0])

    @pl.when(i == 0)
    def _():
        for h in range(high):
            fetch(0, h).start()
            fetch(1, h).start()
        for h in range(high):
            fetch(2, h).start()
        fetch_a1().start()
        ex.signal()
        mean, scale, mult, first, second = norm_terms(mom2, gain2, tot5, inv)
        mask = spread(m[...], MIX)

        def grad(q, z):
            return (mult * (q - mask * (first + (z - mean) * scale * second))).astype(bf16)

        far = high + 1
        wide[far * ex.ha] = jnp.zeros((cols + 2, slab, MIX), bf16)
        wide[:, far * ex.wa] = jnp.zeros((high + 2, slab, MIX), bf16)
        wide[far * (1 - ex.ha), 1 : 1 + cols] = grad(qrow[...], zrow[...])
        wide[1 : 1 + high, far * (1 - ex.wa)] = grad(qcol[...], zcol[...])
        wide[far * (1 - ex.ha), far * (1 - ex.wa)] = grad(qcorner[...], zcorner[...])

        def fill(h, carry):
            fetch(0, h).wait()
            fetch(1, h).wait()
            wide[h + 1, 1 : 1 + cols] = grad(q2[h], z2[h])
            return carry

        lax.fori_loop(0, high, fill, 0)
        sums[...] = jnp.zeros_like(sums)

        def space(h, carry):
            fetch(2, h).wait()
            slow = jnp.zeros((rows, C_MID), f32)
            fast = jnp.zeros((rows, 128), f32)
            for a in range(3):
                for c in range(3):
                    v = wide[h + 2 - a, 2 - c : 2 - c + cols].reshape(rows, MIX)
                    slow = slow + dot_nt(v[:, :C_MID], wb[a, c])
                    fast = fast + dot_nt(v[:, C_MID:], wfb[3 * a + c])
            grads = jnp.concatenate([slow, fast], axis=1).reshape(cols, slab, MIX)
            slope_back(grads, z1[h], mom1, gain1, shift1, m, q_out.at[h], sums)
            return carry

        lax.fori_loop(0, high, space, 0)
        ex.part[...] = sums[...]
        ex.meet()
        ex.send_near()
        fetch_a1().wait()

    @pl.when(i == 3)
    def _():
        ex.send_far()

    @pl.when(i > 0)
    def _():
        tap = i - 1
        v = a1[pl.ds(tap // 3, high), pl.ds(lax.rem(tap, 3), cols)].reshape(high * rows, MIX)
        d = wide[1 : 1 + high, 1 : 1 + cols].reshape(high * rows, MIX)
        wb_out[...] = dot_tn(v[:, :C_MID], d[:, :C_MID]).astype(bf16)
        both = dot_tn(v[:, C_MID:], d[:, C_MID:])
        wfb_out[tap] = sum(
            both[p * C_FMID : (p + 1) * C_FMID, p * C_FMID : (p + 1) * C_FMID] for p in range(ALPHA)
        )

    @pl.when(i == 9)
    def _():
        ex.finish(tot, weight)


def first_back(clips, q1, z1, mom1, tot, inv, gain1, m, perm, dzp, gf, wl, wa, wp, wfa, sx, fx, da_out, dl_out, df_out,
               taps, ends):
    h = pl.program_id(0)
    cols, slab, _ = q1.shape
    rows = cols * slab

    @pl.when(h == 0)
    def _():
        frames_matrix(wfa, taps, ends)

    mean, scale, mult, first, second = norm_terms(mom1, gain1, tot, inv)
    zhat = (z1[...] - mean) * scale
    dz = mult * (q1[...] - spread(m[...], MIX) * (first + zhat * second))
    up, down = sooner(dz, clips), later(dz, clips)
    for k, v in enumerate((up, dz, down)):
        da_out[:, :, k * C_MID : (k + 1) * C_MID] = v[:, :, :C_MID].astype(bf16)
        df_out[:, :, k * 128 : (k + 1) * 128] = v[:, :, C_MID:].astype(bf16)
    dj = dot_nt(dzp[...].reshape(rows, C_IN), wp[...])
    for k in range(3):
        dj = dj + dot_nt(da_out[:, :, k * C_MID : (k + 1) * C_MID].reshape(rows, C_MID), wa[k])
    mask = spread(m[...], C_IN)
    dj = dj.reshape(cols, slab, C_JOIN)
    for w in range(cols):
        sx[:, w] = (dj[w, :, :C_IN] * mask).astype(bf16).reshape(slab // clips, clips, C_IN)
    dlat = dj[:, :, C_IN:].astype(bf16).astype(f32)
    dl_out[:, :, :C_LAT] = dlat.astype(bf16)
    dl_out[:, :, C_LAT:] = sooner(dlat, clips).astype(bf16)
    df = df_out[...].reshape(rows, 3 * 128)
    dl = dl_out[...].reshape(rows, 2 * C_LAT)
    total = gf[...].reshape(rows, WIDE_FAST).astype(f32) + dot(df[:, 128:256], taps[...])
    head = dot_nt(dl[:, :C_LAT], wl[2:5].reshape(3 * C_FAST, C_LAT))
    tail = dot_nt(dl[:, C_LAT:], wl[0:2].reshape(2 * C_FAST, C_LAT))
    blocks = [total[:, p * C_FAST : (p + 1) * C_FAST] for p in range(ALPHA)]
    for p in range(3):
        blocks[p] = blocks[p] + head[:, p * C_FAST : (p + 1) * C_FAST]
    for p in range(2):
        blocks[2 + p] = blocks[2 + p] + tail[:, p * C_FAST : (p + 1) * C_FAST]
    blocks[3] = blocks[3] + dot(df[:, :128], ends[0])
    blocks[0] = blocks[0] + dot(df[:, 256:], ends[1])
    blocks = [v.astype(bf16) for v in blocks]
    for w in range(cols):
        stacked = jnp.concatenate([v[w * slab : (w + 1) * slab] for v in blocks], axis=0)
        fx[:, w] = dot_tn(perm[...], stacked).astype(bf16).reshape(clips, slab, C_FAST)


def first_weights(x, f, da, dl, df, dwfc, dwfb, wa_out, wl_out, small_out):
    i = pl.program_id(0)
    n, slab, _ = x.shape
    rows = n * slab
    for k in range(3):
        wa_out[k] = dot_tn(x[...].reshape(rows, C_MID), da[:, :, k * C_MID : (k + 1) * C_MID].reshape(rows, C_MID)).astype(bf16)

    @pl.when(i == pl.num_programs(0) - 1)
    def _():
        fast = f[...].reshape(rows, WIDE_FAST)
        d = dl[...].reshape(rows, 2 * C_LAT)
        wl_out[2:5] = dot_tn(fast[:, : 3 * C_FAST], d[:, :C_LAT]).reshape(3, C_FAST, C_LAT).astype(bf16)
        wl_out[0:2] = dot_tn(fast[:, 2 * C_FAST :], d[:, C_LAT:]).reshape(2, C_FAST, C_LAT).astype(bf16)
        g = df[...].reshape(rows, 3 * 128)
        mid = dot_tn(g[:, 128:256], fast)
        sums = [jnp.zeros((C_FMID, C_FAST), f32) for _ in range(3)]
        for p in range(ALPHA):
            for s in range(max(p - 1, 0), min(p + 2, ALPHA)):
                sums[s - p + 1] += mid[p * C_FMID : (p + 1) * C_FMID, s * C_FAST : (s + 1) * C_FAST]
        sums[0] += dot_tn(g[:, :128], fast[:, 3 * C_FAST :])[:C_FMID]
        sums[2] += dot_tn(g[:, 256:], fast[:, :C_FAST])[3 * C_FMID :]
        small_out[...] = jnp.zeros_like(small_out)
        for k in range(3):
            small_out[k * C_FMID : (k + 1) * C_FMID] = sums[k].astype(bf16)
        small_out[3 * C_FMID : 4 * C_FMID] = dwfc[...].astype(bf16)
        for k in range(9):
            at = (4 + k) * C_FMID
            small_out[at : at + C_FMID, :C_FMID] = dwfb[k].astype(bf16)


UNIT = 512


def bit_of(axis, power):
    return lax.rem(lax.axis_index(axis) // (1 << power), 2)


def partner_of(axis, power, bit):
    where = {name: lax.axis_index(name) for name in ("clip", "ha", "wa")}
    where[axis] = where[axis] + (1 - 2 * bit) * (1 << power)
    return (where["clip"], where["ha"], where["wa"])


def stage_orders(n_clip, sets):
    rest = [("wa", 0)] + [("clip", b) for b in range(n_clip.bit_length() - 1)]
    turn, last = rest[:3], rest[3:]
    return [[("ha", 0)] + turn[s % len(turn) :] + turn[: s % len(turn)] + last for s in range(sets)]


def chunk_of(rows):
    best = 16
    for k in range(16, min(rows, 256) + 1, 16):
        if rows % k == 0:
            best = k
    return best


def land_plan(n_clip, sizes):
    stages = len(stage_orders(n_clip, 1)[0])
    starts, total = [], 0
    for size in sizes:
        starts.append(total)
        for _ in range(stages):
            size = size // 2 if size % 32 == 0 else size
            total += size
    return starts, total


def reduce_sets(n_clip, starts, sizes, mine, land, done, rs_send, rs_recv, ag_send, ag_recv):
    orders = stage_orders(n_clip, len(starts))
    stages = len(orders[0])
    low = [jnp.int32(v) for v in starts]
    size = list(sizes)
    at = land_plan(n_clip, sizes)[0]
    trail = [[] for _ in starts]
    sent = []

    def rows(ref, begin, count):
        return ref.at[pl.ds(pl.multiple_of(begin, 16), count)]

    def send(s, k):
        axis, power = orders[s][k]
        bit = bit_of(axis, power)
        halve = size[s] % 32 == 0
        count = size[s] // 2 if halve else size[s]
        begin = low[s] + (1 - bit) * count if halve else low[s]
        copy = pltpu.make_async_remote_copy(
            src_ref=rows(mine, begin, count), dst_ref=rows(land, at[s], count),
            send_sem=rs_send.at[s, k], recv_sem=rs_recv.at[s, k],
            device_id=partner_of(axis, power, bit), device_id_type=MESH,
        )
        copy.start()
        trail[s].append((copy, low[s], count, halve, axis, power, bit, at[s]))
        if halve:
            low[s] = low[s] + bit * count
            size[s] = count
        at[s] += count

    def gather(s, k):
        copy, _, count, halve, axis, power, bit, begin = trail[s][k]
        copy.wait_recv()
        if not halve:
            copy.wait_send()
        step = chunk_of(count)

        def add(i, carry):
            own = pl.ds(pl.multiple_of(low[s] + i * step, 16), step)
            came = pl.ds(pl.multiple_of(begin + i * step, 16), step)
            mine[own, :] = (mine[own, :].astype(f32) + land[came, :].astype(f32)).astype(bf16)
            return carry

        lax.fori_loop(0, count // step, add, 0)
        if halve:
            sent.append(copy)

    for s in range(len(starts)):
        send(s, 0)
    for k in range(stages):
        for s in range(len(starts)):
            gather(s, k)
            if k + 1 < stages:
                send(s, k + 1)
    for copy in sent:
        copy.wait_send()

    for s in range(len(starts)):
        step = chunk_of(size[s])

        def keep(i, carry):
            own = pl.ds(pl.multiple_of(low[s] + i * step, 16), step)
            done[own, :] = mine[own, :]
            return carry

        lax.fori_loop(0, size[s] // step, keep, 0)

    copies = []
    pending = [None] * len(starts)

    def spread_out(s, k):
        _, before, count, halve, axis, power, bit, _ = trail[s][k]
        if not halve:
            return
        copy = pltpu.make_async_remote_copy(
            src_ref=rows(done, low[s], count), dst_ref=rows(done, low[s], count),
            send_sem=ag_send.at[s, k], recv_sem=ag_recv.at[s, k],
            device_id=partner_of(axis, power, bit), device_id_type=MESH,
        )
        copy.start()
        other = before + (1 - bit) * count
        pending[s] = pltpu.make_async_remote_copy(
            src_ref=rows(done, other, count), dst_ref=rows(done, other, count),
            send_sem=ag_send.at[s, k], recv_sem=ag_recv.at[s, k],
            device_id=partner_of(axis, power, bit), device_id_type=MESH,
        )
        low[s] = before
        copies.append(copy)

    for s in range(len(starts)):
        spread_out(s, stages - 1)
    for k in range(stages - 1, -1, -1):
        for s in range(len(starts)):
            if pending[s] is not None:
                pending[s].wait_recv()
                pending[s] = None
            if k > 0:
                spread_out(s, k - 1)
    for copy in copies:
        copy.wait_send()


def greet(n_clip):
    barrier = pltpu.get_barrier_semaphore()
    stages = stage_orders(n_clip, 1)[0]
    for axis, power in stages:
        bit = bit_of(axis, power)
        pl.semaphore_signal(barrier, inc=1, device_id=partner_of(axis, power, bit), device_id_type=MESH)
    pl.semaphore_wait(barrier, len(stages))


def weight_pieces(dws_rows):
    pieces = []
    row = 0
    for which, count in ((0, C_JOIN), (1, C_MID)):
        for b in range(C_IN // 256):
            pieces.append((row, count, which, (slice(None), slice(b * 256, (b + 1) * 256))))
            row += count
    for i in range(3):
        for j in range(3):
            pieces.append((row, C_MID, 2, (i, j)))
            row += C_MID
    for k in range(3):
        pieces.append((row, C_JOIN, 3, (k,)))
        row += C_JOIN
    for k in range(5):
        pieces.append((row, C_FAST, 4, (k,)))
        row += C_FAST
    return pieces, row


def reduce_weights(n_clip, starts, sizes, dwp, dwc, dwb, dwa, dwl, dws, done,
                   mine, land, rs_send, rs_recv, ag_send, ag_recv):
    sources = (dwp, dwc, dwb, dwa, dwl)
    pieces, row = weight_pieces(dws.shape[0])
    for begin, count, which, at in pieces:
        mine[begin : begin + count, :] = sources[which].at[at][...]
    half = dws.shape[0] // 2
    mine[row : row + half, :128] = dws[:half]
    mine[row : row + half, 128:] = dws[half:]
    end = row + half
    if end < mine.shape[0]:
        mine[end:, :] = jnp.zeros((mine.shape[0] - end, 256), bf16)
    greet(n_clip)
    reduce_sets(n_clip, starts, sizes, mine, land, done, rs_send, rs_recv, ag_send, ag_recv)


def unpack_weights(done, wp_out, wc_out, wb_out, wa_out, wl_out, ws_out):
    targets = (wp_out, wc_out, wb_out, wa_out, wl_out)
    pieces, row = weight_pieces(ws_out.shape[0])
    for begin, count, which, at in pieces:
        targets[which].at[at][...] = done[begin : begin + count, :].astype(f32)
    half = ws_out.shape[0] // 2
    ws_out[:half] = done[row : row + half, :128].astype(f32)
    ws_out[half:] = done[row : row + half, 128:].astype(f32)


def vmem_spec():
    return pl.BlockSpec(memory_space=pltpu.VMEM)


def shaped(shape, kind):
    return jax.ShapeDtypeStruct(shape, kind)


def run_reduce(ident, n_clip, arrays):
    total = sum(v.size for v in arrays) // 256
    units = -(-total // UNIT)
    share = [-(-units // 3), -(-(units - units // 3) // 2), units // 3]
    share[1] = units - share[0] - share[2]
    sizes = [v * UNIT for v in share]
    starts = [0, sizes[0], sizes[0] + sizes[1]]
    rows = units * UNIT
    land_rows = land_plan(n_clip, sizes)[1]
    stages = len(stage_orders(n_clip, 1)[0])
    sems = [pltpu.SemaphoreType.DMA((3, stages))] * 4
    vm = vmem_spec()
    done = pl.pallas_call(
        functools.partial(reduce_weights, n_clip, starts, sizes),
        in_specs=[vm] * len(arrays),
        out_specs=vm,
        out_shape=shaped((rows, 256), bf16),
        scratch_shapes=[pltpu.VMEM((v, 256), bf16) for v in (rows, land_rows)] + sems,
        compiler_params=pltpu.CompilerParams(
            collective_id=ident, has_side_effects=True, vmem_limit_bytes=60 * MIB
        ),
        name=f"reduce{ident}",
    )(*arrays)
    return pl.pallas_call(
        unpack_weights,
        in_specs=[vm],
        out_specs=(vm,) * len(arrays),
        out_shape=tuple(shaped(v.shape, f32) for v in arrays),
        compiler_params=params(60),
        name="unpack_weights",
    )(done)


def whole(shape):
    return pl.BlockSpec(shape, lambda h: (0,) * len(shape))


def per_line(shape):
    return pl.BlockSpec((None,) + tuple(shape), lambda h: (h,) + (0,) * len(shape))


def params(limit):
    return pltpu.CompilerParams(vmem_limit_bytes=60 * MIB)


def on_device(
    slow_input,
    fast_input,
    frame_counts,
    lateral_weight,
    slow_a_weight,
    slow_b_weight,
    slow_c_weight,
    slow_proj_weight,
    fast_a_weight,
    fast_b_weight,
    fast_c_weight,
    slow_gain,
    slow_shift,
    fast_gain,
    fast_shift,
    slow_cotangent,
    fast_cotangent,
):
    n_clip = lax.axis_size("clip")
    clips, frames, high, cols, _ = slow_input.shape
    slab = clips * frames
    own = lax.dynamic_slice_in_dim(frame_counts, lax.axis_index("clip") * clips, clips)
    row_t = jnp.arange(slab) // clips
    row_c = jnp.arange(slab) % clips
    real = row_t < own[row_c]
    m = jnp.broadcast_to(real.astype(f32)[:, None], (slab, 128))
    col_c = jnp.arange(ALPHA * slab) // (ALPHA * frames)
    col_f = jnp.arange(ALPHA * slab) % (ALPHA * frames)
    want_f = (ALPHA * row_t[None, :] + jnp.arange(ALPHA)[:, None]).reshape(-1)
    want_c = jnp.tile(row_c, ALPHA)
    perm = (
        (want_f[:, None] == col_f[None, :]) & (want_c[:, None] == col_c[None, :]) & jnp.tile(real, ALPHA)[:, None]
    ).astype(bf16)
    real_total = jnp.sum(frame_counts).astype(f32)
    weight = jnp.broadcast_to(
        (jnp.sum(frame_counts.reshape(n_clip, clips), axis=1).astype(f32) / real_total)[:, None, None], (n_clip, 1, 128)
    )
    inv = jnp.full((1, 128), 1.0, f32) / (real_total * (H * W))
    def mixed(slow, fast, k):
        lo = fast[k * C_FMID : (k + 1) * C_FMID]
        return jnp.concatenate([slow[k * C_MID : (k + 1) * C_MID], jnp.tile(lo, ALPHA)])[None]

    gain1, shift1 = mixed(slow_gain, fast_gain, 0), mixed(slow_shift, fast_shift, 0)
    gain2, shift2 = mixed(slow_gain, fast_gain, 1), mixed(slow_shift, fast_shift, 1)
    sgain, sshift = slow_gain[None, 2 * C_MID :], slow_shift[None, 2 * C_MID :]
    fgain, fshift = fast_gain[None, 2 * C_FMID :], fast_shift[None, 2 * C_FMID :]
    wfa = fast_a_weight.transpose(0, 2, 1)
    eye = jnp.eye(ALPHA, dtype=bf16)
    wfb = (eye[None, :, None, :, None] * fast_b_weight.reshape(9, 1, C_FMID, 1, C_FMID)).reshape(9, 128, 128)

    xs = slow_input.transpose(1, 2, 3, 0, 4)
    xf = fast_input.transpose(0, 2, 3, 1, 4)
    cot = slow_cotangent.transpose(1, 2, 3, 0, 4)
    fcot = fast_cotangent.transpose(0, 2, 3, 1, 4)
    def lines(c, kind):
        return shaped((high, cols, slab, c), kind)

    m_spec = whole((slab, 128))
    vm = vmem_spec()
    hbm = pl.BlockSpec(memory_space=pl.ANY)

    def early_line(shape):
        return pl.BlockSpec((None,) + tuple(shape), lambda i: (jnp.minimum(i, high - 1),) + (0,) * len(shape))

    def late_line(shape, begin):
        return pl.BlockSpec((None,) + tuple(shape), lambda i: (jnp.maximum(i - begin, 0),) + (0,) * len(shape))

    def slow_block(index):
        return pl.BlockSpec((frames, None, cols, clips, C_IN), lambda i: (0, index(i), 0, 0, 0))

    def fast_block(index):
        return pl.BlockSpec((clips, None, cols, ALPHA * frames, C_FAST), lambda i: (0, index(i), 0, 0, 0))

    def early(i):
        return jnp.minimum(i, high - 1)

    def after(begin):
        return lambda i: jnp.maximum(i - begin, 0)

    def remote(ident):
        return pltpu.CompilerParams(collective_id=ident, has_side_effects=True, vmem_limit_bytes=60 * MIB)

    rim_shapes = (shaped((cols, slab, MIX), f32), shaped((high, slab, MIX), f32), shaped((slab, MIX), f32))
    edge_scratch = [pltpu.VMEM((cols, slab, MIX), f32), pltpu.VMEM((high, slab, MIX), f32)]
    rims = rim_scratch(cols, slab)
    L1 = MIX + C_IN
    x, f, z1, zp, stp, base, mom1, row1, col1, corner1 = pl.pallas_call(
        functools.partial(first_pass, clips, n_clip),
        grid=(2 * high,),
        in_specs=[slow_block(early), fast_block(early)] + [vm] * 7,
        out_specs=(
            early_line((cols, slab, C_JOIN)), early_line((cols, slab, WIDE_FAST)), early_line((cols, slab, MIX)),
            late_line((cols, slab, C_IN), high), vm, vm, vm, vm, vm, vm,
        ),
        out_shape=(
            lines(C_JOIN, bf16), lines(WIDE_FAST, bf16), lines(MIX, f32), lines(C_IN, bf16), shaped((2, C_IN), f32),
            shaped((1, C_IN), f32), shaped((2, MIX), f32),
        ) + rim_shapes,
        scratch_shapes=[
            pltpu.VMEM((high, cols, slab, C_JOIN), bf16), pltpu.VMEM((128, WIDE_FAST), bf16),
            pltpu.VMEM((2, 128, C_FAST), bf16), pltpu.VMEM((1, L1), f32), pltpu.VMEM((1, L1), f32),
            pltpu.VMEM((1, L1), f32),
        ] + edge_scratch + exchange_scratch(n_clip, 2, MIX) + rims,
        compiler_params=remote(1),
        name="first_pass",
    )(xs, xf, m, perm, lateral_weight, slow_a_weight, slow_proj_weight, wfa, weight)

    a1, z2, mom2, zrow, zcol, zcorner, cot = pl.pallas_call(
        functools.partial(second_pass, n_clip),
        grid=(high + 1,),
        in_specs=[hbm] + [vm] * 11 + [slow_block(after(1))],
        out_specs=(vm, vm, vm, vm, vm, vm, late_line((cols, slab, C_IN), 1)),
        out_shape=(
            shaped((high + 2, cols + 2, slab, MIX), bf16), lines(MIX, f32), shaped((2, L1), f32),
        ) + rim_shapes + (lines(C_IN, bf16),),
        scratch_shapes=[
            pltpu.VMEM((high, cols, slab, MIX), f32), pltpu.SemaphoreType.DMA((high,)), pltpu.VMEM((1, MIX), f32),
            pltpu.VMEM((1, MIX), f32),
        ] + exchange_scratch(n_clip, 2, L1) + rims,
        compiler_params=remote(2),
        name="second_pass",
    )(z1, row1, col1, corner1, mom1, gain1, shift1, m, slow_b_weight, wfb, stp, weight, cot)

    L3 = C_IN + C_FAST
    a2, mom3, fcot = pl.pallas_call(
        functools.partial(third_pass, n_clip),
        grid=(2 * high,),
        in_specs=[early_line((cols, slab, MIX))] + [vm] * 7 + [fast_block(after(high)), vm],
        out_specs=(early_line((cols, slab, MIX)), vm, late_line((cols, slab, WIDE_FAST), high)),
        out_shape=(lines(MIX, bf16), shaped((2, L3), f32), lines(WIDE_FAST, bf16)),
        scratch_shapes=[pltpu.VMEM((128, WIDE_FAST), bf16)] + [pltpu.VMEM((1, L3), f32)] * 3
        + exchange_scratch(n_clip, 2, L3),
        compiler_params=remote(3),
        name="third_pass",
    )(z2, mom2, gain2, shift2, m, slow_c_weight, fast_c_weight, weight, fcot, perm)

    L4 = 3 * C_IN + 2 * C_FAST
    so, fo, gs, gf, tot4 = pl.pallas_call(
        functools.partial(fourth_pass, n_clip, clips),
        grid=(2 * high,),
        in_specs=[early_line((cols, slab, MIX)), early_line((cols, slab, C_IN))] + [vm] * 7 + [
            early_line((cols, slab, C_IN)), early_line((cols, slab, WIDE_FAST)), early_line((cols, slab, WIDE_FAST)),
        ] + [vm] * 5,
        out_specs=(
            slow_block(after(high)), fast_block(after(high)), early_line((cols, slab, C_IN)),
            early_line((cols, slab, WIDE_FAST)), vm,
        ),
        out_shape=(
            shaped(xs.shape, bf16), shaped(xf.shape, bf16), lines(C_IN, f32), lines(WIDE_FAST, f32),
            shaped((1, L4), f32),
        ),
        scratch_shapes=[
            pltpu.VMEM((high, cols, slab, C_IN), bf16), pltpu.VMEM((high, cols, slab, WIDE_FAST), bf16),
            pltpu.VMEM((1, L4), f32), pltpu.VMEM((128, WIDE_FAST), bf16),
        ] + exchange_scratch(n_clip, 1, L4),
        compiler_params=remote(4),
        name="fourth_pass",
    )(
        a2, zp, base, mom2, mom3, sgain, sshift, fgain, fshift, cot, fcot, f, m, perm, slow_c_weight, fast_c_weight, weight,
    )

    n = high * cols

    def flat(v):
        return v.reshape((n,) + v.shape[2:])

    steps = C_JOIN // C_MID
    dzp, q2, tot5, qrow, qcol, qcorner, dwp, dwc, dwfc = pl.pallas_call(
        functools.partial(fifth_pass, n_clip),
        grid=(high + steps,),
        in_specs=[
            early_line((cols, slab, C_IN)), early_line((cols, slab, WIDE_FAST)), early_line((cols, slab, MIX)),
            early_line((cols, slab, C_IN)), vm, early_line((cols, slab, MIX)),
        ] + [vm] * 11 + [pl.BlockSpec((n, slab, C_MID), lambda i: (0, 0, jnp.maximum(i - high, 0))), vm],
        out_specs=(
            early_line((cols, slab, C_IN)), early_line((cols, slab, MIX)), vm, vm, vm, vm,
            pl.BlockSpec((C_MID, C_IN), lambda i: (jnp.maximum(i - high, 0), 0)), vm, vm,
        ),
        out_shape=(lines(C_IN, bf16), lines(MIX, f32), shaped((1, 2 * MIX), f32)) + rim_shapes + (
            shaped((C_JOIN, C_IN), bf16), shaped((C_MID, C_IN), bf16), shaped((C_FMID, C_FAST), f32),
        ),
        scratch_shapes=[
            pltpu.VMEM((high, cols, slab, C_IN), bf16), pltpu.VMEM((high, cols, slab, C_IN), bf16),
            pltpu.VMEM((high, cols, slab, WIDE_FAST), bf16), pltpu.VMEM((high, cols, slab, MIX), bf16),
            pltpu.VMEM((1, 2 * MIX), f32), pltpu.VMEM((128, WIDE_FAST), bf16),
        ] + edge_scratch + exchange_scratch(n_clip, 1, 2 * MIX) + rims,
        compiler_params=remote(5),
        name="fifth_pass",
    )(
        gs, gf, a2, zp, base, z2, mom2, mom3, tot4, inv, sgain, fgain, gain2, shift2, m, slow_c_weight, fast_c_weight,
        flat(x), weight,
    )

    q1, tot6, dwb, dwfb = pl.pallas_call(
        functools.partial(sixth_pass, n_clip),
        grid=(10,),
        in_specs=[hbm] * 4 + [vm] * 17,
        out_specs=(
            vm, vm, pl.BlockSpec((None, None, C_MID, C_MID), lambda i: (jnp.maximum(i - 1, 0) // 3, lax.rem(jnp.maximum(i - 1, 0), 3), 0, 0)),
            vm,
        ),
        out_shape=(
            lines(MIX, f32), shaped((1, 2 * MIX), f32), shaped((3, 3, C_MID, C_MID), bf16),
            shaped((9, C_FMID, C_FMID), f32),
        ),
        scratch_shapes=[pltpu.VMEM((high + 2, cols + 2, slab, MIX), bf16)]
        + [pltpu.VMEM((high, cols, slab, MIX), f32)] * 3
        + [pltpu.VMEM((high + 2, cols + 2, slab, MIX), bf16)]
        + [pltpu.SemaphoreType.DMA((high,))] * 3
        + [pltpu.SemaphoreType.DMA((1,)), pltpu.VMEM((1, 2 * MIX), f32)]
        + exchange_scratch(n_clip, 1, 2 * MIX),
        compiler_params=remote(6),
        name="sixth_pass",
    )(
        q2, z2, z1, a1, qrow, qcol, qcorner, zrow, zcol, zcorner, mom1, mom2, tot5, inv, gain1, shift1, gain2, m,
        slow_b_weight, wfb, weight,
    )

    perm_spec = whole((ALPHA * slab, ALPHA * slab))
    sx, fx, da, dl, df = pl.pallas_call(
        functools.partial(first_back, clips),
        grid=(high,),
        in_specs=[
            per_line((cols, slab, MIX)), per_line((cols, slab, MIX)), whole((2, MIX)), whole((1, 2 * MIX)),
            whole((1, 128)), whole((1, MIX)), m_spec, perm_spec, per_line((cols, slab, C_IN)),
            per_line((cols, slab, WIDE_FAST)), whole((5, C_FAST, C_LAT)), whole((3, C_JOIN, C_MID)),
            whole((C_JOIN, C_IN)), whole((3, C_FMID, C_FAST)),
        ],
        out_specs=(
            slow_block(early), fast_block(early), per_line((cols, slab, 3 * C_MID)), per_line((cols, slab, 2 * C_LAT)),
            per_line((cols, slab, 3 * 128)),
        ),
        out_shape=(
            shaped(xs.shape, bf16), shaped(xf.shape, bf16), lines(3 * C_MID, bf16), lines(2 * C_LAT, bf16),
            lines(3 * 128, bf16),
        ),
        scratch_shapes=[pltpu.VMEM((128, WIDE_FAST), bf16), pltpu.VMEM((2, 128, C_FAST), bf16)],
        compiler_params=params(40),
        name="first_back",
    )(q1, z1, mom1, tot6, inv, gain1, m, perm, dzp, gf, lateral_weight, slow_a_weight, slow_proj_weight, wfa)

    dwa, dwl, dws = pl.pallas_call(
        first_weights,
        grid=(C_JOIN // C_MID,),
        in_specs=[
            pl.BlockSpec((n, slab, C_MID), lambda i: (0, 0, i)), whole((n, slab, WIDE_FAST)),
            whole((n, slab, 3 * C_MID)), whole((n, slab, 2 * C_LAT)), whole((n, slab, 3 * 128)),
            whole((C_FMID, C_FAST)), whole((9, C_FMID, C_FMID)),
        ],
        out_specs=(
            pl.BlockSpec((3, C_MID, C_MID), lambda i: (0, i, 0)), whole((5, C_FAST, C_LAT)), whole((512, C_FAST)),
        ),
        out_shape=(
            shaped((3, C_JOIN, C_MID), bf16), shaped((5, C_FAST, C_LAT), bf16), shaped((512, C_FAST), bf16),
        ),
        compiler_params=params(48),
        name="first_weights",
    )(flat(x), flat(f), flat(da), flat(dl), flat(df), dwfc, dwfb)

    dwp, dwc, dwb, dwa, dwl, dws = run_reduce(7, n_clip, (dwp, dwc, dwb, dwa, dwl, dws))
    dwfa = dws[: 3 * C_FMID].reshape(3, C_FMID, C_FAST)
    dwfc = dws[3 * C_FMID : 4 * C_FMID]
    dwfb = dws[4 * C_FMID : 13 * C_FMID, :C_FMID]

    def joined_sums(k):
        first = [tot6[0, k * MIX : (k + 1) * MIX], tot5[0, k * MIX : (k + 1) * MIX]]
        last = tot4[0, :C_IN] if k == 0 else tot4[0, C_IN : 2 * C_IN]
        proj = tot4[0, :C_IN] if k == 0 else tot4[0, 2 * C_IN : 3 * C_IN]
        at = 3 * C_IN + k * C_FAST
        slow = jnp.concatenate([first[0][:C_MID], first[1][:C_MID], last, proj])
        lo = C_MID + C_FMID
        fast = jnp.concatenate([first[0][C_MID:lo], first[1][C_MID:lo], tot4[0, at : at + C_FAST]])
        return slow, fast

    slow_shift_grad, fast_shift_grad = joined_sums(0)
    slow_gain_grad, fast_gain_grad = joined_sums(1)
    return (
        so.transpose(3, 0, 1, 2, 4),
        fo.transpose(0, 3, 1, 2, 4),
        sx.transpose(3, 0, 1, 2, 4),
        fx.transpose(0, 3, 1, 2, 4),
        dwl,
        dwa,
        dwb,
        dwc,
        dwp,
        dwfa.transpose(0, 2, 1),
        dwfb.reshape(3, 3, C_FMID, C_FMID),
        dwfc,
        slow_gain_grad,
        slow_shift_grad,
        fast_gain_grad,
        fast_shift_grad,
    )


def solution(mesh):
    tiles = P("clip", None, "ha", "wa", None)
    return jax.shard_map(
        on_device,
        mesh=mesh,
        in_specs=(tiles, tiles) + (P(),) * 13 + (tiles, tiles),
        out_specs=(tiles,) * 4 + (P(),) * 12,
        check_vma=False,
    )
```

time: 365 us -> 331 us (0.907)
  Pallas kernels: 341 us -> 299 us
  local copies, waits for them, and re-layouts: 13.9 us -> 22.3 us
    pallas_call x13 -> x6, Pallas kernels: 206 us -> 161 us  [the longest x1 31.5 us: on_device(): pl.pallas_call(functools.partial(fifth_pass, n_clip), grid=(high + steps,...]
    unnamed x18 -> x20, local copies, waits for them, and re-layouts: 0.05 us -> 7.84 us
where the time goes in v3:
time: 331 us
  Pallas kernels  299 us (90%)
  local copies, waits for them, and re-layouts  22.3 us (7%)
  other arithmetic  8.09 us (2%)
    pallas_call x1, Pallas kernels, run_reduce(): pl.pallas_call(functools.partial(reduce_weights, n_clip, starts, sizes),...  90.8 us
    pallas_call x1, Pallas kernels, on_device(): pl.pallas_call(functools.partial(fifth_pass, n_clip), grid=(high + steps,...  31.5 us
    pallas_call x1, Pallas kernels, on_device(): pl.pallas_call(functools.partial(first_pass, clips, n_clip), grid=(2 * hi...  31.5 us
    pallas_call x1, Pallas kernels, on_device(): pl.pallas_call(functools.partial(fourth_pass, n_clip, clips), grid=(2 * h...  28.1 us
    pallas_call x1, Pallas kernels, on_device(): pl.pallas_call(functools.partial(second_pass, n_clip), grid=(high + 1,),...  25.9 us
    pallas_call x1, Pallas kernels, on_device(): pl.pallas_call(functools.partial(first_back, clips), grid=(high,), in_spe...  25.4 us
    pallas_call x1, Pallas kernels, on_device(): pl.pallas_call(functools.partial(sixth_pass, n_clip), grid=(10,), in_spec...  24.9 us
    pallas_call x1, Pallas kernels, on_device(): pl.pallas_call(functools.partial(third_pass, n_clip), grid=(2 * high,), i...  18.9 us

profile of v3, /device:TPU:0, one launch (start us, length us, event | category | flops | bytes accessed | tf_op | source)
XLA Modules:
  0.0 330.7 jit_solution(18192609209680417732)
XLA Ops:
  0.7 0.7 dynamic_slice.3
  1.4 0.6 fusion.13
  2.0 2.6 fusion.4
  4.6 0.7 broadcast_in_dim.22.m
  5.6 0.8 and_convert_fusion.perm
  6.4 0.7 reshape.201
  7.2 1.3 reduce_sum.19
  9.2 0.7 broadcast_in_dim.46.weight
  9.9 31.5 %first_pass.1 = (bf16[7,7,48,1280]{3,2,1,0:T(8,128)(2,1)}, bf16[7,7,48,512]{3,2,1,0:T(8,128)(2,1)}, f32[7,7,48,384]{3,2,1,0:T(8,128)}, bf16[7,7,48,1024]{3,2,1,0...) custom-call(bf16[12,7,7,4,1024]{4,3,2,1,0:T(4,128)(2,1)} %bitcast.57, ...), custom_call_target="tpu_custom_call" | custom-call | tf_op jit(solution)/shard_map/first_pass/pallas_call | solution.py:1144
  43.6 0.6 mul.47
  44.4 0.7 broadcast_multiply_fusion.wfb
  45.1 25.9 %second_pass.1 = (bf16[9,9,48,384]{3,2,1,0:T(8,128)(2,1)}, f32[7,7,48,384]{3,2,1,0:T(8,128)}, f32[2,1408]{1,0:T(2,128)}, f32[7,48,384]{2,1,0:T(8,128)}, f32[7,48...) custom-call(f32[7,7,48,384]{3,2,1,0:T(8,128)} %get-tuple-element.68.z1_hbm.z1, ...), custom_call_target="tpu_custom_call" | custom-call | tf_op jit(solution)/shard_map/second_pass/pallas_call | solution.py:1165
  72.2 18.9 %third_pass.1 = (bf16[7,7,48,384]{3,2,1,0:T(8,128)(2,1)}, f32[2,1152]{1,0:T(2,128)}, bf16[7,7,48,512]{3,2,1,0:T(8,128)(2,1)}) custom-call(f32[7,7,48,384]{3,2,1,0:T(8,128)} %get-tuple-element.74.z2.z2_hbm, f32[2,1408]{1,0:T(2,128)} %get-tuple-element.75.mom.mom2, f32[1,384]{1,0:T(1,128)} %broadcast_in_dim.49.gain.gain2, ...), custom_call_target="tpu_custom_call" | custom-call | tf_op jit(solution)/shard_map/third_pass/pallas_call | solution.py:1182
  91.1 0.6 slice.129
  91.7 0.6 slice.130
  92.3 0.6 slice_bitcast_fusion.6
  92.9 28.1 %fourth_pass.1 = (bf16[12,7,7,4,1024]{4,3,2,1,0:T(4,128)(2,1)}, bf16[4,7,7,48,128]{4,3,2,1,0:T(8,128)(2,1)}, f32[7,7,48,1024]{3,2,1,0:T(8,128)}, f32[7,7,48,512]{3,2,1,0:T(8,128)}, f32[1,3328]{1,0:T(1,128)}) custom-call(bf16[7,7,48,384]{3,2,1,0:T(8,128)(2,1)} %get-tuple-element.76.a2, bf16[7,7,48,1024]{3,2,1,0:T(8,128)(2,1)} %get-tuple-element.77.zp, ...), custom_call_target="tpu_custom_call" | custom-call | tf_op jit(solution)/shard_map/fourth_pass/pallas_call | solution.py:1195
  121.6 31.5 %fifth_pass.1 = (bf16[7,7,48,1024]{3,2,1,0:T(8,128)(2,1)}, f32[7,7,48,384]{3,2,1,0:T(8,128)}, f32[1,768]{1,0:T(1,128)}, f32[7,48,384]{2,1,0:T(8,128)}, f32[7,48,...) custom-call(f32[7,7,48,1024]{3,2,1,0:T(8,128)} %get-tuple-element.85, ...), custom_call_target="tpu_custom_call" | custom-call | tf_op jit(solution)/shard_map/fifth_pass/pallas_call | solution.py:1225
  153.2 24.9 %sixth_pass.1 = (f32[7,7,48,384]{3,2,1,0:T(8,128)}, f32[1,768]{1,0:T(1,128)}, bf16[3,3,256,256]{3,2,1,0:T(8,128)(2,1)}, f32[9,32,32]{2,1,0:T(8,128)}) custom-call(f32[7,7,48,384]{3,2,1,0:T(8,128)} %get-tuple-element.89.q2_hbm, f32[7,7,48,384]{3,2,1,0:T(8,128)} %get-tuple-element.74.z2.z2_hbm, f32[7,7,48,384]{3,2,1,0:T(8,128)} %get-tuple-element.68.z1_hbm.z1, ...), custom_call_target="tpu_custom_call" | custom-call | tf_op jit(solution)/shard_map/sixth_pass/pallas_call | solution.py:1251
  178.1 25.4 %first_back.1 = (bf16[12,7,7,4,1024]{4,3,2,1,0:T(4,128)(2,1)}, bf16[4,7,7,48,128]{4,3,2,1,0:T(8,128)(2,1)}, bf16[7,7,48,768]{3,2,1,0:T(8,128)(2,1)}, bf16[7,7,48...) custom-call(f32[7,7,48,384]{3,2,1,0:T(8,128)} %get-tuple-element.98.q1, f32[7,7,48,384]{3,2,1,0:T(8,128)} %get-tuple-element.68.z1_hbm.z1, ...), custom_call_target="tpu_custom_call" | custom-call | tf_op jit(solution)/shard_map/first_back/pallas_call | solution.py:1277
  203.6 13.8 %first_weights.1 = (bf16[3,1280,256]{2,1,0:T(8,128)(2,1)}, bf16[5,128,256]{2,1,0:T(8,128)(2,1)}, bf16[512,128]{1,0:T(8,128)(2,1)}) custom-call(bf16[49,48,1280]{2,1,0:T(8,128)(2,1)} %bitcast.54, bf16[49,48,512]{2,1,0:T(8,128)(2,1)} %bitcast.55, bf16[49,48,768]{2,1,0:T(8,128)(2,1)} %bitcast.59, bf16[49,48,512]{2,1,0:T(8,128)(2,1)} %bitcast.63, ...), custom_call_target="tpu_custom_call" | custom-call | tf_op jit(solution)/shard_map/first_weights/pallas_call | solution.py:1299
  217.4 90.8 %reduce7.1.done = bf16[13312,256]{1,0:T(8,128)(2,1)} custom-call(bf16[1280,1024]{1,0:T(8,128)(2,1)} %get-tuple-element.103.dwp, bf16[256,1024]{1,0:T(8,128)(2,1)} %get-tuple-element.104.dwc, bf16[3,3,256,256]{3,2,1,0:T(8,128)(2,1)} %get-tuple-element.105.dwb, bf16[3,1280,256]{2,1,0:T(8,128)(2,1)} %get-tuple-element.111.dwa, ...), custom_call_target="tpu_custom_call" | custom-call | tf_op jit(solution)/shard_map/reduce7/pallas_call | solution.py:1024
  308.2 7.8 %unpack_weights.1 = (f32[1280,1024]{1,0:T(8,128)}, f32[256,1024]{1,0:T(8,128)}, f32[3,3,256,256]{3,2,1,0:T(8,128)}, f32[3,1280,256]{2,1,0:T(8,128)}, f32[5,128,256]{2,1,0:T(8,128)}, /*index=5*/f32[512,128]{1,0:T(8,128)}) custom-call(bf16[13312,256]{1,0:T(8,128)(2,1)} %reduce7.1.done), custom_call_target="tpu_custom_call" | custom-call | tf_op jit(solution)/shard_map/unpack_weights/pallas_call | solution.py:1035
  316.0 1.4 slice.133
  317.4 1.6 slice.134
  319.0 1.3 slice.135
  320.4 0.6 pad_maximum_fusion
  321.0 0.6 pad_maximum_fusion.1
  321.6 0.6 pad_maximum_fusion.6
  322.2 0.6 pad_maximum_fusion.7
  322.9 6.4 %copy.35 = bf16[4,12,7,7,1024]{4,0,3,2,1:T(4,128)(2,1)} copy(bf16[4,12,7,7,1024]{4,0,3,2,1:T(4,128)(2,1)} %bitcast.56) | data formatting | bytes 9633792
  329.3 1.4 copy.36
  (58 shorter events, 4.5 us)
Async XLA Ops:
  9.8 31.5 %copy-start.7 = (f32[192]{0:T(256)S(1)}, f32[192]{0:T(256)}, u32[]{:S(2)}) copy-start(f32[192]{0:T(256)} %param.30) | copy-start | bytes 2308
  9.8 31.7 %copy-start.5 = (f32[2560]{0:T(1024)S(1)}, f32[2560]{0:T(1024)}, u32[]{:S(2)}) copy-start(f32[2560]{0:T(1024)} %param.28) | copy-start | bytes 30724
  9.8 32.3 %copy-start.8 = (f32[192]{0:T(256)S(1)}, f32[192]{0:T(256)}, u32[]{:S(2)}) copy-start(f32[192]{0:T(256)} %param.31) | copy-start | bytes 2308
  9.8 32.5 %copy-start.6 = (f32[2560]{0:T(1024)S(1)}, f32[2560]{0:T(1024)}, u32[]{:S(2)}) copy-start(f32[2560]{0:T(1024)} %param.29) | copy-start | bytes 30724
  9.8 33.2 %copy-start.1 = (bf16[3,3,32,32]{3,2,1,0:T(8,128)(2,1)S(1)}, bf16[3,3,32,32]{3,2,1,0:T(8,128)(2,1)}, u32[]{:S(2)}) copy-start(bf16[3,3,32,32]{3,2,1,0:T(8,128)(2,1)} %param.26) | copy-start | bytes 55300
  308.1 12.2 %copy-start.2 = (f32[1,3328]{1,0:T(1,128)S(1)}, f32[1,3328]{1,0:T(1,128)}, u32[]{:S(2)}) copy-start(f32[1,3328]{1,0:T(1,128)} %get-tuple-element.87.tot4) | copy-start | bytes 39940
  308.1 12.2 %copy-start.4 = (f32[1,768]{1,0:T(1,128)S(1)}, f32[1,768]{1,0:T(1,128)}, u32[]{:S(2)}) copy-start(f32[1,768]{1,0:T(1,128)} %get-tuple-element.97.tot5) | copy-start | bytes 9220
  308.2 12.2 %copy-start.3 = (f32[1,768]{1,0:T(1,128)S(1)}, f32[1,768]{1,0:T(1,128)}, u32[]{:S(2)}) copy-start(f32[1,768]{1,0:T(1,128)} %get-tuple-element.99.tot) | copy-start | bytes 9220
  322.9 6.4 %copy-start = (bf16[4,7,7,48,128]{4,3,2,1,0:T(8,128)(2,1)S(1)}, bf16[4,7,7,48,128]{4,3,2,1,0:T(8,128)(2,1)}, u32[]{:S(2)}) copy-start(bf16[4,7,7,48,128]{4,3,2,1,0:T(8,128)(2,1)} %get-tuple-element.84) | copy-start | bytes 7225348

commit v4 on v3

--- a/solution.py
+++ b/solution.py
@@ -318,10 +318,10 @@
 def affine(moments, gain, shift, at, width):
     mean = moments[0:1, at : at + width]
     scale = lax.rsqrt(moments[1:2, at : at + width] + eps_norm)
-    return mean, scale, gain[...], shift[...]
-
-
-def second_pass(n_clip, z1_hbm, row, col, corner, mom, gain, shift, m, wb, wfb, stp, weight, cot,
+    return mean, scale, gain, shift
+
+
+def second_pass(n_clip, z1_hbm, row, col, corner, mom, mids, m, wb, wfb, stp, weight, cot,
                 a_out, z_out, mom_out, zrow, zcol, zcorner, cot_out, z1, z1_sem, one, two, *refs):
     i = pl.program_id(0)
     high, cols, slab, _ = z1.shape
@@ -336,7 +336,7 @@
         for h in range(high):
             fetch(h).start()
         ex.signal()
-        mean, scale, g, b = affine(mom, gain, shift, 0, MIX)
+        mean, scale, g, b = affine(mom, mids[0], mids[1], 0, MIX)
         mult = scale * g
         mask = spread(m[...], MIX)
 
@@ -405,7 +405,7 @@
         ex.finish_rims((zrow, zcol, zcorner))
 
 
-def third_pass(n_clip, z2, mom, gain, shift, m, wc, wfc, weight, fcot, perm,
+def third_pass(n_clip, z2, mom, mids, m, wc, wfc, weight, fcot, perm,
                a_out, mom_out, fcot_out, big, base, one, two, *refs):
     i = pl.program_id(0)
     high = pl.num_programs(0) // 2
@@ -421,7 +421,7 @@
 
     @pl.when(i < high)
     def _():
-        mean, scale, g, b = affine(mom, gain, shift, 0, MIX)
+        mean, scale, g, b = affine(mom, mids[2], mids[3], 0, MIX)
         v = (z2[...] - mean) * (scale * g) + b
         a_out[...] = (v * sigmoid(v) * spread(m[...], MIX)).astype(bf16)
         a2 = a_out[...].reshape(rows, MIX)
@@ -464,7 +464,7 @@
         ex.finish(mom_out, weight)
 
 
-def fourth_pass(n_clip, clips, a2, zp, base, mom2, mom3, sgain, sshift, fgain, fshift, cot, fcot, fast_in, m, perm, wc,
+def fourth_pass(n_clip, clips, a2, zp, base, mom2, mom3, sgain, sshift, fends, cot, fcot, fast_in, m, perm, wc,
                 wfc, weight, so, fo, gs, gf, tot, so_keep, fo_keep, sums, big, *refs):
     i = pl.program_id(0)
     high = pl.num_programs(0) // 2
@@ -490,10 +490,11 @@
         scale_p = lax.rsqrt(mom2[1:2, MIX:] + eps_norm)
         mean_f = jnp.tile(mom3[0:1, C_IN:], (1, ALPHA))
         scale_f = jnp.tile(lax.rsqrt(mom3[1:2, C_IN:] + eps_norm), (1, ALPHA))
-        gain_c, gain_p = sgain[:, :C_IN], sgain[:, C_IN:]
-        shift_cp = sshift[:, :C_IN] + sshift[:, C_IN:]
-        gain_f = jnp.tile(fgain[...], (1, ALPHA))
-        shift_f = jnp.tile(fshift[...], (1, ALPHA))
+        mid, far = 2 * C_MID, 2 * C_MID + C_IN
+        gain_c, gain_p = sgain[:, mid:far], sgain[:, far:]
+        shift_cp = sshift[:, mid:far] + sshift[:, far:]
+        gain_f = jnp.tile(fends[0], (1, ALPHA))
+        shift_f = jnp.tile(fends[1], (1, ALPHA))
         totals = [jnp.zeros((8, C_IN), f32)] * 3 + [jnp.zeros((8, WIDE_FAST), f32)] * 2
         for w in range(cols):
             zc = (dot(a2[w, :, :C_MID], wc[...]) - mean_c) * scale_c
@@ -543,8 +544,8 @@
         ex.finish(tot, weight)
 
 
-def fifth_pass(n_clip, gs, gf, a2, zp, base, z2, mom2, mom3, tot4, inv, sgain, fgain, gain2, shift2, m, wc, wfc, x, weight,
-               dzp_out, q_out, tot, row, col, corner, wp_out, wc_out, wfc_out,
+def fifth_pass(n_clip, gs, gf, a2, zp, base, z2, mom2, mom3, tot4, inv, sgain, fends, mids, m, wc, wfc, x, weight,
+               dzp_out, q_out, tot, row, col, corner, w_out, wfc_out,
                dzc_keep, dzp_keep, dfc_keep, a_keep, sums, big, line, side, *refs):
     i = pl.program_id(0)
     high, cols, slab, _ = dzc_keep.shape
@@ -569,9 +570,9 @@
         scale_p = lax.rsqrt(mom2[1:2, MIX:] + eps_norm)
         mean_f = jnp.tile(mom3[0:1, C_IN:], (1, ALPHA))
         scale_f = jnp.tile(lax.rsqrt(mom3[1:2, C_IN:] + eps_norm), (1, ALPHA))
-        mult_c = sgain[:, :C_IN] * scale_c
-        mult_p = sgain[:, C_IN:] * scale_p
-        mult_f = jnp.tile(fgain[...], (1, ALPHA)) * scale_f
+        mult_c = sgain[:, 2 * C_MID : 2 * C_MID + C_IN] * scale_c
+        mult_p = sgain[:, 2 * C_MID + C_IN :] * scale_p
+        mult_f = jnp.tile(fends[0], (1, ALPHA)) * scale_f
         first_s = tot4[:, :C_IN] * inv_s
         second_c = tot4[:, C_IN : 2 * C_IN] * inv_s
         second_p = tot4[:, 2 * C_IN : 3 * C_IN] * inv_s
@@ -592,7 +593,7 @@
         da = dot_nt(dzc_keep[i].reshape(rows, C_IN), wc[...]).reshape(cols, slab, C_MID)
         df = dot_nt(dfc_keep[i].reshape(rows, WIDE_FAST), big[...]).reshape(cols, slab, 128)
         grads = jnp.concatenate([da, df], axis=2)
-        slope_back(grads, z2[...], mom2, gain2, shift2, m, q_out, sums)
+        slope_back(grads, z2[...], mom2, mids[2], mids[3], m, q_out, sums)
         keep_rims(ex, i, high, q_out, line, side)
 
     @pl.when(i == high)
@@ -608,14 +609,19 @@
 
     @pl.when(i >= high)
     def _():
-        wp_out[...] = dot_tn(
-            x[...].reshape(n * slab, C_MID), dzp_keep[...].reshape(n * slab, C_IN)
-        ).astype(bf16)
+        c = i - high
+        got = dot_tn(x[...].reshape(n * slab, C_MID), dzp_keep[...].reshape(n * slab, C_IN)).astype(bf16)
+        for b in range(C_IN // 256):
+            at = pl.multiple_of(b * C_JOIN + c * C_MID, C_MID)
+            w_out[pl.ds(at, C_MID), :] = got[:, b * 256 : (b + 1) * 256]
 
     @pl.when(i == pl.num_programs(0) - 1)
     def _():
         a = a_keep[...].reshape(n * slab, MIX)
-        wc_out[...] = dot_tn(a[:, :C_MID], dzc_keep[...].reshape(n * slab, C_IN)).astype(bf16)
+        got = dot_tn(a[:, :C_MID], dzc_keep[...].reshape(n * slab, C_IN)).astype(bf16)
+        for b in range(C_IN // 256):
+            at = 4 * C_JOIN + b * C_MID
+            w_out[at : at + C_MID, :] = got[:, b * 256 : (b + 1) * 256]
         wide = dot_tn(a[:, C_MID:], dfc_keep[...].reshape(n * slab, WIDE_FAST))
         wfc_out[...] = sum(
             wide[p * C_FMID : (p + 1) * C_FMID, p * C_FAST : (p + 1) * C_FAST] for p in range(ALPHA)
@@ -641,16 +647,21 @@
     mean = mom[0:1, :MIX]
     scale = lax.rsqrt(mom[1:2, :MIX] + eps_norm)
     share = jnp.concatenate([spread(inv[...], C_MID), 0.25 * inv[...]], axis=1)
-    return mean, scale, gain[...] * scale, tot[:, :MIX] * share, tot[:, MIX:] * share
-
-
-def sixth_pass(n_clip, q2_hbm, z2_hbm, z1_hbm, a1_hbm, qrow, qcol, qcorner, zrow, zcol, zcorner, mom1, mom2, tot5, inv,
-               gain1, shift1, gain2, m, wb, wfb, weight, q_out, tot, wb_out, wfb_out,
-               wide, q2, z2, z1, a1, q2_sem, z2_sem, z1_sem, a1_sem, sums, *refs):
+    return mean, scale, gain * scale, tot[:, :MIX] * share, tot[:, MIX:] * share
+
+
+def sixth_pass(n_clip, early_sizes, q2_hbm, z2_hbm, z1_hbm, a1_hbm, qrow, qcol, qcorner, zrow, zcol, zcorner, mom1, mom2, tot5, inv,
+               mids, m, wb, wfb, weight, dwfc, w_hbm, q_out, tot, wb_out, kept_out,
+               fast_sums, wide, q2, z2, z1, a1, q2_sem, z2_sem, z1_sem, a1_sem, sums, mine, land, *refs):
     i = pl.program_id(0)
     high, cols, slab, _ = z1.shape
     rows = cols * slab
-    ex = Exchange(n_clip, False, refs)
+    ex = Exchange(n_clip, False, refs[:8])
+    early = Reducer(n_clip, early_sizes, mine, land, None, refs[8:10] + (None, None))
+    end = early.stages - 1
+
+    def fetch_w():
+        return pltpu.make_async_copy(w_hbm, mine, a1_sem.at[1])
 
     moved = ((q2_hbm, q2, q2_sem), (z2_hbm, z2, z2_sem), (z1_hbm, z1, z1_sem))
 
@@ -663,6 +674,8 @@
 
     @pl.when(i == 0)
     def _():
+        fetch_w().start()
+        wb_out[9 * C_MID :, :] = jnp.zeros((wb_out.shape[0] - 9 * C_MID, 256), bf16)
         for h in range(high):
             fetch(0, h).start()
             fetch(1, h).start()
@@ -670,7 +683,7 @@
             fetch(2, h).start()
         fetch_a1().start()
         ex.signal()
-        mean, scale, mult, first, second = norm_terms(mom2, gain2, tot5, inv)
+        mean, scale, mult, first, second = norm_terms(mom2, mids[2], tot5, inv)
         mask = spread(m[...], MIX)
 
         def grad(q, z):
@@ -682,6 +695,9 @@
         wide[far * (1 - ex.ha), 1 : 1 + cols] = grad(qrow[...], zrow[...])
         wide[1 : 1 + high, far * (1 - ex.wa)] = grad(qcol[...], zcol[...])
         wide[far * (1 - ex.ha), far * (1 - ex.wa)] = grad(qcorner[...], zcorner[...])
+        fetch_w().wait()
+        ex.meet()
+        early.send(0)
 
         def fill(h, carry):
             fetch(0, h).wait()
@@ -702,12 +718,13 @@
                     slow = slow + dot_nt(v[:, :C_MID], wb[a, c])
                     fast = fast + dot_nt(v[:, C_MID:], wfb[3 * a + c])
             grads = jnp.concatenate([slow, fast], axis=1).reshape(cols, slab, MIX)
-            slope_back(grads, z1[h], mom1, gain1, shift1, m, q_out.at[h], sums)
+            slope_back(grads, z1[h], mom1, mids[0], mids[1], m, q_out.at[h], sums)
             return carry
 
-        lax.fori_loop(0, high, space, 0)
+        lax.fori_loop(0, 3, space, 0)
+        early.gather(0)
+        lax.fori_loop(3, high, space, 0)
         ex.part[...] = sums[...]
-        ex.meet()
         ex.send_near()
         fetch_a1().wait()
 
@@ -720,76 +737,284 @@
         tap = i - 1
         v = a1[pl.ds(tap // 3, high), pl.ds(lax.rem(tap, 3), cols)].reshape(high * rows, MIX)
         d = wide[1 : 1 + high, 1 : 1 + cols].reshape(high * rows, MIX)
-        wb_out[...] = dot_tn(v[:, :C_MID], d[:, :C_MID]).astype(bf16)
+        wb_out[pl.ds(pl.multiple_of(tap * C_MID, C_MID), C_MID), :] = dot_tn(v[:, :C_MID], d[:, :C_MID]).astype(bf16)
         both = dot_tn(v[:, C_MID:], d[:, C_MID:])
-        wfb_out[tap] = sum(
+        fast_sums[tap] = sum(
             both[p * C_FMID : (p + 1) * C_FMID, p * C_FMID : (p + 1) * C_FMID] for p in range(ALPHA)
         )
 
+    for k, step in ((1, 1), (2, 5), (3, 7)):
+
+        @pl.when(i == step)
+        def _():
+            early.gather(k)
+
     @pl.when(i == 9)
     def _():
         ex.finish(tot, weight)
-
-
-def first_back(clips, q1, z1, mom1, tot, inv, gain1, m, perm, dzp, gf, wl, wa, wp, wfa, sx, fx, da_out, dl_out, df_out,
-               taps, ends):
-    h = pl.program_id(0)
+        for k in range(4, end + 1):
+            early.gather(k)
+        early.export(kept_out)
+        for q in range(10):
+            r, c, width = small_place(q)
+            wb_out[r : r + C_FMID, c : c + width] = (fast_sums[q] if q < 9 else dwfc[...]).astype(bf16)
+
+
+def bit_of(axis, power):
+    return lax.rem(lax.axis_index(axis) // (1 << power), 2)
+
+
+def partner_of(axis, power):
+    where = {name: lax.axis_index(name) for name in ("clip", "ha", "wa")}
+    where[axis] = where[axis] + (1 - 2 * bit_of(axis, power)) * (1 << power)
+    return (where["clip"], where["ha"], where["wa"])
+
+
+def stage_orders(n_clip, sets):
+    rest = [("wa", 0)] + [("clip", b) for b in range(n_clip.bit_length() - 1)]
+    turn, last = rest[:3], rest[3:]
+    return [[("ha", 0)] + turn[s % len(turn) :] + turn[: s % len(turn)] + last for s in range(sets)]
+
+
+def chunk_of(rows):
+    return max(k for k in range(16, min(rows, 256) + 1, 16) if rows % k == 0)
+
+
+class Reducer:
+    def __init__(self, n_clip, sizes, mine, land, done, sems):
+        self.mine, self.land, self.done = mine, land, done
+        self.rs_sent, self.rs_came, self.ag_sent, self.ag_came = sems
+        self.sets = range(len(sizes))
+        self.orders = stage_orders(n_clip, len(sizes))
+        self.stages = len(self.orders[0])
+        self.plan, self.starts, self.kept = Reducer.layout(n_clip, sizes)
+
+    @staticmethod
+    def layout(n_clip, sizes):
+        stages = len(stage_orders(n_clip, 1)[0])
+        plan, starts, kept = [], [], []
+        start = land = 0
+        for size in sizes:
+            starts.append(start)
+            start += size
+            row = []
+            for _ in range(stages):
+                halve = size % 32 == 0
+                size = size // 2 if halve else size
+                row.append((halve, size, land))
+                land += size
+            plan.append(row)
+            kept.append(size)
+        return plan, starts, kept
+
+    @staticmethod
+    def scratch(n_clip, sizes):
+        plan = Reducer.layout(n_clip, sizes)[0]
+        last = plan[-1][-1]
+        return pltpu.VMEM((last[1] + last[2], 256), bf16)
+
+    @staticmethod
+    def sems(n_clip, sizes, count=4):
+        stages = len(stage_orders(n_clip, 1)[0])
+        return [pltpu.SemaphoreType.DMA((len(sizes), stages)) for _ in range(count)]
+
+    def low(self, s, k):
+        low = jnp.int32(self.starts[s])
+        for j in range(k):
+            halve, count, _ = self.plan[s][j]
+            if halve:
+                low = low + bit_of(*self.orders[s][j]) * count
+        return low
+
+    @staticmethod
+    def rows(ref, begin, count):
+        return ref.at[pl.ds(pl.multiple_of(begin, 16), count)]
+
+    def scatter_copy(self, s, k):
+        halve, count, land = self.plan[s][k]
+        axis, power = self.orders[s][k]
+        begin = self.low(s, k)
+        if halve:
+            begin = begin + (1 - bit_of(axis, power)) * count
+        return pltpu.make_async_remote_copy(
+            src_ref=self.rows(self.mine, begin, count), dst_ref=self.rows(self.land, land, count),
+            send_sem=self.rs_sent.at[s, k], recv_sem=self.rs_came.at[s, k],
+            device_id=partner_of(axis, power), device_id_type=MESH,
+        )
+
+    def send(self, k):
+        for s in self.sets:
+            self.scatter_copy(s, k).start()
+
+    def gather(self, k):
+        for s in self.sets:
+            halve, count, land = self.plan[s][k]
+            copy = self.scatter_copy(s, k)
+            copy.wait_recv()
+            copy.wait_send()
+            begin = self.low(s, k + 1)
+            step = chunk_of(count)
+
+            def add(i, carry):
+                own = pl.ds(pl.multiple_of(begin + i * step, 16), step)
+                came = pl.ds(pl.multiple_of(land + i * step, 16), step)
+                self.mine[own, :] = (self.mine[own, :].astype(f32) + self.land[came, :].astype(f32)).astype(bf16)
+                return carry
+
+            lax.fori_loop(0, count // step, add, 0)
+            if k + 1 < self.stages:
+                self.scatter_copy(s, k + 1).start()
+
+    def export(self, out):
+        at = 0
+        for s in self.sets:
+            count = self.kept[s]
+            out[at : at + count] = self.mine[pl.ds(pl.multiple_of(self.low(s, self.stages), 16), count), :]
+            at += count
+
+    def load(self, kept):
+        at = 0
+        for s in self.sets:
+            count = self.kept[s]
+            self.done[pl.ds(pl.multiple_of(self.low(s, self.stages), 16), count), :] = kept[at : at + count]
+            at += count
+
+    def keep(self):
+        for s in self.sets:
+            own = pl.ds(pl.multiple_of(self.low(s, self.stages), 16), self.kept[s])
+            self.done[own, :] = self.mine[own, :]
+
+    def regain(self):
+        self.keep()
+        self.spread(self.stages - 1)
+
+    def gather_copy(self, s, k, other):
+        halve, count, _ = self.plan[s][k]
+        axis, power = self.orders[s][k]
+        bit = bit_of(axis, power)
+        begin = self.low(s, k) + ((1 - bit) if other else bit) * count
+        return pltpu.make_async_remote_copy(
+            src_ref=self.rows(self.done, begin, count), dst_ref=self.rows(self.done, begin, count),
+            send_sem=self.ag_sent.at[s, k], recv_sem=self.ag_came.at[s, k],
+            device_id=partner_of(axis, power), device_id_type=MESH,
+        )
+
+    def spread(self, k):
+        for s in self.sets:
+            if self.plan[s][k][0]:
+                self.gather_copy(s, k, False).start()
+
+    def take(self, k):
+        for s in self.sets:
+            if self.plan[s][k][0]:
+                self.gather_copy(s, k, True).wait_recv()
+                self.gather_copy(s, k, False).wait_send()
+            if k > 0 and self.plan[s][k - 1][0]:
+                self.gather_copy(s, k - 1, False).start()
+
+
+SPACE_STEPS = (2, 5, 7, 8, 10)
+FIRST_STEPS = (5, 7, 9, 12, 14)
+HALF_STEPS = (10, 11, 13, 14, 15)
+SPACE_BACK = (11, 13, 14, 15, 16, 17)
+HALF_BACK = (15, 16, 17, 18, 18, 18)
+LATE_STEPS = (14, 16, 18)
+
+
+def seventh_pass(clips, n_clip, early_sizes, space_sizes, half_sizes, late_sizes, q1, z1, dzp, gf, x, f, kept, space_hbm, mom1, tot6, inv,
+                 mids, m, perm, wl, wa, wp, wfa, sx, fx, out1, out_b, out_h, out_a,
+                 done1, done_b, done_h, done_a, da, dl, df, taps, ends, mine_b, land_b, mine_h, land_h, mine_a, land_a, load_sem, *sems):
+    i = pl.program_id(0)
     cols, slab, _ = q1.shape
+    high = da.shape[0]
     rows = cols * slab
-
-    @pl.when(h == 0)
-    def _():
+    every = high * rows
+    steps = C_JOIN // C_MID
+    late = high + steps
+    sems = iter(sems)
+    first = Reducer(n_clip, early_sizes, None, None, done1, (None, None, next(sems), next(sems)))
+    space = Reducer(n_clip, space_sizes, mine_b, land_b, done_b, [next(sems) for _ in range(4)])
+    half = Reducer(n_clip, half_sizes, mine_h, land_h, done_h, [next(sems) for _ in range(4)])
+    last = Reducer(n_clip, late_sizes, mine_a, land_a, done_a, [next(sems) for _ in range(4)])
+    end = last.stages - 1
+
+    @pl.when(i == 0)
+    def _():
+        load = pltpu.make_async_copy(space_hbm, mine_b, load_sem.at[0])
+        load.start()
+        greet_signal(n_clip)
         frames_matrix(wfa, taps, ends)
-
-    mean, scale, mult, first, second = norm_terms(mom1, gain1, tot, inv)
-    zhat = (z1[...] - mean) * scale
-    dz = mult * (q1[...] - spread(m[...], MIX) * (first + zhat * second))
-    up, down = sooner(dz, clips), later(dz, clips)
-    for k, v in enumerate((up, dz, down)):
-        da_out[:, :, k * C_MID : (k + 1) * C_MID] = v[:, :, :C_MID].astype(bf16)
-        df_out[:, :, k * 128 : (k + 1) * 128] = v[:, :, C_MID:].astype(bf16)
-    dj = dot_nt(dzp[...].reshape(rows, C_IN), wp[...])
-    for k in range(3):
-        dj = dj + dot_nt(da_out[:, :, k * C_MID : (k + 1) * C_MID].reshape(rows, C_MID), wa[k])
-    mask = spread(m[...], C_IN)
-    dj = dj.reshape(cols, slab, C_JOIN)
-    for w in range(cols):
-        sx[:, w] = (dj[w, :, :C_IN] * mask).astype(bf16).reshape(slab // clips, clips, C_IN)
-    dlat = dj[:, :, C_IN:].astype(bf16).astype(f32)
-    dl_out[:, :, :C_LAT] = dlat.astype(bf16)
-    dl_out[:, :, C_LAT:] = sooner(dlat, clips).astype(bf16)
-    df = df_out[...].reshape(rows, 3 * 128)
-    dl = dl_out[...].reshape(rows, 2 * C_LAT)
-    total = gf[...].reshape(rows, WIDE_FAST).astype(f32) + dot(df[:, 128:256], taps[...])
-    head = dot_nt(dl[:, :C_LAT], wl[2:5].reshape(3 * C_FAST, C_LAT))
-    tail = dot_nt(dl[:, C_LAT:], wl[0:2].reshape(2 * C_FAST, C_LAT))
-    blocks = [total[:, p * C_FAST : (p + 1) * C_FAST] for p in range(ALPHA)]
-    for p in range(3):
-        blocks[p] = blocks[p] + head[:, p * C_FAST : (p + 1) * C_FAST]
-    for p in range(2):
-        blocks[2 + p] = blocks[2 + p] + tail[:, p * C_FAST : (p + 1) * C_FAST]
-    blocks[3] = blocks[3] + dot(df[:, :128], ends[0])
-    blocks[0] = blocks[0] + dot(df[:, 256:], ends[1])
-    blocks = [v.astype(bf16) for v in blocks]
-    for w in range(cols):
-        stacked = jnp.concatenate([v[w * slab : (w + 1) * slab] for v in blocks], axis=0)
-        fx[:, w] = dot_tn(perm[...], stacked).astype(bf16).reshape(clips, slab, C_FAST)
-
-
-def first_weights(x, f, da, dl, df, dwfc, dwfb, wa_out, wl_out, small_out):
-    i = pl.program_id(0)
-    n, slab, _ = x.shape
-    rows = n * slab
-    for k in range(3):
-        wa_out[k] = dot_tn(x[...].reshape(rows, C_MID), da[:, :, k * C_MID : (k + 1) * C_MID].reshape(rows, C_MID)).astype(bf16)
-
-    @pl.when(i == pl.num_programs(0) - 1)
-    def _():
-        fast = f[...].reshape(rows, WIDE_FAST)
-        d = dl[...].reshape(rows, 2 * C_LAT)
-        wl_out[2:5] = dot_tn(fast[:, : 3 * C_FAST], d[:, :C_LAT]).reshape(3, C_FAST, C_LAT).astype(bf16)
-        wl_out[0:2] = dot_tn(fast[:, 2 * C_FAST :], d[:, C_LAT:]).reshape(2, C_FAST, C_LAT).astype(bf16)
-        g = df[...].reshape(rows, 3 * 128)
+        first.load(kept)
+        greet_wait(n_clip)
+        first.spread(end)
+        load.wait()
+        space.send(0)
+
+    plan = {}
+
+    def book(ops, steps):
+        for j, op in enumerate(ops):
+            plan.setdefault(steps[j * len(steps) // len(ops)], []).append(op)
+
+    book([functools.partial(space.gather, k) for k in range(end + 1)], SPACE_STEPS)
+    book([functools.partial(first.take, k) for k in range(end, -1, -1)], FIRST_STEPS)
+    book([functools.partial(half.gather, k) for k in range(end + 1)], HALF_STEPS)
+    book([space.regain] + [functools.partial(space.take, k) for k in range(end, -1, -1)], SPACE_BACK)
+    book([half.regain] + [functools.partial(half.take, k) for k in range(end, -1, -1)], HALF_BACK)
+    book([functools.partial(last.gather, k) for k in range(3)], LATE_STEPS)
+    final = pl.num_programs(0) - 1
+    for step, ops in sorted(plan.items()):
+
+        @pl.when((i == step) & (i < final))
+        def _():
+            for op in ops:
+                op()
+
+    @pl.when(i < high)
+    def _():
+        mean, scale, mult, one, two = norm_terms(mom1, mids[0], tot6, inv)
+        zhat = (z1[...] - mean) * scale
+        dz = mult * (q1[...] - spread(m[...], MIX) * (one + zhat * two))
+        up, down = sooner(dz, clips), later(dz, clips)
+        for k, v in enumerate((up, dz, down)):
+            da[i, :, :, k * C_MID : (k + 1) * C_MID] = v[:, :, :C_MID].astype(bf16)
+            df[i, :, :, k * 128 : (k + 1) * 128] = v[:, :, C_MID:].astype(bf16)
+        dlat = dot_nt(dzp[...].reshape(rows, C_IN), wp[C_IN:])
+        for k in range(3):
+            dlat = dlat + dot_nt(da[i, :, :, k * C_MID : (k + 1) * C_MID].reshape(rows, C_MID), wa[k, C_IN:])
+        dlat = dlat.astype(bf16).astype(f32).reshape(cols, slab, C_LAT)
+        dl[i, :, :, :C_LAT] = dlat.astype(bf16)
+        dl[i, :, :, C_LAT:] = sooner(dlat, clips).astype(bf16)
+
+    @pl.when((i >= high) & (i < late))
+    def _():
+        c = i - high
+        got = dot_tn(x[...].reshape(every, C_MID), da[...].reshape(every, 3 * C_MID)).astype(bf16)
+
+        @pl.when(c < 2)
+        def _():
+            for k in range(3):
+                mine_h[pl.ds(pl.multiple_of((2 * k + c) * C_MID, C_MID), C_MID), :] = got[:, k * C_MID : (k + 1) * C_MID]
+
+        @pl.when(c >= 2)
+        def _():
+            for k in range(3):
+                at = pl.multiple_of((3 * k + c - 2) * C_MID, C_MID)
+                mine_a[pl.ds(at, C_MID), :] = got[:, k * C_MID : (k + 1) * C_MID]
+
+        @pl.when(c == 1)
+        def _():
+            half.send(0)
+
+    @pl.when(i == late - 1)
+    def _():
+        fast = f[...].reshape(every, WIDE_FAST)
+        d = dl[...].reshape(every, 2 * C_LAT)
+        at = 9 * C_MID
+        mine_a[at + 2 * C_FAST : at + 5 * C_FAST, :] = dot_tn(fast[:, : 3 * C_FAST], d[:, :C_LAT]).astype(bf16)
+        mine_a[at : at + 2 * C_FAST, :] = dot_tn(fast[:, 2 * C_FAST :], d[:, C_LAT:]).astype(bf16)
+        at += 5 * C_FAST
+        g = df[...].reshape(every, 3 * 128)
         mid = dot_tn(g[:, 128:256], fast)
         sums = [jnp.zeros((C_FMID, C_FAST), f32) for _ in range(3)]
         for p in range(ALPHA):
@@ -797,208 +1022,198 @@
                 sums[s - p + 1] += mid[p * C_FMID : (p + 1) * C_FMID, s * C_FAST : (s + 1) * C_FAST]
         sums[0] += dot_tn(g[:, :128], fast[:, 3 * C_FAST :])[:C_FMID]
         sums[2] += dot_tn(g[:, 256:], fast[:, :C_FAST])[3 * C_FMID :]
-        small_out[...] = jnp.zeros_like(small_out)
+        mine_a[at:, :] = jnp.zeros((mine_a.shape[0] - at, 256), bf16)
+        for q in range(3):
+            mine_a[at + q * C_FMID : at + (q + 1) * C_FMID, :C_FAST] = sums[q].astype(bf16)
+        last.send(0)
+
+    @pl.when(i >= late)
+    def _():
+        h = i - late
+        dj = dot_nt(dzp[...].reshape(rows, C_IN), wp[:C_IN])
         for k in range(3):
-            small_out[k * C_FMID : (k + 1) * C_FMID] = sums[k].astype(bf16)
-        small_out[3 * C_FMID : 4 * C_FMID] = dwfc[...].astype(bf16)
-        for k in range(9):
-            at = (4 + k) * C_FMID
-            small_out[at : at + C_FMID, :C_FMID] = dwfb[k].astype(bf16)
-
-
-UNIT = 512
-
-
-def bit_of(axis, power):
-    return lax.rem(lax.axis_index(axis) // (1 << power), 2)
-
-
-def partner_of(axis, power, bit):
-    where = {name: lax.axis_index(name) for name in ("clip", "ha", "wa")}
-    where[axis] = where[axis] + (1 - 2 * bit) * (1 << power)
-    return (where["clip"], where["ha"], where["wa"])
-
-
-def stage_orders(n_clip, sets):
-    rest = [("wa", 0)] + [("clip", b) for b in range(n_clip.bit_length() - 1)]
-    turn, last = rest[:3], rest[3:]
-    return [[("ha", 0)] + turn[s % len(turn) :] + turn[: s % len(turn)] + last for s in range(sets)]
-
-
-def chunk_of(rows):
-    best = 16
-    for k in range(16, min(rows, 256) + 1, 16):
-        if rows % k == 0:
-            best = k
-    return best
-
-
-def land_plan(n_clip, sizes):
-    stages = len(stage_orders(n_clip, 1)[0])
-    starts, total = [], 0
-    for size in sizes:
-        starts.append(total)
-        for _ in range(stages):
-            size = size // 2 if size % 32 == 0 else size
-            total += size
-    return starts, total
-
-
-def reduce_sets(n_clip, starts, sizes, mine, land, done, rs_send, rs_recv, ag_send, ag_recv):
-    orders = stage_orders(n_clip, len(starts))
-    stages = len(orders[0])
-    low = [jnp.int32(v) for v in starts]
-    size = list(sizes)
-    at = land_plan(n_clip, sizes)[0]
-    trail = [[] for _ in starts]
-    sent = []
-
-    def rows(ref, begin, count):
-        return ref.at[pl.ds(pl.multiple_of(begin, 16), count)]
-
-    def send(s, k):
-        axis, power = orders[s][k]
-        bit = bit_of(axis, power)
-        halve = size[s] % 32 == 0
-        count = size[s] // 2 if halve else size[s]
-        begin = low[s] + (1 - bit) * count if halve else low[s]
-        copy = pltpu.make_async_remote_copy(
-            src_ref=rows(mine, begin, count), dst_ref=rows(land, at[s], count),
-            send_sem=rs_send.at[s, k], recv_sem=rs_recv.at[s, k],
-            device_id=partner_of(axis, power, bit), device_id_type=MESH,
-        )
-        copy.start()
-        trail[s].append((copy, low[s], count, halve, axis, power, bit, at[s]))
-        if halve:
-            low[s] = low[s] + bit * count
-            size[s] = count
-        at[s] += count
-
-    def gather(s, k):
-        copy, _, count, halve, axis, power, bit, begin = trail[s][k]
-        copy.wait_recv()
-        if not halve:
-            copy.wait_send()
-        step = chunk_of(count)
-
-        def add(i, carry):
-            own = pl.ds(pl.multiple_of(low[s] + i * step, 16), step)
-            came = pl.ds(pl.multiple_of(begin + i * step, 16), step)
-            mine[own, :] = (mine[own, :].astype(f32) + land[came, :].astype(f32)).astype(bf16)
-            return carry
-
-        lax.fori_loop(0, count // step, add, 0)
-        if halve:
-            sent.append(copy)
-
-    for s in range(len(starts)):
-        send(s, 0)
-    for k in range(stages):
-        for s in range(len(starts)):
-            gather(s, k)
-            if k + 1 < stages:
-                send(s, k + 1)
-    for copy in sent:
-        copy.wait_send()
-
-    for s in range(len(starts)):
-        step = chunk_of(size[s])
-
-        def keep(i, carry):
-            own = pl.ds(pl.multiple_of(low[s] + i * step, 16), step)
-            done[own, :] = mine[own, :]
-            return carry
-
-        lax.fori_loop(0, size[s] // step, keep, 0)
-
-    copies = []
-    pending = [None] * len(starts)
-
-    def spread_out(s, k):
-        _, before, count, halve, axis, power, bit, _ = trail[s][k]
-        if not halve:
-            return
-        copy = pltpu.make_async_remote_copy(
-            src_ref=rows(done, low[s], count), dst_ref=rows(done, low[s], count),
-            send_sem=ag_send.at[s, k], recv_sem=ag_recv.at[s, k],
-            device_id=partner_of(axis, power, bit), device_id_type=MESH,
-        )
-        copy.start()
-        other = before + (1 - bit) * count
-        pending[s] = pltpu.make_async_remote_copy(
-            src_ref=rows(done, other, count), dst_ref=rows(done, other, count),
-            send_sem=ag_send.at[s, k], recv_sem=ag_recv.at[s, k],
-            device_id=partner_of(axis, power, bit), device_id_type=MESH,
-        )
-        low[s] = before
-        copies.append(copy)
-
-    for s in range(len(starts)):
-        spread_out(s, stages - 1)
-    for k in range(stages - 1, -1, -1):
-        for s in range(len(starts)):
-            if pending[s] is not None:
-                pending[s].wait_recv()
-                pending[s] = None
-            if k > 0:
-                spread_out(s, k - 1)
-    for copy in copies:
-        copy.wait_send()
-
-
-def greet(n_clip):
+            dj = dj + dot_nt(da[h, :, :, k * C_MID : (k + 1) * C_MID].reshape(rows, C_MID), wa[k, :C_IN])
+        mask = spread(m[...], C_IN)
+        dj = dj.reshape(cols, slab, C_IN)
+        for w in range(cols):
+            sx[:, w] = (dj[w] * mask).astype(bf16).reshape(slab // clips, clips, C_IN)
+        g = df[h].reshape(rows, 3 * 128)
+        d = dl[h].reshape(rows, 2 * C_LAT)
+        total = gf[...].reshape(rows, WIDE_FAST) + dot(g[:, 128:256], taps[...])
+        head = dot_nt(d[:, :C_LAT], wl[2:5].reshape(3 * C_FAST, C_LAT))
+        tail = dot_nt(d[:, C_LAT:], wl[0:2].reshape(2 * C_FAST, C_LAT))
+        blocks = [total[:, p * C_FAST : (p + 1) * C_FAST] for p in range(ALPHA)]
+        for p in range(3):
+            blocks[p] = blocks[p] + head[:, p * C_FAST : (p + 1) * C_FAST]
+        for p in range(2):
+            blocks[2 + p] = blocks[2 + p] + tail[:, p * C_FAST : (p + 1) * C_FAST]
+        blocks[3] = blocks[3] + dot(g[:, :128], ends[0])
+        blocks[0] = blocks[0] + dot(g[:, 256:], ends[1])
+        blocks = [v.astype(bf16) for v in blocks]
+        for w in range(cols):
+            stacked = jnp.concatenate([v[w * slab : (w + 1) * slab] for v in blocks], axis=0)
+            fx[:, w] = dot_tn(perm[...], stacked).astype(bf16).reshape(clips, slab, C_FAST)
+
+    @pl.when(i == final)
+    def _():
+        for step, ops in sorted(plan.items()):
+            if step >= 2 * high + steps - 1:
+                for op in ops:
+                    op()
+        for k in range(3, end + 1):
+            last.gather(k)
+        last.regain()
+        for k in range(end, -1, -1):
+            last.take(k)
+        saves = [
+            pltpu.make_async_copy(a, b, load_sem.at[k])
+            for k, (a, b) in enumerate(((done1, out1), (done_b, out_b), (done_h, out_h), (done_a, out_a)))
+        ]
+        for save in saves:
+            save.start()
+        for save in saves:
+            save.wait()
+
+
+def small_place(q):
+    return 9 * C_MID + (q % 5) * C_FMID, (q // 5) * 128, C_FMID if q < 9 else C_FAST
+
+
+def greet_signal(n_clip):
     barrier = pltpu.get_barrier_semaphore()
-    stages = stage_orders(n_clip, 1)[0]
-    for axis, power in stages:
-        bit = bit_of(axis, power)
-        pl.semaphore_signal(barrier, inc=1, device_id=partner_of(axis, power, bit), device_id_type=MESH)
-    pl.semaphore_wait(barrier, len(stages))
-
-
-def weight_pieces(dws_rows):
-    pieces = []
-    row = 0
-    for which, count in ((0, C_JOIN), (1, C_MID)):
+    for axis, power in stage_orders(n_clip, 1)[0]:
+        pl.semaphore_signal(barrier, inc=1, device_id=partner_of(axis, power), device_id_type=MESH)
+
+
+def greet_wait(n_clip):
+    pl.semaphore_wait(pltpu.get_barrier_semaphore(), len(stage_orders(n_clip, 1)[0]))
+
+
+def finish_outputs(so, fo, sx, fx, done1, done_b, done_h, done_a, tot4, tot5, tot6, so_out, fo_out, sx_out, fx_out,
+                   wp_hbm, wc_hbm, wb_hbm, wa_hbm, wl_hbm, wfa_out, wfc_out, wfb_out, sgain_out, sshift_out, fgain_out,
+                   fshift_out, wp, wc, wb, wa, wl, sem):
+    i = pl.program_id(0)
+    moves = ((wp, wp_hbm), (wc, wc_hbm), (wb, wb_hbm), (wa, wa_hbm), (wl, wl_hbm))
+
+    def move(k):
+        return pltpu.make_async_copy(moves[k][0], moves[k][1], sem.at[k])
+
+    @pl.when(i == 0)
+    def _():
         for b in range(C_IN // 256):
-            pieces.append((row, count, which, (slice(None), slice(b * 256, (b + 1) * 256))))
-            row += count
-    for i in range(3):
-        for j in range(3):
-            pieces.append((row, C_MID, 2, (i, j)))
-            row += C_MID
-    for k in range(3):
-        pieces.append((row, C_JOIN, 3, (k,)))
-        row += C_JOIN
-    for k in range(5):
-        pieces.append((row, C_FAST, 4, (k,)))
-        row += C_FAST
-    return pieces, row
-
-
-def reduce_weights(n_clip, starts, sizes, dwp, dwc, dwb, dwa, dwl, dws, done,
-                   mine, land, rs_send, rs_recv, ag_send, ag_recv):
-    sources = (dwp, dwc, dwb, dwa, dwl)
-    pieces, row = weight_pieces(dws.shape[0])
-    for begin, count, which, at in pieces:
-        mine[begin : begin + count, :] = sources[which].at[at][...]
-    half = dws.shape[0] // 2
-    mine[row : row + half, :128] = dws[:half]
-    mine[row : row + half, 128:] = dws[half:]
-    end = row + half
-    if end < mine.shape[0]:
-        mine[end:, :] = jnp.zeros((mine.shape[0] - end, 256), bf16)
-    greet(n_clip)
-    reduce_sets(n_clip, starts, sizes, mine, land, done, rs_send, rs_recv, ag_send, ag_recv)
-
-
-def unpack_weights(done, wp_out, wc_out, wb_out, wa_out, wl_out, ws_out):
-    targets = (wp_out, wc_out, wb_out, wa_out, wl_out)
-    pieces, row = weight_pieces(ws_out.shape[0])
-    for begin, count, which, at in pieces:
-        targets[which].at[at][...] = done[begin : begin + count, :].astype(f32)
-    half = ws_out.shape[0] // 2
-    ws_out[:half] = done[row : row + half, :128].astype(f32)
-    ws_out[half:] = done[row : row + half, 128:].astype(f32)
+            wp[:, b * 256 : (b + 1) * 256] = done1[b * C_JOIN : (b + 1) * C_JOIN, :].astype(f32)
+        move(0).start()
+        for b in range(C_IN // 256):
+            at = 4 * C_JOIN + b * C_MID
+            wc[:, b * 256 : (b + 1) * 256] = done1[at : at + C_MID, :].astype(f32)
+        move(1).start()
+
+    @pl.when(i == 1)
+    def _():
+        for t in range(9):
+            wb[t // 3, t % 3] = done_b[t * C_MID : (t + 1) * C_MID, :].astype(f32)
+        move(2).start()
+
+    @pl.when(i == 2)
+    def _():
+        for k in range(3):
+            wa[k, : 2 * C_MID] = done_h[2 * k * C_MID : 2 * (k + 1) * C_MID, :].astype(f32)
+            wa[k, 2 * C_MID :] = done_a[3 * k * C_MID : 3 * (k + 1) * C_MID, :].astype(f32)
+        move(3).start()
+        at = 9 * C_MID
+        for k in range(5):
+            wl[k] = done_a[at + k * C_FAST : at + (k + 1) * C_FAST, :].astype(f32)
+        move(4).start()
+
+    @pl.when(i == 3)
+    def _():
+        at = 9 * C_MID + 5 * C_FAST
+        for q in range(3):
+            wfa_out[q] = done_a[at + q * C_FMID : at + (q + 1) * C_FMID, :C_FAST].astype(f32)
+        for q in range(10):
+            r, c, width = small_place(q)
+            piece = done_b[r : r + C_FMID, c : c + width].astype(f32)
+            if q < 9:
+                wfb_out[q] = piece
+            else:
+                wfc_out[...] = piece
+        lane = lax.broadcasted_iota(jnp.int32, (1, 128), 1)
+        for k, slow, fast in ((0, sshift_out, fshift_out), (1, sgain_out, fgain_out)):
+            at = k * MIX
+            row = 0
+            for source, begin, width in (
+                (tot6, at, C_MID), (tot5, at, C_MID), (tot4, k * C_IN, C_IN), (tot4, 2 * k * C_IN, C_IN)
+            ):
+                for c in range(begin, begin + width, 128):
+                    slow[row : row + 1] = source[:, c : c + 128]
+                    row += 1
+            c = pltpu.roll(tot4[:, 3 * C_IN + k * C_FAST : 3 * C_IN + (k + 1) * C_FAST], 2 * C_FMID, 1)
+            a, b = tot6[:, at + C_MID : at + MIX], tot5[:, at + C_MID : at + MIX]
+            fast[:, :128] = jnp.where(lane < C_FMID, a, jnp.where(lane < 2 * C_FMID, b, c))
+            fast[:, 128:] = c[:, : 2 * C_FMID]
+
+    so_out[...] = so[...]
+    fo_out[...] = fo[...]
+    sx_out[...] = sx[...]
+    fx_out[...] = fx[...]
+
+    @pl.when(i == pl.num_programs(0) - 1)
+    def _():
+        for k in range(5):
+            move(k).wait()
+
+
+def prepare(clips, n_clip, counts, sgain_rows, sshift_rows, fgain, fshift, wb, m, perm, weight, inv, mids, last, wide,
+            sgain, sshift):
+    for k in range(sgain_rows.shape[0]):
+        sgain[:, k * 128 : (k + 1) * 128] = sgain_rows[k : k + 1]
+        sshift[:, k * 128 : (k + 1) * 128] = sshift_rows[k : k + 1]
+    slab = m.shape[0]
+    frames = slab // clips
+    me = lax.axis_index("clip") * clips
+    shift = clips.bit_length() - 1
+
+    def real(shape):
+        r = lax.broadcasted_iota(jnp.int32, shape, 0)
+        own = jnp.zeros(shape, jnp.int32)
+        for c in range(clips):
+            own = jnp.where((r & (clips - 1)) == c, counts[me + c], own)
+        return r, (r >> shift) < own
+
+    m[...] = real(m.shape)[1].astype(f32)
+    width = perm.shape[1]
+    r, there = real((slab, width))
+    col = lax.broadcasted_iota(jnp.int32, (slab, width), 1)
+    for p in range(ALPHA):
+        want = (r & (clips - 1)) * (ALPHA * frames) + ALPHA * (r >> shift) + p
+        perm[p * slab : (p + 1) * slab] = ((want == col) & there).astype(f32).astype(bf16)
+    groups = []
+    for g in range(n_clip):
+        part = counts[g * clips]
+        for c in range(1, clips):
+            part = part + counts[g * clips + c]
+        groups.append(part)
+    total = groups[0]
+    for part in groups[1:]:
+        total = total + part
+    whole_count = jnp.full((1, 128), total, jnp.int32).astype(f32)
+    inv[...] = 1.0 / (whole_count * (H * W))
+    for g in range(n_clip):
+        weight[g] = jnp.full((1, 128), groups[g], jnp.int32).astype(f32) / whole_count
+    lane = lax.broadcasted_iota(jnp.int32, (1, 128), 1)
+    for k in range(2):
+        for j, (slow, fast) in enumerate(((sgain, fgain), (sshift, fshift))):
+            mine = (lane >= k * C_FMID) & (lane < (k + 1) * C_FMID)
+            mids[2 * k + j, :, :C_MID] = slow[:, k * C_MID : (k + 1) * C_MID]
+            mids[2 * k + j, :, C_MID:] = phase_sum(jnp.where(mine, fast[:, :128], 0.0))
+    for j, fast in enumerate((fgain, fshift)):
+        last[j] = fast[:, 2 * C_FMID :]
+    for t in range(9):
+        w = wb[t]
+        for p in range(ALPHA):
+            parts = [jnp.zeros((C_FMID, C_FMID), bf16)] * ALPHA
+            parts[p] = w
+            wide[t, p * C_FMID : (p + 1) * C_FMID] = jnp.concatenate(parts, axis=1)
 
 
 def vmem_spec():
@@ -1007,39 +1222,6 @@
 
 def shaped(shape, kind):
     return jax.ShapeDtypeStruct(shape, kind)
-
-
-def run_reduce(ident, n_clip, arrays):
-    total = sum(v.size for v in arrays) // 256
-    units = -(-total // UNIT)
-    share = [-(-units // 3), -(-(units - units // 3) // 2), units // 3]
-    share[1] = units - share[0] - share[2]
-    sizes = [v * UNIT for v in share]
-    starts = [0, sizes[0], sizes[0] + sizes[1]]
-    rows = units * UNIT
-    land_rows = land_plan(n_clip, sizes)[1]
-    stages = len(stage_orders(n_clip, 1)[0])
-    sems = [pltpu.SemaphoreType.DMA((3, stages))] * 4
-    vm = vmem_spec()
-    done = pl.pallas_call(
-        functools.partial(reduce_weights, n_clip, starts, sizes),
-        in_specs=[vm] * len(arrays),
-        out_specs=vm,
-        out_shape=shaped((rows, 256), bf16),
-        scratch_shapes=[pltpu.VMEM((v, 256), bf16) for v in (rows, land_rows)] + sems,
-        compiler_params=pltpu.CompilerParams(
-            collective_id=ident, has_side_effects=True, vmem_limit_bytes=60 * MIB
-        ),
-        name=f"reduce{ident}",
-    )(*arrays)
-    return pl.pallas_call(
-        unpack_weights,
-        in_specs=[vm],
-        out_specs=(vm,) * len(arrays),
-        out_shape=tuple(shaped(v.shape, f32) for v in arrays),
-        compiler_params=params(60),
-        name="unpack_weights",
-    )(done)
 
 
 def whole(shape):
@@ -1076,35 +1258,22 @@
     n_clip = lax.axis_size("clip")
     clips, frames, high, cols, _ = slow_input.shape
     slab = clips * frames
-    own = lax.dynamic_slice_in_dim(frame_counts, lax.axis_index("clip") * clips, clips)
-    row_t = jnp.arange(slab) // clips
-    row_c = jnp.arange(slab) % clips
-    real = row_t < own[row_c]
-    m = jnp.broadcast_to(real.astype(f32)[:, None], (slab, 128))
-    col_c = jnp.arange(ALPHA * slab) // (ALPHA * frames)
-    col_f = jnp.arange(ALPHA * slab) % (ALPHA * frames)
-    want_f = (ALPHA * row_t[None, :] + jnp.arange(ALPHA)[:, None]).reshape(-1)
-    want_c = jnp.tile(row_c, ALPHA)
-    perm = (
-        (want_f[:, None] == col_f[None, :]) & (want_c[:, None] == col_c[None, :]) & jnp.tile(real, ALPHA)[:, None]
-    ).astype(bf16)
-    real_total = jnp.sum(frame_counts).astype(f32)
-    weight = jnp.broadcast_to(
-        (jnp.sum(frame_counts.reshape(n_clip, clips), axis=1).astype(f32) / real_total)[:, None, None], (n_clip, 1, 128)
-    )
-    inv = jnp.full((1, 128), 1.0, f32) / (real_total * (H * W))
-    def mixed(slow, fast, k):
-        lo = fast[k * C_FMID : (k + 1) * C_FMID]
-        return jnp.concatenate([slow[k * C_MID : (k + 1) * C_MID], jnp.tile(lo, ALPHA)])[None]
-
-    gain1, shift1 = mixed(slow_gain, fast_gain, 0), mixed(slow_shift, fast_shift, 0)
-    gain2, shift2 = mixed(slow_gain, fast_gain, 1), mixed(slow_shift, fast_shift, 1)
-    sgain, sshift = slow_gain[None, 2 * C_MID :], slow_shift[None, 2 * C_MID :]
-    fgain, fshift = fast_gain[None, 2 * C_FMID :], fast_shift[None, 2 * C_FMID :]
+    lanes = slow_gain.reshape(-1, 128), slow_shift.reshape(-1, 128)
+    slow_row = shaped((1, slow_gain.shape[0]), f32)
+    vm = vmem_spec()
+    m, perm, weight, inv, mids, ends, wfb, sgain, sshift = pl.pallas_call(
+        functools.partial(prepare, clips, n_clip),
+        in_specs=[pl.BlockSpec(memory_space=pltpu.SMEM)] + [vm] * 5,
+        out_specs=(vm,) * 9,
+        out_shape=(
+            shaped((slab, 128), f32), shaped((ALPHA * slab, ALPHA * slab), bf16), shaped((n_clip, 1, 128), f32),
+            shaped((1, 128), f32), shaped((4, 1, MIX), f32), shaped((2, 1, C_FAST), f32), shaped((9, 128, 128), bf16),
+            slow_row, slow_row,
+        ),
+        compiler_params=params(60),
+        name="prepare",
+    )(frame_counts, *lanes, fast_gain[None], fast_shift[None], fast_b_weight.reshape(9, C_FMID, C_FMID))
     wfa = fast_a_weight.transpose(0, 2, 1)
-    eye = jnp.eye(ALPHA, dtype=bf16)
-    wfb = (eye[None, :, None, :, None] * fast_b_weight.reshape(9, 1, C_FMID, 1, C_FMID)).reshape(9, 128, 128)
-
     xs = slow_input.transpose(1, 2, 3, 0, 4)
     xf = fast_input.transpose(0, 2, 3, 1, 4)
     cot = slow_cotangent.transpose(1, 2, 3, 0, 4)
@@ -1165,7 +1334,7 @@
     a1, z2, mom2, zrow, zcol, zcorner, cot = pl.pallas_call(
         functools.partial(second_pass, n_clip),
         grid=(high + 1,),
-        in_specs=[hbm] + [vm] * 11 + [slow_block(after(1))],
+        in_specs=[hbm] + [vm] * 10 + [slow_block(after(1))],
         out_specs=(vm, vm, vm, vm, vm, vm, late_line((cols, slab, C_IN), 1)),
         out_shape=(
             shaped((high + 2, cols + 2, slab, MIX), bf16), lines(MIX, f32), shaped((2, L1), f32),
@@ -1176,26 +1345,26 @@
         ] + exchange_scratch(n_clip, 2, L1) + rims,
         compiler_params=remote(2),
         name="second_pass",
-    )(z1, row1, col1, corner1, mom1, gain1, shift1, m, slow_b_weight, wfb, stp, weight, cot)
+    )(z1, row1, col1, corner1, mom1, mids, m, slow_b_weight, wfb, stp, weight, cot)
 
     L3 = C_IN + C_FAST
     a2, mom3, fcot = pl.pallas_call(
         functools.partial(third_pass, n_clip),
         grid=(2 * high,),
-        in_specs=[early_line((cols, slab, MIX))] + [vm] * 7 + [fast_block(after(high)), vm],
+        in_specs=[early_line((cols, slab, MIX))] + [vm] * 6 + [fast_block(after(high)), vm],
         out_specs=(early_line((cols, slab, MIX)), vm, late_line((cols, slab, WIDE_FAST), high)),
         out_shape=(lines(MIX, bf16), shaped((2, L3), f32), lines(WIDE_FAST, bf16)),
         scratch_shapes=[pltpu.VMEM((128, WIDE_FAST), bf16)] + [pltpu.VMEM((1, L3), f32)] * 3
         + exchange_scratch(n_clip, 2, L3),
         compiler_params=remote(3),
         name="third_pass",
-    )(z2, mom2, gain2, shift2, m, slow_c_weight, fast_c_weight, weight, fcot, perm)
+    )(z2, mom2, mids, m, slow_c_weight, fast_c_weight, weight, fcot, perm)
 
     L4 = 3 * C_IN + 2 * C_FAST
     so, fo, gs, gf, tot4 = pl.pallas_call(
         functools.partial(fourth_pass, n_clip, clips),
         grid=(2 * high,),
-        in_specs=[early_line((cols, slab, MIX)), early_line((cols, slab, C_IN))] + [vm] * 7 + [
+        in_specs=[early_line((cols, slab, MIX)), early_line((cols, slab, C_IN))] + [vm] * 6 + [
             early_line((cols, slab, C_IN)), early_line((cols, slab, WIDE_FAST)), early_line((cols, slab, WIDE_FAST)),
         ] + [vm] * 5,
         out_specs=(
@@ -1213,28 +1382,31 @@
         compiler_params=remote(4),
         name="fourth_pass",
     )(
-        a2, zp, base, mom2, mom3, sgain, sshift, fgain, fshift, cot, fcot, f, m, perm, slow_c_weight, fast_c_weight, weight,
+        a2, zp, base, mom2, mom3, sgain, sshift, ends, cot, fcot, f, m, perm, slow_c_weight, fast_c_weight, weight,
     )
 
     n = high * cols
+    early_sizes = (2048, 2048, 2048)
+    space_sizes = (1024, 1024, 512)
+    half_sizes = (512, 512, 512)
+    late_sizes = (1024, 1024, 1024)
 
     def flat(v):
         return v.reshape((n,) + v.shape[2:])
 
     steps = C_JOIN // C_MID
-    dzp, q2, tot5, qrow, qcol, qcorner, dwp, dwc, dwfc = pl.pallas_call(
+    dzp, q2, tot5, qrow, qcol, qcorner, dw1, dwfc = pl.pallas_call(
         functools.partial(fifth_pass, n_clip),
         grid=(high + steps,),
         in_specs=[
             early_line((cols, slab, C_IN)), early_line((cols, slab, WIDE_FAST)), early_line((cols, slab, MIX)),
             early_line((cols, slab, C_IN)), vm, early_line((cols, slab, MIX)),
-        ] + [vm] * 11 + [pl.BlockSpec((n, slab, C_MID), lambda i: (0, 0, jnp.maximum(i - high, 0))), vm],
+        ] + [vm] * 10 + [pl.BlockSpec((n, slab, C_MID), lambda i: (0, 0, jnp.clip(i - high, 0, steps - 1))), vm],
         out_specs=(
-            early_line((cols, slab, C_IN)), early_line((cols, slab, MIX)), vm, vm, vm, vm,
-            pl.BlockSpec((C_MID, C_IN), lambda i: (jnp.maximum(i - high, 0), 0)), vm, vm,
+            early_line((cols, slab, C_IN)), early_line((cols, slab, MIX)), vm, vm, vm, vm, vm, vm,
         ),
         out_shape=(lines(C_IN, bf16), lines(MIX, f32), shaped((1, 2 * MIX), f32)) + rim_shapes + (
-            shaped((C_JOIN, C_IN), bf16), shaped((C_MID, C_IN), bf16), shaped((C_FMID, C_FAST), f32),
+            shaped((sum(early_sizes), 256), bf16), shaped((C_FMID, C_FAST), f32),
         ),
         scratch_shapes=[
             pltpu.VMEM((high, cols, slab, C_IN), bf16), pltpu.VMEM((high, cols, slab, C_IN), bf16),
@@ -1244,93 +1416,93 @@
         compiler_params=remote(5),
         name="fifth_pass",
     )(
-        gs, gf, a2, zp, base, z2, mom2, mom3, tot4, inv, sgain, fgain, gain2, shift2, m, slow_c_weight, fast_c_weight,
+        gs, gf, a2, zp, base, z2, mom2, mom3, tot4, inv, sgain, ends, mids, m, slow_c_weight, fast_c_weight,
         flat(x), weight,
     )
 
-    q1, tot6, dwb, dwfb = pl.pallas_call(
-        functools.partial(sixth_pass, n_clip),
+    q1, tot6, dwb, kept = pl.pallas_call(
+        functools.partial(sixth_pass, n_clip, early_sizes),
         grid=(10,),
-        in_specs=[hbm] * 4 + [vm] * 17,
-        out_specs=(
-            vm, vm, pl.BlockSpec((None, None, C_MID, C_MID), lambda i: (jnp.maximum(i - 1, 0) // 3, lax.rem(jnp.maximum(i - 1, 0), 3), 0, 0)),
-            vm,
+        in_specs=[hbm] * 4 + [vm] * 16 + [hbm],
+        out_specs=(vm,) * 4,
+        out_shape=(
+            lines(MIX, f32), shaped((1, 2 * MIX), f32), shaped((sum(space_sizes), 256), bf16),
+            shaped((sum(Reducer.layout(n_clip, early_sizes)[2]), 256), bf16),
         ),
-        out_shape=(
-            lines(MIX, f32), shaped((1, 2 * MIX), f32), shaped((3, 3, C_MID, C_MID), bf16),
-            shaped((9, C_FMID, C_FMID), f32),
-        ),
-        scratch_shapes=[pltpu.VMEM((high + 2, cols + 2, slab, MIX), bf16)]
+        scratch_shapes=[pltpu.VMEM((9, C_FMID, C_FMID), f32), pltpu.VMEM((high + 2, cols + 2, slab, MIX), bf16)]
         + [pltpu.VMEM((high, cols, slab, MIX), f32)] * 3
         + [pltpu.VMEM((high + 2, cols + 2, slab, MIX), bf16)]
         + [pltpu.SemaphoreType.DMA((high,))] * 3
-        + [pltpu.SemaphoreType.DMA((1,)), pltpu.VMEM((1, 2 * MIX), f32)]
-        + exchange_scratch(n_clip, 1, 2 * MIX),
+        + [pltpu.SemaphoreType.DMA((2,)), pltpu.VMEM((1, 2 * MIX), f32)]
+        + [pltpu.VMEM((sum(early_sizes), 256), bf16), Reducer.scratch(n_clip, early_sizes)]
+        + exchange_scratch(n_clip, 1, 2 * MIX) + Reducer.sems(n_clip, early_sizes, 2),
         compiler_params=remote(6),
         name="sixth_pass",
     )(
-        q2, z2, z1, a1, qrow, qcol, qcorner, zrow, zcol, zcorner, mom1, mom2, tot5, inv, gain1, shift1, gain2, m,
-        slow_b_weight, wfb, weight,
+        q2, z2, z1, a1, qrow, qcol, qcorner, zrow, zcol, zcorner, mom1, mom2, tot5, inv, mids, m,
+        slow_b_weight, wfb, weight, dwfc, dw1,
     )
 
-    perm_spec = whole((ALPHA * slab, ALPHA * slab))
-    sx, fx, da, dl, df = pl.pallas_call(
-        functools.partial(first_back, clips),
+    def twice_line(shape):
+        begin = high + steps
+        return pl.BlockSpec(
+            (None,) + tuple(shape),
+            lambda i: (jnp.where(i < begin, jnp.minimum(i, high - 1), i - begin),) + (0,) * len(shape),
+        )
+
+    sx, fx, done1, done_b, done_h, done_a = pl.pallas_call(
+        functools.partial(seventh_pass, clips, n_clip, early_sizes, space_sizes, half_sizes, late_sizes),
+        grid=(2 * high + steps,),
+        in_specs=[
+            early_line((cols, slab, MIX)), early_line((cols, slab, MIX)), twice_line((cols, slab, C_IN)),
+            late_line((cols, slab, WIDE_FAST), high + steps),
+            pl.BlockSpec((n, slab, C_MID), lambda i: (0, 0, jnp.clip(i - high, 0, steps - 1))), vm, vm, hbm,
+        ] + [vm] * 10,
+        out_specs=(slow_block(after(high + steps)), fast_block(after(high + steps)), hbm, hbm, hbm, hbm),
+        out_shape=(
+            shaped(xs.shape, bf16), shaped(xf.shape, bf16), shaped((sum(early_sizes), 256), bf16),
+            shaped((sum(space_sizes), 256), bf16), shaped((sum(half_sizes), 256), bf16), shaped((sum(late_sizes), 256), bf16),
+        ),
+        scratch_shapes=[
+            pltpu.VMEM((sum(v), 256), bf16) for v in (early_sizes, space_sizes, half_sizes, late_sizes)
+        ] + [
+            pltpu.VMEM((high, cols, slab, 3 * C_MID), bf16), pltpu.VMEM((high, cols, slab, 2 * C_LAT), bf16),
+            pltpu.VMEM((high, cols, slab, 3 * 128), bf16), pltpu.VMEM((128, WIDE_FAST), bf16),
+            pltpu.VMEM((2, 128, C_FAST), bf16), pltpu.VMEM((sum(space_sizes), 256), bf16),
+            Reducer.scratch(n_clip, space_sizes), pltpu.VMEM((sum(half_sizes), 256), bf16),
+            Reducer.scratch(n_clip, half_sizes), pltpu.VMEM((sum(late_sizes), 256), bf16),
+            Reducer.scratch(n_clip, late_sizes), pltpu.SemaphoreType.DMA((4,)),
+        ] + Reducer.sems(n_clip, early_sizes, 2) + Reducer.sems(n_clip, space_sizes) + Reducer.sems(n_clip, half_sizes)
+        + Reducer.sems(n_clip, late_sizes),
+        compiler_params=remote(7),
+        name="seventh_pass",
+    )(
+        q1, z1, dzp, gf, flat(x), flat(f), kept, dwb, mom1, tot6, inv, mids, m, perm, lateral_weight, slow_a_weight,
+        slow_proj_weight, wfa,
+    )
+
+    slow_rows, fast_row = shaped(lanes[0].shape, f32), shaped((1, fast_gain.shape[0]), f32)
+    def here(i):
+        return i
+
+    weights = (
+        shaped((C_JOIN, C_IN), f32), shaped((C_MID, C_IN), f32), shaped((3, 3, C_MID, C_MID), f32),
+        shaped((3, C_JOIN, C_MID), f32), shaped((5, C_FAST, C_LAT), f32),
+    )
+    maps = [slow_block(here), fast_block(here)] * 2
+    so, fo, sx, fx, dwp, dwc, dwb, dwa, dwl, dwfa, dwfc, dwfb, dsg, dss, dfg, dfs = pl.pallas_call(
+        finish_outputs,
         grid=(high,),
-        in_specs=[
-            per_line((cols, slab, MIX)), per_line((cols, slab, MIX)), whole((2, MIX)), whole((1, 2 * MIX)),
-            whole((1, 128)), whole((1, MIX)), m_spec, perm_spec, per_line((cols, slab, C_IN)),
-            per_line((cols, slab, WIDE_FAST)), whole((5, C_FAST, C_LAT)), whole((3, C_JOIN, C_MID)),
-            whole((C_JOIN, C_IN)), whole((3, C_FMID, C_FAST)),
-        ],
-        out_specs=(
-            slow_block(early), fast_block(early), per_line((cols, slab, 3 * C_MID)), per_line((cols, slab, 2 * C_LAT)),
-            per_line((cols, slab, 3 * 128)),
+        in_specs=maps + [vm] * 7,
+        out_specs=tuple(maps) + (hbm,) * 5 + (vm,) * 7,
+        out_shape=(shaped(xs.shape, bf16), shaped(xf.shape, bf16)) * 2 + weights + (
+            shaped((3, C_FMID, C_FAST), f32), shaped((C_FMID, C_FAST), f32), shaped((9, C_FMID, C_FMID), f32),
+            slow_rows, slow_rows, fast_row, fast_row,
         ),
-        out_shape=(
-            shaped(xs.shape, bf16), shaped(xf.shape, bf16), lines(3 * C_MID, bf16), lines(2 * C_LAT, bf16),
-            lines(3 * 128, bf16),
-        ),
-        scratch_shapes=[pltpu.VMEM((128, WIDE_FAST), bf16), pltpu.VMEM((2, 128, C_FAST), bf16)],
-        compiler_params=params(40),
-        name="first_back",
-    )(q1, z1, mom1, tot6, inv, gain1, m, perm, dzp, gf, lateral_weight, slow_a_weight, slow_proj_weight, wfa)
-
-    dwa, dwl, dws = pl.pallas_call(
-        first_weights,
-        grid=(C_JOIN // C_MID,),
-        in_specs=[
-            pl.BlockSpec((n, slab, C_MID), lambda i: (0, 0, i)), whole((n, slab, WIDE_FAST)),
-            whole((n, slab, 3 * C_MID)), whole((n, slab, 2 * C_LAT)), whole((n, slab, 3 * 128)),
-            whole((C_FMID, C_FAST)), whole((9, C_FMID, C_FMID)),
-        ],
-        out_specs=(
-            pl.BlockSpec((3, C_MID, C_MID), lambda i: (0, i, 0)), whole((5, C_FAST, C_LAT)), whole((512, C_FAST)),
-        ),
-        out_shape=(
-            shaped((3, C_JOIN, C_MID), bf16), shaped((5, C_FAST, C_LAT), bf16), shaped((512, C_FAST), bf16),
-        ),
-        compiler_params=params(48),
-        name="first_weights",
-    )(flat(x), flat(f), flat(da), flat(dl), flat(df), dwfc, dwfb)
-
-    dwp, dwc, dwb, dwa, dwl, dws = run_reduce(7, n_clip, (dwp, dwc, dwb, dwa, dwl, dws))
-    dwfa = dws[: 3 * C_FMID].reshape(3, C_FMID, C_FAST)
-    dwfc = dws[3 * C_FMID : 4 * C_FMID]
-    dwfb = dws[4 * C_FMID : 13 * C_FMID, :C_FMID]
-
-    def joined_sums(k):
-        first = [tot6[0, k * MIX : (k + 1) * MIX], tot5[0, k * MIX : (k + 1) * MIX]]
-        last = tot4[0, :C_IN] if k == 0 else tot4[0, C_IN : 2 * C_IN]
-        proj = tot4[0, :C_IN] if k == 0 else tot4[0, 2 * C_IN : 3 * C_IN]
-        at = 3 * C_IN + k * C_FAST
-        slow = jnp.concatenate([first[0][:C_MID], first[1][:C_MID], last, proj])
-        lo = C_MID + C_FMID
-        fast = jnp.concatenate([first[0][C_MID:lo], first[1][C_MID:lo], tot4[0, at : at + C_FAST]])
-        return slow, fast
-
-    slow_shift_grad, fast_shift_grad = joined_sums(0)
-    slow_gain_grad, fast_gain_grad = joined_sums(1)
+        scratch_shapes=[pltpu.VMEM(v.shape, f32) for v in weights] + [pltpu.SemaphoreType.DMA((5,))],
+        compiler_params=params(60),
+        name="finish_outputs",
+    )(so, fo, sx, fx, done1, done_b, done_h, done_a, tot4, tot5, tot6)
     return (
         so.transpose(3, 0, 1, 2, 4),
         fo.transpose(0, 3, 1, 2, 4),
@@ -1344,10 +1516,10 @@
         dwfa.transpose(0, 2, 1),
         dwfb.reshape(3, 3, C_FMID, C_FMID),
         dwfc,
-        slow_gain_grad,
-        slow_shift_grad,
-        fast_gain_grad,
-        fast_shift_grad,
+        dsg.reshape(-1),
+        dss.reshape(-1),
+        dfg[0],
+        dfs[0],
     )
 
 

time: 331 us -> 281 us (0.85)
  local copies, waits for them, and re-layouts: 22.3 us -> 0 us
  Pallas kernels: 299 us -> 279 us
  other arithmetic: 8.09 us -> 0 us
    pallas_call x5 -> x4, Pallas kernels: 163 us -> 142 us  [the longest x1 88.1 us: on_device(): pl.pallas_call(functools.partial(seventh_pass, clips, n_clip, early_sizes...]
    unnamed x20 -> x0, local copies, waits for them, and re-layouts: 7.84 us -> none
    slice x14 -> x0, local copies, waits for them, and re-layouts: 5.69 us -> none  [the longest x1 1.58 us: on_device(): dwfb = dws[4 * C_FMID:13 * C_FMID, :C_FMID]]
    broadcast_in_dim x8 -> x0, local copies, waits for them, and re-layouts: 4.71 us -> none  [the longest x4 2.26 us: mixed(): jnp.concatenate([slow[k * C_MID:(k + 1) * C_MID], jnp.tile(lo, ALPHA)])]
    convert_element_type x3 -> x0, other arithmetic: 3.4 us -> none  [the longest x1 2.59 us: on_device(): m = jnp.broadcast_to(real.astype(f32)[:, None], (slab, 128))]
where the time goes in v4:
time: 281 us; the launch traced here: 280 us
  Pallas kernels  279 us (99%)
    pallas_call x1, Pallas kernels, on_device(): pl.pallas_call(functools.partial(seventh_pass, clips, n_clip, early_sizes...  88.1 us
    pallas_call x1, Pallas kernels, on_device(): pl.pallas_call(functools.partial(sixth_pass, n_clip, early_sizes), grid=(...  34.9 us
    pallas_call x1, Pallas kernels, on_device(): pl.pallas_call(functools.partial(fifth_pass, n_clip), grid=(high + steps,...  32.1 us
    pallas_call x1, Pallas kernels, on_device(): pl.pallas_call(functools.partial(first_pass, clips, n_clip), grid=(2 * hi...  31.4 us
    pallas_call x1, Pallas kernels, on_device(): pl.pallas_call(functools.partial(fourth_pass, n_clip, clips), grid=(2 * h...  28.5 us
    pallas_call x1, Pallas kernels, on_device(): pl.pallas_call(functools.partial(second_pass, n_clip), grid=(high + 1,),...  26.1 us
    pallas_call x1, Pallas kernels, on_device(): pl.pallas_call(functools.partial(third_pass, n_clip), grid=(2 * high,), i...  19 us
    pallas_call x1, Pallas kernels, on_device(): pl.pallas_call(finish_outputs, grid=(high,), in_specs=maps + [vm] * 7, ou...  17.4 us

profile of v4, /device:TPU:0, one launch (start us, length us, event | category | flops | bytes accessed | tf_op | source)
XLA Modules:
  0.0 280.3 jit_solution(12968716068261555274)
XLA Ops:
  0.6 1.9 prepare.1
  2.5 31.4 %first_pass.1 = (bf16[7,7,48,1280]{3,2,1,0:T(8,128)(2,1)}, bf16[7,7,48,512]{3,2,1,0:T(8,128)(2,1)}, f32[7,7,48,384]{3,2,1,0:T(8,128)}, bf16[7,7,48,1024]{3,2,1,0...) custom-call(bf16[12,7,7,4,1024]{4,3,2,1,0:T(4,128)(2,1)} %bitcast.26, ...), custom_call_target="tpu_custom_call" | custom-call | tf_op jit(solution)/shard_map/first_pass/pallas_call | solution.py:1313
  33.9 26.1 %second_pass.1 = (bf16[9,9,48,384]{3,2,1,0:T(8,128)(2,1)}, f32[7,7,48,384]{3,2,1,0:T(8,128)}, f32[2,1408]{1,0:T(2,128)}, f32[7,48,384]{2,1,0:T(8,128)}, f32[7,48...) custom-call(f32[7,7,48,384]{3,2,1,0:T(8,128)} %get-tuple-element.87.z1_hbm.z1, ...), custom_call_target="tpu_custom_call" | custom-call | tf_op jit(solution)/shard_map/second_pass/pallas_call | solution.py:1334
  60.1 19.0 %third_pass.1 = (bf16[7,7,48,384]{3,2,1,0:T(8,128)(2,1)}, f32[2,1152]{1,0:T(2,128)}, bf16[7,7,48,512]{3,2,1,0:T(8,128)(2,1)}) custom-call(f32[7,7,48,384]{3,2,1,0:T(8,128)} %get-tuple-element.95.z2.z2_hbm, f32[2,1408]{1,0:T(2,128)} %get-tuple-element.96.mom.mom2, f32[4,1,384]{2,1,0:T(1,128)} %get-tuple-element.92.mids, f32[48,128]{1,0:T(8,128)} %get-tuple-element.84.m, ...), custom_call_target="tpu_custom_call" | custom-call | tf_op jit(solution)/shard_map/third_pass/pallas_call | solution.py:1351
  79.1 28.5 %fourth_pass.1 = (bf16[12,7,7,4,1024]{4,3,2,1,0:T(4,128)(2,1)}, bf16[4,7,7,48,128]{4,3,2,1,0:T(8,128)(2,1)}, f32[7,7,48,1024]{3,2,1,0:T(8,128)}, f32[7,7,48,512]{3,2,1,0:T(8,128)}, f32[1,3328]{1,0:T(1,128)}) custom-call(bf16[7,7,48,384]{3,2,1,0:T(8,128)(2,1)} %get-tuple-element.97.a2, bf16[7,7,48,1024]{3,2,1,0:T(8,128)(2,1)} %get-tuple-element.98.zp, ...), custom_call_target="tpu_custom_call" | custom-call | tf_op jit(solution)/shard_map/fourth_pass/pallas_call | solution.py:1364
  107.6 32.1 %fifth_pass.1 = (bf16[7,7,48,1024]{3,2,1,0:T(8,128)(2,1)}, f32[7,7,48,384]{3,2,1,0:T(8,128)}, f32[1,768]{1,0:T(1,128)}, f32[7,48,384]{2,1,0:T(8,128)}, f32[7,48,...) custom-call(f32[7,7,48,1024]{3,2,1,0:T(8,128)} %get-tuple-element.109.gs, ...), custom_call_target="tpu_custom_call" | custom-call | tf_op jit(solution)/shard_map/fifth_pass/pallas_call | solution.py:1398
  139.7 34.9 %sixth_pass.1 = (f32[7,7,48,384]{3,2,1,0:T(8,128)}, f32[1,768]{1,0:T(1,128)}, bf16[2560,256]{1,0:T(8,128)(2,1)}, bf16[192,256]{1,0:T(8,128)(2,1)}) custom-call(f32[7,7,48,384]{3,2,1,0:T(8,128)} %get-tuple-element.114.q2_hbm, f32[7,7,48,384]{3,2,1,0:T(8,128)} %get-tuple-element.95.z2.z2_hbm, f32[7,7,48,384]{3,2,1,0:T(8,128)} %get-tuple-element.87.z1_hbm.z1, ...), custom_call_target="tpu_custom_call" | custom-call | tf_op jit(solution)/shard_map/sixth_pass/pallas_call | solution.py:1423
  174.6 88.1 %seventh_pass.1 = (bf16[12,7,7,4,1024]{4,3,2,1,0:T(4,128)(2,1)}, bf16[4,7,7,48,128]{4,3,2,1,0:T(8,128)(2,1)}, bf16[6144,256]{1,0:T(8,128)(2,1)}, bf16[2560,256]{...) custom-call(f32[7,7,48,384]{3,2,1,0:T(8,128)} %get-tuple-element.125.q1, ...), custom_call_target="tpu_custom_call" | custom-call | tf_op jit(solution)/shard_map/seventh_pass/pallas_call | solution.py:1453
  262.7 17.4 %finish_outputs.1 = (bf16[12,7,7,4,1024]{4,3,2,1,0:T(4,128)(2,1)}, bf16[4,7,7,48,128]{4,3,2,1,0:T(8,128)(2,1)}, bf16[12,7,7,4,1024]{4,3,2,1,0:T(4,128)(2,1)}, bf...) custom-call(bf16[12,7,7,4,1024]{4,3,2,1,0:T(4,128)(2,1)} %get-tuple-, ...), custom_call_target="tpu_custom_call" | custom-call | tf_op jit(solution)/shard_map/finish_outputs/pallas_call | solution.py:1493

commit v5 on v4

--- a/solution.py
+++ b/solution.py
@@ -396,8 +396,9 @@
 
     @pl.when(i > 0)
     def _():
+        half_mask = (0.5 * spread(m[...], C_IN)).astype(bf16)
         for w in range(cols):
-            cot_out[w] = cot[:, w].reshape(slab, C_IN)
+            cot_out[w] = cot[:, w].reshape(slab, C_IN) * half_mask
 
     @pl.when(i == high)
     def _():
@@ -457,7 +458,7 @@
         for w in range(cols):
             phases = dot(perm[...], fcot[:, w].reshape(ALPHA * slab, C_FAST)).astype(bf16)
             for p in range(ALPHA):
-                fcot_out[w, :, p * C_FAST : (p + 1) * C_FAST] = phases[p * slab : (p + 1) * slab]
+                fcot_out[w, :, p * C_FAST : (p + 1) * C_FAST] = 0.5 * phases[p * slab : (p + 1) * slab]
 
     @pl.when(i == 2 * high - 1)
     def _():
@@ -465,7 +466,7 @@
 
 
 def fourth_pass(n_clip, clips, a2, zp, base, mom2, mom3, sgain, sshift, fends, cot, fcot, fast_in, m, perm, wc,
-                wfc, weight, so, fo, gs, gf, tot, so_keep, fo_keep, sums, big, *refs):
+                wfc, weight, so, fo, gs, gf, tot, so_keep, fo_keep, sums, big, z_line, f_line, *refs):
     i = pl.program_id(0)
     high = pl.num_programs(0) // 2
     cols, slab, _ = a2.shape
@@ -482,44 +483,51 @@
 
     @pl.when(i < high)
     def _():
-        mask = spread(m[...], C_IN)
-        mask_f = spread(m[...], WIDE_FAST)
+        mid, far = 2 * C_MID, 2 * C_MID + C_IN
         mean_c = mom3[0:1, :C_IN]
         scale_c = lax.rsqrt(mom3[1:2, :C_IN] + eps_norm)
         mean_p = mom2[0:1, MIX:] - base[...]
         scale_p = lax.rsqrt(mom2[1:2, MIX:] + eps_norm)
         mean_f = jnp.tile(mom3[0:1, C_IN:], (1, ALPHA))
         scale_f = jnp.tile(lax.rsqrt(mom3[1:2, C_IN:] + eps_norm), (1, ALPHA))
-        mid, far = 2 * C_MID, 2 * C_MID + C_IN
-        gain_c, gain_p = sgain[:, mid:far], sgain[:, far:]
-        shift_cp = sshift[:, mid:far] + sshift[:, far:]
-        gain_f = jnp.tile(fends[0], (1, ALPHA))
-        shift_f = jnp.tile(fends[1], (1, ALPHA))
+        mult_c = 0.5 * sgain[:, mid:far] * scale_c
+        mult_p = 0.5 * sgain[:, far:] * scale_p
+        shift_cp = 0.5 * (sshift[:, mid:far] + sshift[:, far:])
+        mult_f = 0.5 * jnp.tile(fends[0], (1, ALPHA)) * scale_f
+        shift_f = 0.5 * jnp.tile(fends[1], (1, ALPHA))
+
+        def gate(v, g):
+            u = 1.0 + jnp.tanh(v)
+            o = v * u
+            return o, g * (u + o * (2.0 - u))
+
         totals = [jnp.zeros((8, C_IN), f32)] * 3 + [jnp.zeros((8, WIDE_FAST), f32)] * 2
+        rows = a2[...].reshape(cols * slab, MIX)
+        z_line[...] = dot(rows[:, :C_MID], wc[...]).reshape(cols, slab, C_IN)
+        f_line[...] = dot(rows[:, C_MID:], big[...]).reshape(cols, slab, WIDE_FAST)
         for w in range(cols):
-            zc = (dot(a2[w, :, :C_MID], wc[...]) - mean_c) * scale_c
-            zq = (zp[w].astype(f32) - mean_p) * scale_p
-            ps = gain_c * zc + gain_p * zq + shift_cp
-            sig = sigmoid(ps)
-            so_keep[i, w] = (ps * sig * mask).astype(bf16)
-            back = cot[w].astype(f32) * (sig * (1.0 + ps * (1.0 - sig)) * mask)
+            zc = z_line[w] - mean_c
+            zq = zp[w].astype(f32) - mean_p
+            res, back = gate(mult_c * zc + mult_p * zq + shift_cp, cot[w].astype(f32))
+            so_keep[i, w] = res.astype(bf16)
             gs[w] = back
             totals[0] += tile_sum(back)
             totals[1] += tile_sum(back * zc)
             totals[2] += tile_sum(back * zq)
-            fc = (dot(a2[w, :, C_MID:], big[...]) - mean_f) * scale_f
-            pf = gain_f * fc + shift_f + fast_in[w].astype(f32)
-            sig = sigmoid(pf)
-            fo_keep[i, w] = (pf * sig).astype(bf16)
-            fback = fcot[w].astype(f32) * (sig * (1.0 + pf * (1.0 - sig)))
+            fc = f_line[w] - mean_f
+            res, fback = gate(mult_f * fc + shift_f + 0.5 * fast_in[w].astype(f32), fcot[w].astype(f32))
+            fo_keep[i, w] = res.astype(bf16)
             gf[w] = fback
             totals[3] += tile_sum(fback)
             totals[4] += tile_sum(fback * fc)
+        scales = (None, scale_c, scale_p)
         for k in range(3):
-            sums[:, k * C_IN : (k + 1) * C_IN] += jnp.sum(totals[k], axis=0, keepdims=True)
+            total = jnp.sum(totals[k], axis=0, keepdims=True)
+            sums[:, k * C_IN : (k + 1) * C_IN] += total if k == 0 else total * scales[k]
         for k in range(2):
             at = 3 * C_IN + k * C_FAST
-            sums[:, at : at + C_FAST] += block_sum(jnp.sum(totals[3 + k], axis=0, keepdims=True))
+            total = jnp.sum(totals[3 + k], axis=0, keepdims=True)
+            sums[:, at : at + C_FAST] += block_sum(total if k == 0 else total * scale_f)
 
     @pl.when(i == high)
     def _():
@@ -533,8 +541,9 @@
 
     @pl.when(i >= high)
     def _():
+        mask = spread(m[...], C_IN).astype(bf16)
         for w in range(cols):
-            so[:, w] = so_keep[i - high, w].reshape(slab // clips, clips, C_IN)
+            so[:, w] = (so_keep[i - high, w] * mask).reshape(slab // clips, clips, C_IN)
             wide = fo_keep[i - high, w]
             stacked = jnp.concatenate([wide[:, p * C_FAST : (p + 1) * C_FAST] for p in range(ALPHA)], axis=0)
             fo[:, w] = dot_tn(perm[...], stacked).astype(bf16).reshape(clips, slab, C_FAST)
@@ -546,7 +555,7 @@
 
 def fifth_pass(n_clip, gs, gf, a2, zp, base, z2, mom2, mom3, tot4, inv, sgain, fends, mids, m, wc, wfc, x, weight,
                dzp_out, q_out, tot, row, col, corner, w_out, wfc_out,
-               dzc_keep, dzp_keep, dfc_keep, a_keep, sums, big, line, side, *refs):
+               dzc_keep, dzp_keep, dfc_keep, a_keep, sums, big, z_line, f_line, line, side, *refs):
     i = pl.program_id(0)
     high, cols, slab, _ = dzc_keep.shape
     n = high * cols
@@ -574,22 +583,27 @@
         mult_p = sgain[:, 2 * C_MID + C_IN :] * scale_p
         mult_f = jnp.tile(fends[0], (1, ALPHA)) * scale_f
         first_s = tot4[:, :C_IN] * inv_s
-        second_c = tot4[:, C_IN : 2 * C_IN] * inv_s
-        second_p = tot4[:, 2 * C_IN : 3 * C_IN] * inv_s
-        first_f = jnp.tile(tot4[:, 3 * C_IN : 3 * C_IN + C_FAST] * inv_f, (1, ALPHA))
-        second_f = jnp.tile(tot4[:, 3 * C_IN + C_FAST :] * inv_f, (1, ALPHA))
+        second_c = mult_c * scale_c * tot4[:, C_IN : 2 * C_IN] * inv_s
+        second_p = mult_p * scale_p * tot4[:, 2 * C_IN : 3 * C_IN] * inv_s
+        first_f = mult_f * jnp.tile(tot4[:, 3 * C_IN : 3 * C_IN + C_FAST] * inv_f, (1, ALPHA))
+        second_f = mult_f * scale_f * jnp.tile(tot4[:, 3 * C_IN + C_FAST :] * inv_f, (1, ALPHA))
+        first_c = mult_c * first_s - mean_c * second_c
+        first_p = mult_p * first_s - mean_p * second_p
+        first_f = first_f - mean_f * second_f
         mask_f = spread(m[...], WIDE_FAST)
         a_keep[i] = a2[...]
+        flat = a2[...].reshape(rows, MIX)
+        z_line[...] = dot(flat[:, :C_MID], wc[...]).reshape(cols, slab, C_IN)
+        f_line[...] = dot(flat[:, C_MID:], big[...]).reshape(cols, slab, WIDE_FAST)
         for w in range(cols):
-            zc = (dot(a2[w, :, :C_MID], wc[...]) - mean_c) * scale_c
-            zq = (zp[w].astype(f32) - mean_p) * scale_p
+            zc = z_line[w]
             g = gs[w]
-            dzc_keep[i, w] = (mult_c * (g - mask * (first_s + zc * second_c))).astype(bf16)
-            dzp = (mult_p * (g - mask * (first_s + zq * second_p))).astype(bf16)
+            dzc_keep[i, w] = (mult_c * g - mask * (first_c + zc * second_c)).astype(bf16)
+            dzp = (mult_p * g - mask * (first_p + zp[w].astype(f32) * second_p)).astype(bf16)
             dzp_keep[i, w] = dzp
             dzp_out[w] = dzp
-            fc = (dot(a2[w, :, C_MID:], big[...]) - mean_f) * scale_f
-            dfc_keep[i, w] = (mult_f * (gf[w] - mask_f * (first_f + fc * second_f))).astype(bf16)
+            fc = f_line[w]
+            dfc_keep[i, w] = (mult_f * gf[w] - mask_f * (first_f + fc * second_f)).astype(bf16)
         da = dot_nt(dzc_keep[i].reshape(rows, C_IN), wc[...]).reshape(cols, slab, C_MID)
         df = dot_nt(dfc_keep[i].reshape(rows, WIDE_FAST), big[...]).reshape(cols, slab, 128)
         grads = jnp.concatenate([da, df], axis=2)
@@ -913,12 +927,10 @@
                 self.gather_copy(s, k - 1, False).start()
 
 
-SPACE_STEPS = (2, 5, 7, 8, 10)
-FIRST_STEPS = (5, 7, 9, 12, 14)
-HALF_STEPS = (10, 11, 13, 14, 15)
-SPACE_BACK = (11, 13, 14, 15, 16, 17)
-HALF_BACK = (15, 16, 17, 18, 18, 18)
-LATE_STEPS = (14, 16, 18)
+SPACE_STEPS = (5, 9, 12, 15, 18, 18, 18, 18, 18, 18, 18)
+FIRST_STEPS = (5, 9, 12, 15, 18)
+HALF_STEPS = (12, 15, 18, 18, 18, 18, 18, 18, 18, 18, 18)
+LATE_STEPS = (15, 18, 18, 18, 18, 18, 18, 18, 18, 18, 18)
 
 
 def seventh_pass(clips, n_clip, early_sizes, space_sizes, half_sizes, late_sizes, q1, z1, dzp, gf, x, f, kept, space_hbm, mom1, tot6, inv,
@@ -950,22 +962,36 @@
         load.wait()
         space.send(0)
 
-    plan = {}
+    plan, rest = {}, []
+    final = pl.num_programs(0) - 1
 
     def book(ops, steps):
+        left = []
         for j, op in enumerate(ops):
-            plan.setdefault(steps[j * len(steps) // len(ops)], []).append(op)
-
-    book([functools.partial(space.gather, k) for k in range(end + 1)], SPACE_STEPS)
-    book([functools.partial(first.take, k) for k in range(end, -1, -1)], FIRST_STEPS)
-    book([functools.partial(half.gather, k) for k in range(end + 1)], HALF_STEPS)
-    book([space.regain] + [functools.partial(space.take, k) for k in range(end, -1, -1)], SPACE_BACK)
-    book([half.regain] + [functools.partial(half.take, k) for k in range(end, -1, -1)], HALF_BACK)
-    book([functools.partial(last.gather, k) for k in range(3)], LATE_STEPS)
-    final = pl.num_programs(0) - 1
+            step = steps[j * len(steps) // len(ops)]
+            if step >= 2 * high + C_JOIN // C_MID - 1:
+                left.append(op)
+            else:
+                plan.setdefault(step, []).append(op)
+        rest.append(left)
+
+    down, up = range(end + 1), range(end, -1, -1)
+    book(
+        [functools.partial(space.gather, k) for k in down] + [space.regain]
+        + [functools.partial(space.take, k) for k in up], SPACE_STEPS,
+    )
+    book([functools.partial(first.take, k) for k in up], FIRST_STEPS)
+    book(
+        [functools.partial(half.gather, k) for k in down] + [half.regain]
+        + [functools.partial(half.take, k) for k in up], HALF_STEPS,
+    )
+    book(
+        [functools.partial(last.gather, k) for k in down] + [last.regain]
+        + [functools.partial(last.take, k) for k in up], LATE_STEPS,
+    )
     for step, ops in sorted(plan.items()):
 
-        @pl.when((i == step) & (i < final))
+        @pl.when(i == step)
         def _():
             for op in ops:
                 op()
@@ -1056,15 +1082,10 @@
 
     @pl.when(i == final)
     def _():
-        for step, ops in sorted(plan.items()):
-            if step >= 2 * high + steps - 1:
-                for op in ops:
-                    op()
-        for k in range(3, end + 1):
-            last.gather(k)
-        last.regain()
-        for k in range(end, -1, -1):
-            last.take(k)
+        for k in range(max(len(left) for left in rest)):
+            for left in rest:
+                if k < len(left):
+                    left[k]()
         saves = [
             pltpu.make_async_copy(a, b, load_sem.at[k])
             for k, (a, b) in enumerate(((done1, out1), (done_b, out_b), (done_h, out_h), (done_a, out_a)))
@@ -1377,7 +1398,8 @@
         ),
         scratch_shapes=[
             pltpu.VMEM((high, cols, slab, C_IN), bf16), pltpu.VMEM((high, cols, slab, WIDE_FAST), bf16),
-            pltpu.VMEM((1, L4), f32), pltpu.VMEM((128, WIDE_FAST), bf16),
+            pltpu.VMEM((1, L4), f32), pltpu.VMEM((128, WIDE_FAST), bf16), pltpu.VMEM((cols, slab, C_IN), f32),
+            pltpu.VMEM((cols, slab, WIDE_FAST), f32),
         ] + exchange_scratch(n_clip, 1, L4),
         compiler_params=remote(4),
         name="fourth_pass",
@@ -1411,7 +1433,8 @@
         scratch_shapes=[
             pltpu.VMEM((high, cols, slab, C_IN), bf16), pltpu.VMEM((high, cols, slab, C_IN), bf16),
             pltpu.VMEM((high, cols, slab, WIDE_FAST), bf16), pltpu.VMEM((high, cols, slab, MIX), bf16),
-            pltpu.VMEM((1, 2 * MIX), f32), pltpu.VMEM((128, WIDE_FAST), bf16),
+            pltpu.VMEM((1, 2 * MIX), f32), pltpu.VMEM((128, WIDE_FAST), bf16), pltpu.VMEM((cols, slab, C_IN), f32),
+            pltpu.VMEM((cols, slab, WIDE_FAST), f32),
         ] + edge_scratch + exchange_scratch(n_clip, 1, 2 * MIX) + rims,
         compiler_params=remote(5),
         name="fifth_pass",

time: 281 us -> 263 us (0.936)
  Pallas kernels: 279 us -> 261 us
    pallas_call x1, Pallas kernels: 88.1 us -> 76.1 us  [on_device(): pl.pallas_call(functools.partial(seventh_pass, clips, n_clip, early_sizes...]
    pallas_call x1, Pallas kernels: 28.5 us -> 25 us  [on_device(): pl.pallas_call(functools.partial(fourth_pass, n_clip, clips), grid=(2 * h...]
where the time goes in v5:
time: 263 us; the launch traced here: 262 us
  Pallas kernels  261 us (99%)
    pallas_call x1, Pallas kernels, on_device(): pl.pallas_call(functools.partial(seventh_pass, clips, n_clip, early_sizes...  76.1 us
    pallas_call x1, Pallas kernels, on_device(): pl.pallas_call(functools.partial(sixth_pass, n_clip, early_sizes), grid=(...  34.9 us
    pallas_call x1, Pallas kernels, on_device(): pl.pallas_call(functools.partial(first_pass, clips, n_clip), grid=(2 * hi...  31.4 us
    pallas_call x1, Pallas kernels, on_device(): pl.pallas_call(functools.partial(fifth_pass, n_clip), grid=(high + steps,...  29.8 us
    pallas_call x1, Pallas kernels, on_device(): pl.pallas_call(functools.partial(second_pass, n_clip), grid=(high + 1,),...  26.1 us
    pallas_call x1, Pallas kernels, on_device(): pl.pallas_call(functools.partial(fourth_pass, n_clip, clips), grid=(2 * h...  25 us
    pallas_call x1, Pallas kernels, on_device(): pl.pallas_call(functools.partial(third_pass, n_clip), grid=(2 * high,), i...  19 us
    pallas_call x1, Pallas kernels, on_device(): pl.pallas_call(finish_outputs, grid=(high,), in_specs=maps + [vm] * 7, ou...  17.4 us

profile of v5, /device:TPU:0, one launch (start us, length us, event | category | flops | bytes accessed | tf_op | source)
XLA Modules:
  0.0 262.4 jit_solution(1448737074848415367)
XLA Ops:
  0.6 1.9 prepare.1
  2.5 31.4 %first_pass.1 = (bf16[7,7,48,1280]{3,2,1,0:T(8,128)(2,1)}, bf16[7,7,48,512]{3,2,1,0:T(8,128)(2,1)}, f32[7,7,48,384]{3,2,1,0:T(8,128)}, bf16[7,7,48,1024]{3,2,1,0...) custom-call(bf16[12,7,7,4,1024]{4,3,2,1,0:T(4,128)(2,1)} %bitcast.26, ...), custom_call_target="tpu_custom_call" | custom-call | tf_op jit(solution)/shard_map/first_pass/pallas_call | solution.py:1334
  33.9 26.1 %second_pass.1 = (bf16[9,9,48,384]{3,2,1,0:T(8,128)(2,1)}, f32[7,7,48,384]{3,2,1,0:T(8,128)}, f32[2,1408]{1,0:T(2,128)}, f32[7,48,384]{2,1,0:T(8,128)}, f32[7,48...) custom-call(f32[7,7,48,384]{3,2,1,0:T(8,128)} %get-tuple-element.87.z1_hbm.z1, ...), custom_call_target="tpu_custom_call" | custom-call | tf_op jit(solution)/shard_map/second_pass/pallas_call | solution.py:1355
  60.1 19.0 %third_pass.1 = (bf16[7,7,48,384]{3,2,1,0:T(8,128)(2,1)}, f32[2,1152]{1,0:T(2,128)}, bf16[7,7,48,512]{3,2,1,0:T(8,128)(2,1)}) custom-call(f32[7,7,48,384]{3,2,1,0:T(8,128)} %get-tuple-element.95.z2.z2_hbm, f32[2,1408]{1,0:T(2,128)} %get-tuple-element.96.mom.mom2, f32[4,1,384]{2,1,0:T(1,128)} %get-tuple-element.92.mids, f32[48,128]{1,0:T(8,128)} %get-tuple-element.84.m, ...), custom_call_target="tpu_custom_call" | custom-call | tf_op jit(solution)/shard_map/third_pass/pallas_call | solution.py:1372
  79.1 25.0 %fourth_pass.1 = (bf16[12,7,7,4,1024]{4,3,2,1,0:T(4,128)(2,1)}, bf16[4,7,7,48,128]{4,3,2,1,0:T(8,128)(2,1)}, f32[7,7,48,1024]{3,2,1,0:T(8,128)}, f32[7,7,48,512]{3,2,1,0:T(8,128)}, f32[1,3328]{1,0:T(1,128)}) custom-call(bf16[7,7,48,384]{3,2,1,0:T(8,128)(2,1)} %get-tuple-element.97.a2, bf16[7,7,48,1024]{3,2,1,0:T(8,128)(2,1)} %get-tuple-element.98.zp, ...), custom_call_target="tpu_custom_call" | custom-call | tf_op jit(solution)/shard_map/fourth_pass/pallas_call | solution.py:1385
  104.0 29.8 %fifth_pass.1 = (bf16[7,7,48,1024]{3,2,1,0:T(8,128)(2,1)}, f32[7,7,48,384]{3,2,1,0:T(8,128)}, f32[1,768]{1,0:T(1,128)}, f32[7,48,384]{2,1,0:T(8,128)}, f32[7,48,...) custom-call(f32[7,7,48,1024]{3,2,1,0:T(8,128)} %get-tuple-element.109.gs, ...), custom_call_target="tpu_custom_call" | custom-call | tf_op jit(solution)/shard_map/fifth_pass/pallas_call | solution.py:1420
  133.8 34.9 %sixth_pass.1 = (f32[7,7,48,384]{3,2,1,0:T(8,128)}, f32[1,768]{1,0:T(1,128)}, bf16[2560,256]{1,0:T(8,128)(2,1)}, bf16[192,256]{1,0:T(8,128)(2,1)}) custom-call(f32[7,7,48,384]{3,2,1,0:T(8,128)} %get-tuple-element.114.q2_hbm, f32[7,7,48,384]{3,2,1,0:T(8,128)} %get-tuple-element.95.z2.z2_hbm, f32[7,7,48,384]{3,2,1,0:T(8,128)} %get-tuple-element.87.z1_hbm.z1, ...), custom_call_target="tpu_custom_call" | custom-call | tf_op jit(solution)/shard_map/sixth_pass/pallas_call | solution.py:1446
  168.7 76.1 %seventh_pass.1 = (bf16[12,7,7,4,1024]{4,3,2,1,0:T(4,128)(2,1)}, bf16[4,7,7,48,128]{4,3,2,1,0:T(8,128)(2,1)}, bf16[6144,256]{1,0:T(8,128)(2,1)}, bf16[2560,256]{...) custom-call(f32[7,7,48,384]{3,2,1,0:T(8,128)} %get-tuple-element.125.q1, ...), custom_call_target="tpu_custom_call" | custom-call | tf_op jit(solution)/shard_map/seventh_pass/pallas_call | solution.py:1476
  244.8 17.4 %finish_outputs.1 = (bf16[12,7,7,4,1024]{4,3,2,1,0:T(4,128)(2,1)}, bf16[4,7,7,48,128]{4,3,2,1,0:T(8,128)(2,1)}, bf16[12,7,7,4,1024]{4,3,2,1,0:T(4,128)(2,1)}, bf...) custom-call(bf16[12,7,7,4,1024]{4,3,2,1,0:T(4,128)(2,1)} %get-tuple-, ...), custom_call_target="tpu_custom_call" | custom-call | tf_op jit(solution)/shard_map/finish_outputs/pallas_call | solution.py:1516

commit v6 on v5

--- a/solution.py
+++ b/solution.py
@@ -262,8 +262,7 @@
     def _():
         joined = keep[i - high].reshape(rows, C_JOIN)
         zp = dot(joined, wp[...]).reshape(cols, slab, C_IN)
-        add_moments(i == high, ((MIX, zp, 0),), m, here, base, one, two)
-        zp_out[...] = (zp - base[:, MIX:]).astype(bf16)
+        add_moments(i == high, ((MIX, zp, 0),), m, here, base, one, two, zp_out)
 
     @pl.when(i == 2 * high - 1)
     def _():
@@ -283,7 +282,7 @@
         line[...] = block[...]
 
 
-def add_moments(first, parts, m, here, base, one, two):
+def add_moments(first, parts, m, here, base, one, two, kept=None):
     @pl.when(first)
     def _():
         for at, z, fast in parts:
@@ -297,7 +296,10 @@
 
     for at, z, _ in parts:
         width = z.shape[-1]
-        off = (z - base[:, at : at + width]) * spread(m[...], width)
+        off = z - base[:, at : at + width]
+        if kept is not None:
+            kept[...] = off.astype(bf16)
+        off = off * spread(m[...], width)
         one[:, at : at + width] += rows_sum(off)
         two[:, at : at + width] += rows_sum(off * off)
 
@@ -362,10 +364,13 @@
             slow = jnp.zeros((rows, C_MID), f32)
             fast = jnp.zeros((rows, 128), f32)
             for a in range(3):
-                for c in range(3):
-                    v = a_out[h + a, c : c + cols].reshape(rows, MIX)
-                    slow = slow + dot(v[:, :C_MID], wb[a, c])
-                    fast = fast + dot(v[:, C_MID:], wfb[3 * a + c])
+                v = [a_out[h + a, c : c + cols].reshape(rows, MIX) for c in range(3)]
+                slow = slow + dot(
+                    jnp.concatenate([u[:, :C_MID] for u in v], axis=1), wb[a].reshape(3 * C_MID, C_MID)
+                )
+                fast = fast + dot(
+                    jnp.concatenate([u[:, C_MID:] for u in v], axis=1), wfb[3 * a : 3 * a + 3].reshape(3 * 128, 128)
+                )
             z_out[h, :, :, :C_MID] = slow.reshape(cols, slab, C_MID)
             z_out[h, :, :, C_MID:] = fast.reshape(cols, slab, 128)
             return carry
@@ -727,10 +732,15 @@
             slow = jnp.zeros((rows, C_MID), f32)
             fast = jnp.zeros((rows, 128), f32)
             for a in range(3):
-                for c in range(3):
-                    v = wide[h + 2 - a, 2 - c : 2 - c + cols].reshape(rows, MIX)
-                    slow = slow + dot_nt(v[:, :C_MID], wb[a, c])
-                    fast = fast + dot_nt(v[:, C_MID:], wfb[3 * a + c])
+                v = [wide[h + 2 - a, 2 - c : 2 - c + cols].reshape(rows, MIX) for c in range(3)]
+                slow = slow + dot_nt(
+                    jnp.concatenate([u[:, :C_MID] for u in v], axis=1),
+                    jnp.concatenate([wb[a, c] for c in range(3)], axis=1),
+                )
+                fast = fast + dot_nt(
+                    jnp.concatenate([u[:, C_MID:] for u in v], axis=1),
+                    jnp.concatenate([wfb[3 * a + c] for c in range(3)], axis=1),
+                )
             grads = jnp.concatenate([slow, fast], axis=1).reshape(cols, slab, MIX)
             slope_back(grads, z1[h], mom1, mids[0], mids[1], m, q_out.at[h], sums)
             return carry
@@ -929,8 +939,8 @@
 
 SPACE_STEPS = (5, 9, 12, 15, 18, 18, 18, 18, 18, 18, 18)
 FIRST_STEPS = (5, 9, 12, 15, 18)
-HALF_STEPS = (12, 15, 18, 18, 18, 18, 18, 18, 18, 18, 18)
-LATE_STEPS = (15, 18, 18, 18, 18, 18, 18, 18, 18, 18, 18)
+HALF_STEPS = (12, 15, 17, 18, 18, 18, 18, 18, 18, 18, 18)
+LATE_STEPS = (15, 17, 18, 18, 18, 18, 18, 18, 18, 18, 18)
 
 
 def seventh_pass(clips, n_clip, early_sizes, space_sizes, half_sizes, late_sizes, q1, z1, dzp, gf, x, f, kept, space_hbm, mom1, tot6, inv,
@@ -1005,9 +1015,10 @@
         for k, v in enumerate((up, dz, down)):
             da[i, :, :, k * C_MID : (k + 1) * C_MID] = v[:, :, :C_MID].astype(bf16)
             df[i, :, :, k * 128 : (k + 1) * 128] = v[:, :, C_MID:].astype(bf16)
-        dlat = dot_nt(dzp[...].reshape(rows, C_IN), wp[C_IN:])
-        for k in range(3):
-            dlat = dlat + dot_nt(da[i, :, :, k * C_MID : (k + 1) * C_MID].reshape(rows, C_MID), wa[k, C_IN:])
+        dlat = dot_nt(
+            jnp.concatenate([dzp[...].reshape(rows, C_IN), da[i].reshape(rows, 3 * C_MID)], axis=1),
+            jnp.concatenate([wp[C_IN:]] + [wa[k, C_IN:] for k in range(3)], axis=1),
+        )
         dlat = dlat.astype(bf16).astype(f32).reshape(cols, slab, C_LAT)
         dl[i, :, :, :C_LAT] = dlat.astype(bf16)
         dl[i, :, :, C_LAT:] = sooner(dlat, clips).astype(bf16)
@@ -1056,9 +1067,10 @@
     @pl.when(i >= late)
     def _():
         h = i - late
-        dj = dot_nt(dzp[...].reshape(rows, C_IN), wp[:C_IN])
-        for k in range(3):
-            dj = dj + dot_nt(da[h, :, :, k * C_MID : (k + 1) * C_MID].reshape(rows, C_MID), wa[k, :C_IN])
+        dj = dot_nt(
+            jnp.concatenate([dzp[...].reshape(rows, C_IN), da[h].reshape(rows, 3 * C_MID)], axis=1),
+            jnp.concatenate([wp[:C_IN]] + [wa[k, :C_IN] for k in range(3)], axis=1),
+        )
         mask = spread(m[...], C_IN)
         dj = dj.reshape(cols, slab, C_IN)
         for w in range(cols):

time: 263 us -> 261 us (level)
  no operation moved by 1% of the time
where the time goes in v6:
time: 261 us; the launch traced here: 260 us
  Pallas kernels  259 us (99%)
    pallas_call x1, Pallas kernels, on_device(): pl.pallas_call(functools.partial(seventh_pass, clips, n_clip, early_sizes...  75.5 us
    pallas_call x1, Pallas kernels, on_device(): pl.pallas_call(functools.partial(sixth_pass, n_clip, early_sizes), grid=(...  34.8 us
    pallas_call x1, Pallas kernels, on_device(): pl.pallas_call(functools.partial(first_pass, clips, n_clip), grid=(2 * hi...  30.4 us
    pallas_call x1, Pallas kernels, on_device(): pl.pallas_call(functools.partial(fifth_pass, n_clip), grid=(high + steps,...  29.8 us
    pallas_call x1, Pallas kernels, on_device(): pl.pallas_call(functools.partial(fourth_pass, n_clip, clips), grid=(2 * h...  25 us
    pallas_call x1, Pallas kernels, on_device(): pl.pallas_call(functools.partial(second_pass, n_clip), grid=(high + 1,),...  24.9 us
    pallas_call x1, Pallas kernels, on_device(): pl.pallas_call(functools.partial(third_pass, n_clip), grid=(2 * high,), i...  19 us
    pallas_call x1, Pallas kernels, on_device(): pl.pallas_call(finish_outputs, grid=(high,), in_specs=maps + [vm] * 7, ou...  17.4 us

profile of v6, /device:TPU:0, one launch (start us, length us, event | category | flops | bytes accessed | tf_op | source)
XLA Modules:
  0.0 259.5 jit_solution(12655425890332719244)
XLA Ops:
  0.6 1.9 prepare.1
  2.5 30.4 %first_pass.1 = (bf16[7,7,48,1280]{3,2,1,0:T(8,128)(2,1)}, bf16[7,7,48,512]{3,2,1,0:T(8,128)(2,1)}, f32[7,7,48,384]{3,2,1,0:T(8,128)}, bf16[7,7,48,1024]{3,2,1,0...) custom-call(bf16[12,7,7,4,1024]{4,3,2,1,0:T(4,128)(2,1)} %bitcast.26, ...), custom_call_target="tpu_custom_call" | custom-call | tf_op jit(solution)/shard_map/first_pass/pallas_call | solution.py:1346
  32.9 24.9 %second_pass.1 = (bf16[9,9,48,384]{3,2,1,0:T(8,128)(2,1)}, f32[7,7,48,384]{3,2,1,0:T(8,128)}, f32[2,1408]{1,0:T(2,128)}, f32[7,48,384]{2,1,0:T(8,128)}, f32[7,48...) custom-call(f32[7,7,48,384]{3,2,1,0:T(8,128)} %get-tuple-element.87.z1_hbm.z1, ...), custom_call_target="tpu_custom_call" | custom-call | tf_op jit(solution)/shard_map/second_pass/pallas_call | solution.py:1367
  57.9 19.0 %third_pass.1 = (bf16[7,7,48,384]{3,2,1,0:T(8,128)(2,1)}, f32[2,1152]{1,0:T(2,128)}, bf16[7,7,48,512]{3,2,1,0:T(8,128)(2,1)}) custom-call(f32[7,7,48,384]{3,2,1,0:T(8,128)} %get-tuple-element.95.z2.z2_hbm, f32[2,1408]{1,0:T(2,128)} %get-tuple-element.96.mom.mom2, f32[4,1,384]{2,1,0:T(1,128)} %get-tuple-element.92.mids, f32[48,128]{1,0:T(8,128)} %get-tuple-element.84.m, ...), custom_call_target="tpu_custom_call" | custom-call | tf_op jit(solution)/shard_map/third_pass/pallas_call | solution.py:1384
  76.9 25.0 %fourth_pass.1 = (bf16[12,7,7,4,1024]{4,3,2,1,0:T(4,128)(2,1)}, bf16[4,7,7,48,128]{4,3,2,1,0:T(8,128)(2,1)}, f32[7,7,48,1024]{3,2,1,0:T(8,128)}, f32[7,7,48,512]{3,2,1,0:T(8,128)}, f32[1,3328]{1,0:T(1,128)}) custom-call(bf16[7,7,48,384]{3,2,1,0:T(8,128)(2,1)} %get-tuple-element.97.a2, bf16[7,7,48,1024]{3,2,1,0:T(8,128)(2,1)} %get-tuple-element.98.zp, ...), custom_call_target="tpu_custom_call" | custom-call | tf_op jit(solution)/shard_map/fourth_pass/pallas_call | solution.py:1397
  101.9 29.8 %fifth_pass.1 = (bf16[7,7,48,1024]{3,2,1,0:T(8,128)(2,1)}, f32[7,7,48,384]{3,2,1,0:T(8,128)}, f32[1,768]{1,0:T(1,128)}, f32[7,48,384]{2,1,0:T(8,128)}, f32[7,48,...) custom-call(f32[7,7,48,1024]{3,2,1,0:T(8,128)} %get-tuple-element.109.gs, ...), custom_call_target="tpu_custom_call" | custom-call | tf_op jit(solution)/shard_map/fifth_pass/pallas_call | solution.py:1432
  131.6 34.8 %sixth_pass.1 = (f32[7,7,48,384]{3,2,1,0:T(8,128)}, f32[1,768]{1,0:T(1,128)}, bf16[2560,256]{1,0:T(8,128)(2,1)}, bf16[192,256]{1,0:T(8,128)(2,1)}) custom-call(f32[7,7,48,384]{3,2,1,0:T(8,128)} %get-tuple-element.114.q2_hbm, f32[7,7,48,384]{3,2,1,0:T(8,128)} %get-tuple-element.95.z2.z2_hbm, f32[7,7,48,384]{3,2,1,0:T(8,128)} %get-tuple-element.87.z1_hbm.z1, ...), custom_call_target="tpu_custom_call" | custom-call | tf_op jit(solution)/shard_map/sixth_pass/pallas_call | solution.py:1458
  166.5 75.5 %seventh_pass.1 = (bf16[12,7,7,4,1024]{4,3,2,1,0:T(4,128)(2,1)}, bf16[4,7,7,48,128]{4,3,2,1,0:T(8,128)(2,1)}, bf16[6144,256]{1,0:T(8,128)(2,1)}, bf16[2560,256]{...) custom-call(f32[7,7,48,384]{3,2,1,0:T(8,128)} %get-tuple-element.125.q1, ...), custom_call_target="tpu_custom_call" | custom-call | tf_op jit(solution)/shard_map/seventh_pass/pallas_call | solution.py:1488
  241.9 17.4 %finish_outputs.1 = (bf16[12,7,7,4,1024]{4,3,2,1,0:T(4,128)(2,1)}, bf16[4,7,7,48,128]{4,3,2,1,0:T(8,128)(2,1)}, bf16[12,7,7,4,1024]{4,3,2,1,0:T(4,128)(2,1)}, bf...) custom-call(bf16[12,7,7,4,1024]{4,3,2,1,0:T(4,128)(2,1)} %get-tuple-, ...), custom_call_target="tpu_custom_call" | custom-call | tf_op jit(solution)/shard_map/finish_outputs/pallas_call | solution.py:1528

commit v7 on v6

--- a/solution.py
+++ b/solution.py
@@ -205,9 +205,9 @@
     ]
 
 
-def first_pass(clips, n_clip, xs, xf, m, perm, wl, wa, wp, wfa, weight,
+def first_pass(clips, n_clip, xs, xf, m, perm, wl, wa, wp_hbm, wfa, weight,
                x_out, f_out, z_out, zp_out, st_out, base_out, mom, row, col, corner,
-               keep, taps, ends, base, one, two, line, side, *refs):
+               wp, wp_sem, keep, taps, ends, base, one, two, line, side, *refs):
     i = pl.program_id(0)
     cols = xs.shape[1]
     slab = m.shape[0]
@@ -217,8 +217,12 @@
     here = cols * jnp.sum(m[...], axis=0, keepdims=True)
     count = high * here
 
+    def fetch_wp():
+        return pltpu.make_async_copy(wp_hbm, wp, wp_sem.at[0])
+
     @pl.when(i == 0)
     def _():
+        fetch_wp().start()
         ex.signal()
         frames_matrix(wfa, taps, ends)
 
@@ -253,6 +257,7 @@
         ex.meet()
         ex.send_near()
         ex.send_rims(line, side)
+        fetch_wp().wait()
 
     @pl.when(i == high + 2)
     def _():
@@ -324,7 +329,7 @@
 
 
 def second_pass(n_clip, z1_hbm, row, col, corner, mom, mids, m, wb, wfb, stp, weight, cot,
-                a_out, z_out, mom_out, zrow, zcol, zcorner, cot_out, z1, z1_sem, one, two, *refs):
+                a_hbm, z_hbm, mom_out, zrow, zcol, zcorner, cot_out, a_out, z_out, save_sem, z1, z1_sem, one, two, *refs):
     i = pl.program_id(0)
     high, cols, slab, _ = z1.shape
     rows = cols * slab
@@ -332,6 +337,10 @@
 
     def fetch(h):
         return pltpu.make_async_copy(z1_hbm.at[h], z1.at[h], z1_sem.at[h])
+
+    def save(k):
+        source, target = ((a_out, a_hbm), (z_out, z_hbm))[k]
+        return pltpu.make_async_copy(source, target, save_sem.at[k])
 
     @pl.when(i == 0)
     def _():
@@ -394,6 +403,8 @@
         ex.meet()
         ex.send_near()
         ex.send_rims(z_out.at[(high - 1) * (1 - ex.ha)], z_out.at[:, (cols - 1) * (1 - ex.wa)])
+        save(0).start()
+        save(1).start()
 
     @pl.when(i == 3)
     def _():
@@ -409,6 +420,8 @@
     def _():
         ex.finish(mom_out, weight)
         ex.finish_rims((zrow, zcol, zcorner))
+        save(0).wait()
+        save(1).wait()
 
 
 def third_pass(n_clip, z2, mom, mids, m, wc, wfc, weight, fcot, perm,
@@ -670,8 +683,8 @@
 
 
 def sixth_pass(n_clip, early_sizes, q2_hbm, z2_hbm, z1_hbm, a1_hbm, qrow, qcol, qcorner, zrow, zcol, zcorner, mom1, mom2, tot5, inv,
-               mids, m, wb, wfb, weight, dwfc, w_hbm, q_out, tot, wb_out, kept_out,
-               fast_sums, wide, q2, z2, z1, a1, q2_sem, z2_sem, z1_sem, a1_sem, sums, mine, land, *refs):
+               mids, m, wb, wfb, weight, dwfc, w_hbm, q_hbm, tot, wb_out, kept_out,
+               q_out, fast_sums, wide, q2, z2, z1, a1, q2_sem, z2_sem, z1_sem, a1_sem, sums, mine, land, *refs):
     i = pl.program_id(0)
     high, cols, slab, _ = z1.shape
     rows = cols * slab
@@ -681,6 +694,9 @@
 
     def fetch_w():
         return pltpu.make_async_copy(w_hbm, mine, a1_sem.at[1])
+
+    def save_q():
+        return pltpu.make_async_copy(q_out, q_hbm, a1_sem.at[2])
 
     moved = ((q2_hbm, q2, q2_sem), (z2_hbm, z2, z2_sem), (z1_hbm, z1, z1_sem))
 
@@ -750,6 +766,7 @@
         lax.fori_loop(3, high, space, 0)
         ex.part[...] = sums[...]
         ex.send_near()
+        save_q().start()
         fetch_a1().wait()
 
     @pl.when(i == 3)
@@ -779,6 +796,7 @@
         for k in range(4, end + 1):
             early.gather(k)
         early.export(kept_out)
+        save_q().wait()
         for q in range(10):
             r, c, width = small_place(q)
             wb_out[r : r + C_FMID, c : c + width] = (fast_sums[q] if q < 9 else dwfc[...]).astype(bf16)
@@ -943,9 +961,9 @@
 LATE_STEPS = (15, 17, 18, 18, 18, 18, 18, 18, 18, 18, 18)
 
 
-def seventh_pass(clips, n_clip, early_sizes, space_sizes, half_sizes, late_sizes, q1, z1, dzp, gf, x, f, kept, space_hbm, mom1, tot6, inv,
+def seventh_pass(clips, n_clip, early_sizes, space_sizes, half_sizes, late_sizes, q1, z1, dzp, gf, x, f_hbm, kept, space_hbm, mom1, tot6, inv,
                  mids, m, perm, wl, wa, wp, wfa, sx, fx, out1, out_b, out_h, out_a,
-                 done1, done_b, done_h, done_a, da, dl, df, taps, ends, mine_b, land_b, mine_h, land_h, mine_a, land_a, load_sem, *sems):
+                 f, done1, done_b, done_h, done_a, da, dl, df, taps, ends, mine_b, land_b, mine_h, land_h, mine_a, land_a, load_sem, *sems):
     i = pl.program_id(0)
     cols, slab, _ = q1.shape
     high = da.shape[0]
@@ -960,10 +978,14 @@
     last = Reducer(n_clip, late_sizes, mine_a, land_a, done_a, [next(sems) for _ in range(4)])
     end = last.stages - 1
 
+    def fetch_f():
+        return pltpu.make_async_copy(f_hbm, f, load_sem.at[4])
+
     @pl.when(i == 0)
     def _():
         load = pltpu.make_async_copy(space_hbm, mine_b, load_sem.at[0])
         load.start()
+        fetch_f().start()
         greet_signal(n_clip)
         frames_matrix(wfa, taps, ends)
         first.load(kept)
@@ -1045,6 +1067,7 @@
 
     @pl.when(i == late - 1)
     def _():
+        fetch_f().wait()
         fast = f[...].reshape(every, WIDE_FAST)
         d = dl[...].reshape(every, 2 * C_LAT)
         at = 9 * C_MID
@@ -1346,7 +1369,7 @@
     x, f, z1, zp, stp, base, mom1, row1, col1, corner1 = pl.pallas_call(
         functools.partial(first_pass, clips, n_clip),
         grid=(2 * high,),
-        in_specs=[slow_block(early), fast_block(early)] + [vm] * 7,
+        in_specs=[slow_block(early), fast_block(early)] + [vm] * 4 + [hbm] + [vm] * 2,
         out_specs=(
             early_line((cols, slab, C_JOIN)), early_line((cols, slab, WIDE_FAST)), early_line((cols, slab, MIX)),
             late_line((cols, slab, C_IN), high), vm, vm, vm, vm, vm, vm,
@@ -1356,6 +1379,7 @@
             shaped((1, C_IN), f32), shaped((2, MIX), f32),
         ) + rim_shapes,
         scratch_shapes=[
+            pltpu.VMEM((C_JOIN, C_IN), bf16), pltpu.SemaphoreType.DMA((1,)),
             pltpu.VMEM((high, cols, slab, C_JOIN), bf16), pltpu.VMEM((128, WIDE_FAST), bf16),
             pltpu.VMEM((2, 128, C_FAST), bf16), pltpu.VMEM((1, L1), f32), pltpu.VMEM((1, L1), f32),
             pltpu.VMEM((1, L1), f32),
@@ -1368,11 +1392,13 @@
         functools.partial(second_pass, n_clip),
         grid=(high + 1,),
         in_specs=[hbm] + [vm] * 10 + [slow_block(after(1))],
-        out_specs=(vm, vm, vm, vm, vm, vm, late_line((cols, slab, C_IN), 1)),
+        out_specs=(hbm, hbm, vm, vm, vm, vm, late_line((cols, slab, C_IN), 1)),
         out_shape=(
             shaped((high + 2, cols + 2, slab, MIX), bf16), lines(MIX, f32), shaped((2, L1), f32),
         ) + rim_shapes + (lines(C_IN, bf16),),
         scratch_shapes=[
+            pltpu.VMEM((high + 2, cols + 2, slab, MIX), bf16), pltpu.VMEM((high, cols, slab, MIX), f32),
+            pltpu.SemaphoreType.DMA((2,)),
             pltpu.VMEM((high, cols, slab, MIX), f32), pltpu.SemaphoreType.DMA((high,)), pltpu.VMEM((1, MIX), f32),
             pltpu.VMEM((1, MIX), f32),
         ] + exchange_scratch(n_clip, 2, L1) + rims,
@@ -1459,16 +1485,19 @@
         functools.partial(sixth_pass, n_clip, early_sizes),
         grid=(10,),
         in_specs=[hbm] * 4 + [vm] * 16 + [hbm],
-        out_specs=(vm,) * 4,
+        out_specs=(hbm,) + (vm,) * 3,
         out_shape=(
             lines(MIX, f32), shaped((1, 2 * MIX), f32), shaped((sum(space_sizes), 256), bf16),
             shaped((sum(Reducer.layout(n_clip, early_sizes)[2]), 256), bf16),
         ),
-        scratch_shapes=[pltpu.VMEM((9, C_FMID, C_FMID), f32), pltpu.VMEM((high + 2, cols + 2, slab, MIX), bf16)]
+        scratch_shapes=[
+            pltpu.VMEM((high, cols, slab, MIX), f32), pltpu.VMEM((9, C_FMID, C_FMID), f32),
+            pltpu.VMEM((high + 2, cols + 2, slab, MIX), bf16),
+        ]
         + [pltpu.VMEM((high, cols, slab, MIX), f32)] * 3
         + [pltpu.VMEM((high + 2, cols + 2, slab, MIX), bf16)]
         + [pltpu.SemaphoreType.DMA((high,))] * 3
-        + [pltpu.SemaphoreType.DMA((2,)), pltpu.VMEM((1, 2 * MIX), f32)]
+        + [pltpu.SemaphoreType.DMA((3,)), pltpu.VMEM((1, 2 * MIX), f32)]
         + [pltpu.VMEM((sum(early_sizes), 256), bf16), Reducer.scratch(n_clip, early_sizes)]
         + exchange_scratch(n_clip, 1, 2 * MIX) + Reducer.sems(n_clip, early_sizes, 2),
         compiler_params=remote(6),
@@ -1491,14 +1520,14 @@
         in_specs=[
             early_line((cols, slab, MIX)), early_line((cols, slab, MIX)), twice_line((cols, slab, C_IN)),
             late_line((cols, slab, WIDE_FAST), high + steps),
-            pl.BlockSpec((n, slab, C_MID), lambda i: (0, 0, jnp.clip(i - high, 0, steps - 1))), vm, vm, hbm,
+            pl.BlockSpec((n, slab, C_MID), lambda i: (0, 0, jnp.clip(i - high, 0, steps - 1))), hbm, vm, hbm,
         ] + [vm] * 10,
         out_specs=(slow_block(after(high + steps)), fast_block(after(high + steps)), hbm, hbm, hbm, hbm),
         out_shape=(
             shaped(xs.shape, bf16), shaped(xf.shape, bf16), shaped((sum(early_sizes), 256), bf16),
             shaped((sum(space_sizes), 256), bf16), shaped((sum(half_sizes), 256), bf16), shaped((sum(late_sizes), 256), bf16),
         ),
-        scratch_shapes=[
+        scratch_shapes=[pltpu.VMEM((n, slab, WIDE_FAST), bf16)] + [
             pltpu.VMEM((sum(v), 256), bf16) for v in (early_sizes, space_sizes, half_sizes, late_sizes)
         ] + [
             pltpu.VMEM((high, cols, slab, 3 * C_MID), bf16), pltpu.VMEM((high, cols, slab, 2 * C_LAT), bf16),
@@ -1506,7 +1535,7 @@
             pltpu.VMEM((2, 128, C_FAST), bf16), pltpu.VMEM((sum(space_sizes), 256), bf16),
             Reducer.scratch(n_clip, space_sizes), pltpu.VMEM((sum(half_sizes), 256), bf16),
             Reducer.scratch(n_clip, half_sizes), pltpu.VMEM((sum(late_sizes), 256), bf16),
-            Reducer.scratch(n_clip, late_sizes), pltpu.SemaphoreType.DMA((4,)),
+            Reducer.scratch(n_clip, late_sizes), pltpu.SemaphoreType.DMA((5,)),
         ] + Reducer.sems(n_clip, early_sizes, 2) + Reducer.sems(n_clip, space_sizes) + Reducer.sems(n_clip, half_sizes)
         + Reducer.sems(n_clip, late_sizes),
         compiler_params=remote(7),

time: 261 us -> 255 us (0.977)
  Pallas kernels: 259 us -> 254 us
where the time goes in v7:
time: 255 us; the launch traced here: 254 us
  Pallas kernels  254 us (100%)
    pallas_call x1, Pallas kernels, on_device(): pl.pallas_call(functools.partial(seventh_pass, clips, n_clip, early_sizes...  74.5 us
    pallas_call x1, Pallas kernels, on_device(): pl.pallas_call(functools.partial(sixth_pass, n_clip, early_sizes), grid=(...  33.7 us
    pallas_call x1, Pallas kernels, on_device(): pl.pallas_call(functools.partial(fifth_pass, n_clip), grid=(high + steps,...  29.8 us
    pallas_call x1, Pallas kernels, on_device(): pl.pallas_call(functools.partial(first_pass, clips, n_clip), grid=(2 * hi...  29.4 us
    pallas_call x1, Pallas kernels, on_device(): pl.pallas_call(functools.partial(fourth_pass, n_clip, clips), grid=(2 * h...  25 us
    pallas_call x1, Pallas kernels, on_device(): pl.pallas_call(functools.partial(second_pass, n_clip), grid=(high + 1,),...  22.9 us
    pallas_call x1, Pallas kernels, on_device(): pl.pallas_call(functools.partial(third_pass, n_clip), grid=(2 * high,), i...  19 us
    pallas_call x1, Pallas kernels, on_device(): pl.pallas_call(finish_outputs, grid=(high,), in_specs=maps + [vm] * 7, ou...  17.4 us

profile of v7, /device:TPU:0, one launch (start us, length us, event | category | flops | bytes accessed | tf_op | source)
XLA Modules:
  0.0 254.4 jit_solution(10543055760471007297)
XLA Ops:
  0.6 1.9 prepare.1
  2.5 29.4 %first_pass.1 = (bf16[7,7,48,1280]{3,2,1,0:T(8,128)(2,1)}, bf16[7,7,48,512]{3,2,1,0:T(8,128)(2,1)}, f32[7,7,48,384]{3,2,1,0:T(8,128)}, bf16[7,7,48,1024]{3,2,1,0...) custom-call(bf16[12,7,7,4,1024]{4,3,2,1,0:T(4,128)(2,1)} %bitcast.26, ...), custom_call_target="tpu_custom_call" | custom-call | tf_op jit(solution)/shard_map/first_pass/pallas_call | solution.py:1369
  32.0 22.9 %second_pass.1 = (bf16[9,9,48,384]{3,2,1,0:T(8,128)(2,1)}, f32[7,7,48,384]{3,2,1,0:T(8,128)}, f32[2,1408]{1,0:T(2,128)}, f32[7,48,384]{2,1,0:T(8,128)}, f32[7,48...) custom-call(f32[7,7,48,384]{3,2,1,0:T(8,128)} %get-tuple-element.87.z1_hbm.z1, ...), custom_call_target="tpu_custom_call" | custom-call | tf_op jit(solution)/shard_map/second_pass/pallas_call | solution.py:1391
  54.8 19.0 %third_pass.1 = (bf16[7,7,48,384]{3,2,1,0:T(8,128)(2,1)}, f32[2,1152]{1,0:T(2,128)}, bf16[7,7,48,512]{3,2,1,0:T(8,128)(2,1)}) custom-call(f32[7,7,48,384]{3,2,1,0:T(8,128)} %get-tuple-element.95.z2.z2_hbm, f32[2,1408]{1,0:T(2,128)} %get-tuple-element.96.mom.mom2, f32[4,1,384]{2,1,0:T(1,128)} %get-tuple-element.92.mids, f32[48,128]{1,0:T(8,128)} %get-tuple-element.84.m, ...), custom_call_target="tpu_custom_call" | custom-call | tf_op jit(solution)/shard_map/third_pass/pallas_call | solution.py:1410
  73.8 25.0 %fourth_pass.1 = (bf16[12,7,7,4,1024]{4,3,2,1,0:T(4,128)(2,1)}, bf16[4,7,7,48,128]{4,3,2,1,0:T(8,128)(2,1)}, f32[7,7,48,1024]{3,2,1,0:T(8,128)}, f32[7,7,48,512]{3,2,1,0:T(8,128)}, f32[1,3328]{1,0:T(1,128)}) custom-call(bf16[7,7,48,384]{3,2,1,0:T(8,128)(2,1)} %get-tuple-element.97.a2, bf16[7,7,48,1024]{3,2,1,0:T(8,128)(2,1)} %get-tuple-element.98.zp, ...), custom_call_target="tpu_custom_call" | custom-call | tf_op jit(solution)/shard_map/fourth_pass/pallas_call | solution.py:1423
  98.8 29.8 %fifth_pass.1 = (bf16[7,7,48,1024]{3,2,1,0:T(8,128)(2,1)}, f32[7,7,48,384]{3,2,1,0:T(8,128)}, f32[1,768]{1,0:T(1,128)}, f32[7,48,384]{2,1,0:T(8,128)}, f32[7,48,...) custom-call(f32[7,7,48,1024]{3,2,1,0:T(8,128)} %get-tuple-element.109.gs, ...), custom_call_target="tpu_custom_call" | custom-call | tf_op jit(solution)/shard_map/fifth_pass/pallas_call | solution.py:1458
  128.6 33.7 %sixth_pass.1 = (f32[7,7,48,384]{3,2,1,0:T(8,128)}, f32[1,768]{1,0:T(1,128)}, bf16[2560,256]{1,0:T(8,128)(2,1)}, bf16[192,256]{1,0:T(8,128)(2,1)}) custom-call(f32[7,7,48,384]{3,2,1,0:T(8,128)} %get-tuple-element.114.q2_hbm, f32[7,7,48,384]{3,2,1,0:T(8,128)} %get-tuple-element.95.z2.z2_hbm, f32[7,7,48,384]{3,2,1,0:T(8,128)} %get-tuple-element.87.z1_hbm.z1, ...), custom_call_target="tpu_custom_call" | custom-call | tf_op jit(solution)/shard_map/sixth_pass/pallas_call | solution.py:1484
  162.3 74.5 %seventh_pass.1 = (bf16[12,7,7,4,1024]{4,3,2,1,0:T(4,128)(2,1)}, bf16[4,7,7,48,128]{4,3,2,1,0:T(8,128)(2,1)}, bf16[6144,256]{1,0:T(8,128)(2,1)}, bf16[2560,256]{...) custom-call(f32[7,7,48,384]{3,2,1,0:T(8,128)} %get-tuple-element.125.q1, ...), custom_call_target="tpu_custom_call" | custom-call | tf_op jit(solution)/shard_map/seventh_pass/pallas_call | solution.py:1517
  236.8 17.4 %finish_outputs.1 = (bf16[12,7,7,4,1024]{4,3,2,1,0:T(4,128)(2,1)}, bf16[4,7,7,48,128]{4,3,2,1,0:T(8,128)(2,1)}, bf16[12,7,7,4,1024]{4,3,2,1,0:T(4,128)(2,1)}, bf...) custom-call(bf16[12,7,7,4,1024]{4,3,2,1,0:T(4,128)(2,1)} %get-tuple-, ...), custom_call_target="tpu_custom_call" | custom-call | tf_op jit(solution)/shard_map/finish_outputs/pallas_call | solution.py:1557

commit v8 on v7

--- a/solution.py
+++ b/solution.py
@@ -962,8 +962,8 @@
 
 
 def seventh_pass(clips, n_clip, early_sizes, space_sizes, half_sizes, late_sizes, q1, z1, dzp, gf, x, f_hbm, kept, space_hbm, mom1, tot6, inv,
-                 mids, m, perm, wl, wa, wp, wfa, sx, fx, out1, out_b, out_h, out_a,
-                 f, done1, done_b, done_h, done_a, da, dl, df, taps, ends, mine_b, land_b, mine_h, land_h, mine_a, land_a, load_sem, *sems):
+                 mids, m, perm, wl, wa_hbm, wp_hbm, wfa, sx, fx, out1, out_b, out_h, out_a,
+                 wa, wp, f, done1, done_b, done_h, done_a, da, dl, df, taps, ends, mine_b, land_b, mine_h, land_h, mine_a, land_a, load_sem, *sems):
     i = pl.program_id(0)
     cols, slab, _ = q1.shape
     high = da.shape[0]
@@ -981,10 +981,16 @@
     def fetch_f():
         return pltpu.make_async_copy(f_hbm, f, load_sem.at[4])
 
+    def fetch_weight(k):
+        source, target = ((wp_hbm, wp), (wa_hbm, wa))[k]
+        return pltpu.make_async_copy(source, target, load_sem.at[5 + k])
+
     @pl.when(i == 0)
     def _():
         load = pltpu.make_async_copy(space_hbm, mine_b, load_sem.at[0])
         load.start()
+        fetch_weight(0).start()
+        fetch_weight(1).start()
         fetch_f().start()
         greet_signal(n_clip)
         frames_matrix(wfa, taps, ends)
@@ -993,6 +999,8 @@
         first.spread(end)
         load.wait()
         space.send(0)
+        fetch_weight(0).wait()
+        fetch_weight(1).wait()
 
     plan, rest = {}, []
     final = pl.num_programs(0) - 1
@@ -1145,17 +1153,28 @@
     pl.semaphore_wait(pltpu.get_barrier_semaphore(), len(stage_orders(n_clip, 1)[0]))
 
 
-def finish_outputs(so, fo, sx, fx, done1, done_b, done_h, done_a, tot4, tot5, tot6, so_out, fo_out, sx_out, fx_out,
+def finish_outputs(so, fo, sx, fx, in1, in_b, in_h, in_a, tot4, tot5, tot6, so_out, fo_out, sx_out, fx_out,
                    wp_hbm, wc_hbm, wb_hbm, wa_hbm, wl_hbm, wfa_out, wfc_out, wfb_out, sgain_out, sshift_out, fgain_out,
-                   fshift_out, wp, wc, wb, wa, wl, sem):
+                   fshift_out, wp, wc, wb, wa, wl, done1, done_b, done_h, done_a, sem, in_sem):
     i = pl.program_id(0)
     moves = ((wp, wp_hbm), (wc, wc_hbm), (wb, wb_hbm), (wa, wa_hbm), (wl, wl_hbm))
 
+    loads = ((in1, done1), (in_b, done_b), (in_h, done_h), (in_a, done_a))
+
     def move(k):
         return pltpu.make_async_copy(moves[k][0], moves[k][1], sem.at[k])
 
+    def load(k):
+        return pltpu.make_async_copy(loads[k][0], loads[k][1], in_sem.at[k])
+
     @pl.when(i == 0)
     def _():
+        for k in range(4):
+            load(k).start()
+
+    @pl.when(i == 1)
+    def _():
+        load(0).wait()
         for b in range(C_IN // 256):
             wp[:, b * 256 : (b + 1) * 256] = done1[b * C_JOIN : (b + 1) * C_JOIN, :].astype(f32)
         move(0).start()
@@ -1164,14 +1183,17 @@
             wc[:, b * 256 : (b + 1) * 256] = done1[at : at + C_MID, :].astype(f32)
         move(1).start()
 
-    @pl.when(i == 1)
-    def _():
+    @pl.when(i == 2)
+    def _():
+        load(1).wait()
         for t in range(9):
             wb[t // 3, t % 3] = done_b[t * C_MID : (t + 1) * C_MID, :].astype(f32)
         move(2).start()
 
-    @pl.when(i == 2)
-    def _():
+    @pl.when(i == 3)
+    def _():
+        load(2).wait()
+        load(3).wait()
         for k in range(3):
             wa[k, : 2 * C_MID] = done_h[2 * k * C_MID : 2 * (k + 1) * C_MID, :].astype(f32)
             wa[k, 2 * C_MID :] = done_a[3 * k * C_MID : 3 * (k + 1) * C_MID, :].astype(f32)
@@ -1181,7 +1203,7 @@
             wl[k] = done_a[at + k * C_FAST : at + (k + 1) * C_FAST, :].astype(f32)
         move(4).start()
 
-    @pl.when(i == 3)
+    @pl.when(i == 4)
     def _():
         at = 9 * C_MID + 5 * C_FAST
         for q in range(3):
@@ -1521,13 +1543,15 @@
             early_line((cols, slab, MIX)), early_line((cols, slab, MIX)), twice_line((cols, slab, C_IN)),
             late_line((cols, slab, WIDE_FAST), high + steps),
             pl.BlockSpec((n, slab, C_MID), lambda i: (0, 0, jnp.clip(i - high, 0, steps - 1))), hbm, vm, hbm,
-        ] + [vm] * 10,
+        ] + [vm] * 7 + [hbm, hbm, vm],
         out_specs=(slow_block(after(high + steps)), fast_block(after(high + steps)), hbm, hbm, hbm, hbm),
         out_shape=(
             shaped(xs.shape, bf16), shaped(xf.shape, bf16), shaped((sum(early_sizes), 256), bf16),
             shaped((sum(space_sizes), 256), bf16), shaped((sum(half_sizes), 256), bf16), shaped((sum(late_sizes), 256), bf16),
         ),
-        scratch_shapes=[pltpu.VMEM((n, slab, WIDE_FAST), bf16)] + [
+        scratch_shapes=[
+            pltpu.VMEM((3, C_JOIN, C_MID), bf16), pltpu.VMEM((C_JOIN, C_IN), bf16), pltpu.VMEM((n, slab, WIDE_FAST), bf16),
+        ] + [
             pltpu.VMEM((sum(v), 256), bf16) for v in (early_sizes, space_sizes, half_sizes, late_sizes)
         ] + [
             pltpu.VMEM((high, cols, slab, 3 * C_MID), bf16), pltpu.VMEM((high, cols, slab, 2 * C_LAT), bf16),
@@ -1535,7 +1559,7 @@
             pltpu.VMEM((2, 128, C_FAST), bf16), pltpu.VMEM((sum(space_sizes), 256), bf16),
             Reducer.scratch(n_clip, space_sizes), pltpu.VMEM((sum(half_sizes), 256), bf16),
             Reducer.scratch(n_clip, half_sizes), pltpu.VMEM((sum(late_sizes), 256), bf16),
-            Reducer.scratch(n_clip, late_sizes), pltpu.SemaphoreType.DMA((5,)),
+            Reducer.scratch(n_clip, late_sizes), pltpu.SemaphoreType.DMA((7,)),
         ] + Reducer.sems(n_clip, early_sizes, 2) + Reducer.sems(n_clip, space_sizes) + Reducer.sems(n_clip, half_sizes)
         + Reducer.sems(n_clip, late_sizes),
         compiler_params=remote(7),
@@ -1557,13 +1581,15 @@
     so, fo, sx, fx, dwp, dwc, dwb, dwa, dwl, dwfa, dwfc, dwfb, dsg, dss, dfg, dfs = pl.pallas_call(
         finish_outputs,
         grid=(high,),
-        in_specs=maps + [vm] * 7,
+        in_specs=maps + [hbm] * 4 + [vm] * 3,
         out_specs=tuple(maps) + (hbm,) * 5 + (vm,) * 7,
         out_shape=(shaped(xs.shape, bf16), shaped(xf.shape, bf16)) * 2 + weights + (
             shaped((3, C_FMID, C_FAST), f32), shaped((C_FMID, C_FAST), f32), shaped((9, C_FMID, C_FMID), f32),
             slow_rows, slow_rows, fast_row, fast_row,
         ),
-        scratch_shapes=[pltpu.VMEM(v.shape, f32) for v in weights] + [pltpu.SemaphoreType.DMA((5,))],
+        scratch_shapes=[pltpu.VMEM(v.shape, f32) for v in weights]
+        + [pltpu.VMEM((sum(v), 256), bf16) for v in (early_sizes, space_sizes, half_sizes, late_sizes)]
+        + [pltpu.SemaphoreType.DMA((5,)), pltpu.SemaphoreType.DMA((4,))],
         compiler_params=params(60),
         name="finish_outputs",
     )(so, fo, sx, fx, done1, done_b, done_h, done_a, tot4, tot5, tot6)

time: 255 us -> 253 us (level)
  Pallas kernels: 254 us -> 251 us
    pallas_call x1, Pallas kernels: 74.5 us -> 71.5 us  [on_device(): pl.pallas_call(functools.partial(seventh_pass, clips, n_clip, early_sizes...]
where the time goes in v8:
time: 253 us; the launch traced here: 252 us
  Pallas kernels  251 us (99%)
    pallas_call x1, Pallas kernels, on_device(): pl.pallas_call(functools.partial(seventh_pass, clips, n_clip, early_sizes...  71.5 us
    pallas_call x1, Pallas kernels, on_device(): pl.pallas_call(functools.partial(sixth_pass, n_clip, early_sizes), grid=(...  33.7 us
    pallas_call x1, Pallas kernels, on_device(): pl.pallas_call(functools.partial(fifth_pass, n_clip), grid=(high + steps,...  29.8 us
    pallas_call x1, Pallas kernels, on_device(): pl.pallas_call(functools.partial(first_pass, clips, n_clip), grid=(2 * hi...  29.4 us
    pallas_call x1, Pallas kernels, on_device(): pl.pallas_call(functools.partial(fourth_pass, n_clip, clips), grid=(2 * h...  25 us
    pallas_call x1, Pallas kernels, on_device(): pl.pallas_call(functools.partial(second_pass, n_clip), grid=(high + 1,),...  22.9 us
    pallas_call x1, Pallas kernels, on_device(): pl.pallas_call(functools.partial(third_pass, n_clip), grid=(2 * high,), i...  19 us
    pallas_call x1, Pallas kernels, on_device(): pl.pallas_call(finish_outputs, grid=(high,), in_specs=maps + [hbm] * 4 +...  17.7 us

profile of v8, /device:TPU:0, one launch (start us, length us, event | category | flops | bytes accessed | tf_op | source)
XLA Modules:
  0.0 251.8 jit_solution(17733382232491146451)
XLA Ops:
  0.6 1.9 prepare.1
  2.5 29.4 %first_pass.1 = (bf16[7,7,48,1280]{3,2,1,0:T(8,128)(2,1)}, bf16[7,7,48,512]{3,2,1,0:T(8,128)(2,1)}, f32[7,7,48,384]{3,2,1,0:T(8,128)}, bf16[7,7,48,1024]{3,2,1,0...) custom-call(bf16[12,7,7,4,1024]{4,3,2,1,0:T(4,128)(2,1)} %bitcast.26, ...), custom_call_target="tpu_custom_call" | custom-call | tf_op jit(solution)/shard_map/first_pass/pallas_call | solution.py:1391
  32.0 22.9 %second_pass.1 = (bf16[9,9,48,384]{3,2,1,0:T(8,128)(2,1)}, f32[7,7,48,384]{3,2,1,0:T(8,128)}, f32[2,1408]{1,0:T(2,128)}, f32[7,48,384]{2,1,0:T(8,128)}, f32[7,48...) custom-call(f32[7,7,48,384]{3,2,1,0:T(8,128)} %get-tuple-element.87.z1_hbm.z1, ...), custom_call_target="tpu_custom_call" | custom-call | tf_op jit(solution)/shard_map/second_pass/pallas_call | solution.py:1413
  54.8 19.0 %third_pass.1 = (bf16[7,7,48,384]{3,2,1,0:T(8,128)(2,1)}, f32[2,1152]{1,0:T(2,128)}, bf16[7,7,48,512]{3,2,1,0:T(8,128)(2,1)}) custom-call(f32[7,7,48,384]{3,2,1,0:T(8,128)} %get-tuple-element.95.z2.z2_hbm, f32[2,1408]{1,0:T(2,128)} %get-tuple-element.96.mom.mom2, f32[4,1,384]{2,1,0:T(1,128)} %get-tuple-element.92.mids, f32[48,128]{1,0:T(8,128)} %get-tuple-element.84.m, ...), custom_call_target="tpu_custom_call" | custom-call | tf_op jit(solution)/shard_map/third_pass/pallas_call | solution.py:1432
  73.8 25.0 %fourth_pass.1 = (bf16[12,7,7,4,1024]{4,3,2,1,0:T(4,128)(2,1)}, bf16[4,7,7,48,128]{4,3,2,1,0:T(8,128)(2,1)}, f32[7,7,48,1024]{3,2,1,0:T(8,128)}, f32[7,7,48,512]{3,2,1,0:T(8,128)}, f32[1,3328]{1,0:T(1,128)}) custom-call(bf16[7,7,48,384]{3,2,1,0:T(8,128)(2,1)} %get-tuple-element.97.a2, bf16[7,7,48,1024]{3,2,1,0:T(8,128)(2,1)} %get-tuple-element.98.zp, ...), custom_call_target="tpu_custom_call" | custom-call | tf_op jit(solution)/shard_map/fourth_pass/pallas_call | solution.py:1445
  98.8 29.8 %fifth_pass.1 = (bf16[7,7,48,1024]{3,2,1,0:T(8,128)(2,1)}, f32[7,7,48,384]{3,2,1,0:T(8,128)}, f32[1,768]{1,0:T(1,128)}, f32[7,48,384]{2,1,0:T(8,128)}, f32[7,48,...) custom-call(f32[7,7,48,1024]{3,2,1,0:T(8,128)} %get-tuple-element.109.gs, ...), custom_call_target="tpu_custom_call" | custom-call | tf_op jit(solution)/shard_map/fifth_pass/pallas_call | solution.py:1480
  128.6 33.7 %sixth_pass.1 = (f32[7,7,48,384]{3,2,1,0:T(8,128)}, f32[1,768]{1,0:T(1,128)}, bf16[2560,256]{1,0:T(8,128)(2,1)}, bf16[192,256]{1,0:T(8,128)(2,1)}) custom-call(f32[7,7,48,384]{3,2,1,0:T(8,128)} %get-tuple-element.114.q2_hbm, f32[7,7,48,384]{3,2,1,0:T(8,128)} %get-tuple-element.95.z2.z2_hbm, f32[7,7,48,384]{3,2,1,0:T(8,128)} %get-tuple-element.87.z1_hbm.z1, ...), custom_call_target="tpu_custom_call" | custom-call | tf_op jit(solution)/shard_map/sixth_pass/pallas_call | solution.py:1506
  162.3 71.5 %seventh_pass.1 = (bf16[12,7,7,4,1024]{4,3,2,1,0:T(4,128)(2,1)}, bf16[4,7,7,48,128]{4,3,2,1,0:T(8,128)(2,1)}, bf16[6144,256]{1,0:T(8,128)(2,1)}, bf16[2560,256]{...) custom-call(f32[7,7,48,384]{3,2,1,0:T(8,128)} %get-tuple-element.125.q1, ...), custom_call_target="tpu_custom_call" | custom-call | tf_op jit(solution)/shard_map/seventh_pass/pallas_call | solution.py:1539
  233.9 17.7 %finish_outputs.1 = (bf16[12,7,7,4,1024]{4,3,2,1,0:T(4,128)(2,1)}, bf16[4,7,7,48,128]{4,3,2,1,0:T(8,128)(2,1)}, bf16[12,7,7,4,1024]{4,3,2,1,0:T(4,128)(2,1)}, bf...) custom-call(bf16[12,7,7,4,1024]{4,3,2,1,0:T(4,128)(2,1)} %get-tuple-, ...), custom_call_target="tpu_custom_call" | custom-call | tf_op jit(solution)/shard_map/finish_outputs/pallas_call | solution.py:1581
